TPU v7x, 128 devices: a whole 4x4x4 slice. The times are simulated.
128 devices in a mesh: expert: 16 (over x, z_hi, core), dp: 8 (over y, z_lo).
Axes of the slice: x: 4, y: 4, z: 4 (z_hi: 2, z_lo: 2; z = z_hi * 2 + z_lo), core: 2. Of those that a mesh axis runs over, the one named last changes fastest.
Arguments:
- rows_x: bfloat16 [4096, 4096], P('expert'), may hold values from -6 to 6
- rows_dy: bfloat16 [4096, 4096], P('expert'), may hold values from -2 to 2
- router_logits: float32 [4096, 16], P('expert'), may hold values from -7.5 to 307.5
- expert_of: int32 [4096, 1], P('expert'), may hold values from 0 to 15, as said below
- w_gate: bfloat16 [16, 1536, 4096], P('expert', 'dp'), may hold values from -0.09375 to 0.09375
- w_up: bfloat16 [16, 1536, 4096], P('expert', 'dp'), may hold values from -0.09375 to 0.09375
- w_down: bfloat16 [16, 1536, 4096], P('expert', 'dp'), may hold values from -0.15625 to 0.15625
Outputs:
- grad_rows: bfloat16 [4096, 4096], P('expert', 'dp')
- grad_logits: float32 [4096, 16], P('expert')
- grad_gate: float32 [16, 1536, 4096], P('expert', 'dp')
- grad_up: float32 [16, 1536, 4096], P('expert', 'dp')
- grad_down: float32 [16, 1536, 4096], P('expert', 'dp')
- grad_norm: float32 [], replicated
Inputs may be any that keep to these rules, and one draw needn't show every extreme that they name: `expert_of`: one expert, the same in every aligned block of 256 rows, is named by exactly 64 rows of each block; a second expert, the same in every block, by exactly 32 rows of each block; every other expert by at most 32 rows of a block.
All inputs are finite; a program needn't handle non-finite values.
Results may differ from a plain program's by a relative error of at most 0.015.
Values may be sent and summed in bfloat16 or wider, within the bound.
A program may use at most 192 MiB of HBM per device.

v0:
```python
import jax
import jax.numpy as jnp
from jax import lax
from jax.sharding import PartitionSpec as P

aux_weight = 1.0


def as_sent(value):

    def short(part):
        return part.astype(jnp.bfloat16) if part.dtype == jnp.float32 else part

    return jax.tree.map(short, value)


def rank_rows(expert_ids, expert_total):
    onehot = (expert_ids[:, None] == jnp.arange(expert_total, dtype=jnp.int32)[None, :]).astype(
        jnp.int32
    )
    earlier = jnp.cumsum(onehot, axis=0) - onehot
    ranking = jnp.sum(earlier * onehot, axis=1)
    return (onehot, ranking)


def place_rows(values, target, total):
    return jnp.zeros((total,) + values.shape[1:], values.dtype).at[target].set(values, mode="drop")


def take_rows(values, target):
    return values[jnp.minimum(target, values.shape[0] - 1)]


def lay_out(sources, target, expert_total, slot_cap):
    return tuple(
        [
            place_rows(values, target, expert_total * slot_cap).reshape(
                (expert_total, slot_cap) + values.shape[1:]
            )
            for values in sources
        ]
    )


def expert_backward(rows_in, grads_in, gates_in, gate_weight, up_weight, down_weight):
    scaled = (gates_in.astype(jnp.float32)[:, None] * grads_in.astype(jnp.float32)).astype(
        jnp.bfloat16
    )
    gate_pre = lax.dot_general(
        rows_in, gate_weight, (((1,), (1,)), ((), ())), preferred_element_type=jnp.float32
    )
    up_pre = lax.dot_general(
        rows_in, up_weight, (((1,), (1,)), ((), ())), preferred_element_type=jnp.float32
    )
    sigmoid_gate = jax.nn.sigmoid(gate_pre)
    active = gate_pre * sigmoid_gate
    hidden = (active * up_pre).astype(jnp.bfloat16)
    output_part = jnp.dot(hidden, down_weight, preferred_element_type=jnp.float32)
    gate_part = jnp.sum(grads_in.astype(jnp.float32) * output_part, axis=1)
    grad_hidden = lax.dot_general(
        scaled, down_weight, (((1,), (1,)), ((), ())), preferred_element_type=jnp.float32
    )
    grad_upper = (grad_hidden * active).astype(jnp.bfloat16)
    grad_pre = (
        grad_hidden * up_pre * sigmoid_gate * (1.0 + gate_pre * (1.0 - sigmoid_gate))
    ).astype(jnp.bfloat16)
    down_grad_t = lax.dot_general(
        scaled, hidden, (((0,), (0,)), ((), ())), preferred_element_type=jnp.float32
    )
    gate_grad_w = lax.dot_general(
        grad_pre, rows_in, (((0,), (0,)), ((), ())), preferred_element_type=jnp.float32
    )
    up_grad_w = lax.dot_general(
        grad_upper, rows_in, (((0,), (0,)), ((), ())), preferred_element_type=jnp.float32
    )
    input_part = jnp.dot(grad_pre, gate_weight, preferred_element_type=jnp.float32)
    input_part = input_part + jnp.dot(grad_upper, up_weight, preferred_element_type=jnp.float32)
    rounded = lax.optimization_barrier(input_part.astype(jnp.bfloat16)).astype(jnp.float32)
    return (rounded, gate_part, gate_grad_w, up_grad_w, down_grad_t)


def local(rows_x, rows_dy, router_logits, expert_of, w_gate, w_up, w_down):
    expert_total = lax.axis_size("expert")
    rows_count = rows_x.shape[0]
    width = rows_x.shape[1]
    capacity = rows_count // 4
    expert_ids = expert_of[:, 0]
    onehot, ranking = rank_rows(expert_ids, expert_total)
    counts = lax.psum(jnp.sum(onehot, axis=0), "expert")
    router_probs = jax.nn.softmax(router_logits, axis=1)
    onehot_f = onehot.astype(jnp.float32)
    gate_b = jnp.sum(router_probs * onehot_f, axis=1).astype(jnp.bfloat16)
    gate_weight, up_weight, down_weight = (w_gate[0], w_up[0], w_down[0])
    sources = (rows_x, rows_dy, gate_b)
    target = expert_ids * capacity + ranking
    arrived_rows, arrived_grads, arrived_gates = lax.all_to_all(
        as_sent(lay_out(sources, target, expert_total, capacity)),
        "expert",
        split_axis=0,
        concat_axis=0,
        tiled=True,
    )
    slot_total = expert_total * capacity
    cold_results = expert_backward(
        arrived_rows.reshape(slot_total, width),
        arrived_grads.reshape(slot_total, width),
        arrived_gates.reshape(slot_total),
        gate_weight,
        up_weight,
        down_weight,
    )
    grad_gate_w, grad_up_w, grad_down_t = (cold_results[2], cold_results[3], cold_results[4])
    input_terms, gate_terms = (cold_results[0], cold_results[1])
    input_sum = lax.psum_scatter(
        input_terms.astype(jnp.bfloat16), "dp", scatter_dimension=1, tiled=True
    )
    gate_sum = lax.psum(gate_terms, "dp").astype(jnp.bfloat16)
    column_width = input_sum.shape[1]
    back_rows, back_gates = (
        lax.all_to_all(
            input_sum.reshape(expert_total, capacity, column_width),
            "expert",
            split_axis=0,
            concat_axis=0,
            tiled=True,
        ),
        lax.all_to_all(
            gate_sum.reshape(expert_total, capacity),
            "expert",
            split_axis=0,
            concat_axis=0,
            tiled=True,
        ),
    )
    grad_rows = take_rows(back_rows.reshape(slot_total, column_width), target)
    gate_rows = take_rows(back_gates.reshape(slot_total), target)
    gate_rows = gate_rows.astype(jnp.float32)
    fractions = counts.astype(jnp.float32) / (rows_count * expert_total)
    pulls = onehot_f * gate_rows[:, None] + aux_weight * expert_total * fractions[None, :]
    grad_logits = router_probs * (pulls - jnp.sum(router_probs * pulls, axis=1, keepdims=True))
    local_squares = (
        jnp.sum(grad_gate_w * grad_gate_w)
        + jnp.sum(grad_up_w * grad_up_w)
        + jnp.sum(grad_down_t * grad_down_t)
    )
    norm_total = lax.psum(local_squares, ("expert", "dp"))
    return (
        grad_rows,
        grad_logits,
        grad_gate_w[None],
        grad_up_w[None],
        grad_down_t.T[None],
        jnp.sqrt(norm_total),
    )


def solution(mesh):
    in_specs = (
        P("expert", None),
        P("expert", None),
        P("expert", None),
        P("expert", None),
        P("expert", "dp", None),
        P("expert", "dp", None),
        P("expert", "dp", None),
    )
    out_specs = (
        P("expert", "dp"),
        P("expert", None),
        P("expert", "dp", None),
        P("expert", "dp", None),
        P("expert", "dp", None),
        P(),
    )
    return jax.shard_map(local, mesh=mesh, in_specs=in_specs, out_specs=out_specs, check_vma=False)
```

profile of v0, /device:TPU:1, one launch (start us, length us, event | category | flops | bytes accessed | tf_op | source)
XLA Modules:
  0.0 675.2 jit_solution(7656628439531156621)
XLA Ops:
  7.2 0.0 copy-start
  7.2 0.8 fusion.28
  8.0 0.6 reduce-window.6
  8.6 0.2 slice_reduce_fusion
  8.8 0.9 convert_reduce_fusion
  9.7 0.7 compare_select_fusion
  10.3 9.3 %scatter_custom_fusion.2 = bf16[1024,4096]{1,0:T(8,128)(2,1)} fusion(s32[256]{0:T(256)S(1)} %bitcast.78, bf16[256,4096]{1,0:T(8,128)(2,1)} %param.7, bf16[]{:T(256)} %constant.9.clone.1), kind=kCustom, calls=%fused_computation.12 | custom fusion | bytes 8389120 | tf_op jit(solution)/shard_map/scatter | solution.py:27
  19.6 9.8 %all-to-all-start.2 = ((bf16[16,64,4096]{2,1,0:T(8,128)(2,1)}), bf16[16,64,4096]{2,1,0:T(8,128)(2,1)}, u32[]{:S(2)}, u32[]{:S(2)}) async-start(bf16[16,64,4096]{2,1,0:T(8,128)(2,1)} %bitcast.67), calls=%async_computation.2 | async-start | bytes 16777216 | tf_op jit(solution)/shard_map/all_to_all | solution.py:96
  29.4 9.3 %scatter_custom_fusion.1 = bf16[1024,4096]{1,0:T(8,128)(2,1)} fusion(s32[256]{0:T(256)S(1)} %bitcast.79, bf16[256,4096]{1,0:T(8,128)(2,1)} %param.8, bf16[]{:T(256)} %constant.9.clone.1), kind=kCustom, calls=%fused_computation.14 | custom fusion | bytes 8389120 | tf_op jit(solution)/shard_map/scatter | solution.py:27
  38.7 122.3 %all-to-all-done.2 = bf16[16,64,4096]{2,1,0:T(8,128)(2,1)} async-done(((bf16[16,64,4096]{2,1,0:T(8,128)(2,1)}), bf16[16,64,4096]{2,1,0:T(8,128)(2,1)}, u32[]{:S(2)}, u32[]{:S(2)}) %all-to-all-start.2) | async-done | bytes 8388640 | tf_op jit(solution)/shard_map/all_to_all | solution.py:96
  161.0 8.3 %all-to-all-start.1 = ((bf16[16,64,4096]{2,1,0:T(8,128)(2,1)}), bf16[16,64,4096]{2,1,0:T(8,128)(2,1)}, u32[]{:S(2)}, u32[]{:S(2)}) async-start(bf16[16,64,4096]{2,1,0:T(8,128)(2,1)} %bitcast.66), calls=%async_computation.1 | async-start | bytes 16777216 | tf_op jit(solution)/shard_map/all_to_all | solution.py:96
  169.4 131.7 %psum.22 = s32[16]{0:T(128)S(1)} all-reduce(s32[16]{0:T(128)S(1)} %get-tuple-element.8), channel_id=1, replica_groups=mesh['expert'=16,'dp'=8] {'expert'}, use_global_device_ids=true, to_apply=%region_13.14 | all-reduce | flops 16 | bytes 128 | tf_op jit(solution)/shard_map/psum | solution.py:89
  301.1 0.0 copy-start.15
  301.1 6.3 fusion.9
  307.5 0.0 copy-start.19
  307.5 0.9 copy-done.19
  308.4 7.4 %multiply_convert_fusion = (bf16[1024,192]{0,1:T(8,128)(2,1)}, f32[1024,192]{0,1:T(8,128)}) fusion(f32[1024,192]{0,1:T(8,128)S(1)} %fusion.9, bf16[1024,4096]{1,0:T(8,128)(2,1)} %bitcast.10, bf16[1,192,4096]{2,1,0:T(8,128)(2,1)S(1)} %copy-done), kind=kOutput, calls=%fused_computation.29 | convolution fusion | flops 1611792384 | bytes 11927552 | tf_op jit(solution)/shard_map/dot_general | solution.py:52
  315.8 6.5 fusion.1
  322.2 15.7 %psum.21 = bf16[1024]{0:T(1024)(128)(2,1)S(1)} all-reduce(f32[1024]{0:T(1024)S(1)} %fusion.1), channel_id=1, replica_groups=mesh['expert'=16,'dp'=8] {'dp'}, use_global_device_ids=true, to_apply=%region_11.12 | all-reduce | flops 1024 | bytes 6144 | tf_op jit(solution)/shard_map/psum | solution.py:117
  337.9 0.7 all_to_all.29
  338.6 12.3 %all-to-all-start.4 = ((bf16[16,1,64]{2,1,0:T(2,128)(2,1)}), bf16[16,1,64]{2,1,0:T(2,128)(2,1)S(1)}, u32[]{:S(2)}, u32[]{:S(2)}) async-start(bf16[16,1,64]{2,1,0:T(2,128)(2,1)} %all_to_all.29), calls=%async_computation.5 | async-start | bytes 16384 | tf_op jit(solution)/shard_map/all_to_all | solution.py:127
  350.9 0.0 reduce-scatter.2.cloned.1.call-start
  351.0 6.9 %all-to-all-done.4 = bf16[16,1,64]{2,1,0:T(2,128)(2,1)S(1)} async-done(((bf16[16,1,64]{2,1,0:T(2,128)(2,1)}), bf16[16,1,64]{2,1,0:T(2,128)(2,1)S(1)}, u32[]{:S(2)}, u32[]{:S(2)}) %all-to-all-start.4) | async-done | bytes 2080 | tf_op jit(solution)/shard_map/all_to_all | solution.py:127
  357.9 0.1 reshape.92
  358.0 1.9 gather_fusion.1
  360.0 0.0 copy-start.12
  360.0 0.7 fusion.26
  360.6 2.2 scatter_custom_fusion
  362.8 0.1 all_to_all.28
  362.9 10.1 %all_to_all.35 = bf16[16,1,64]{2,1,0:T(2,128)(2,1)S(1)} all-to-all(bf16[16,1,64]{2,1,0:T(2,128)(2,1)S(1)} %all_to_all.28), channel_id=1, replica_groups=mesh['expert'=16,'dp'=8] {'expert'}, dimensions={0} | all-to-all | bytes 4096 | tf_op jit(solution)/shard_map/all_to_all | solution.py:96
  373.0 0.0 copy-start.17
  373.0 10.1 %fusion = bf16[16,64,4096]{2,1,0:T(8,128)(2,1)} fusion(bf16[16,64,4096]{2,1,0:T(8,128)(2,1)} %all-to-all-done.1, f32[16,64]{1,0:T(8,128)S(1)} %bitcast.71), kind=kLoop, calls=%fused_computation.8 | loop fusion | flops 12582912 | bytes 16781312 | tf_op jit(solution)/shard_map/convert_element_type | solution.py:46
  383.1 6.9 %multiply_convert_fusion.1 = (bf16[1024,192]{0,1:T(8,128)(2,1)S(1)}, bf16[1024,192]{0,1:T(8,128)(2,1)S(1)}) fusion(f32[1024,192]{0,1:T(8,128)} %copy-done.19, f32[1024,192]{0,1:T(8,128)} %get-tuple-element.15, bf16[1024,4096]{1,0:T(8,128)(2,1)} %bitcast.69, bf16[1,192,4096]{2,1,0:T(8,128)(2,1)S(1)} %copy-done.17), kind=kOutput, calls=%fused_computation.30 | convolution fusion | flops 1613168640 | bytes 12320768 | tf_op jit(solution)/shard_map/dot_general | solution.py:60
  390.0 0.0 copy-start.2
  390.0 8.1 %fusion.7 = f32[1024,4096]{1,0:T(8,128)} fusion(bf16[1024,192]{0,1:T(8,128)(2,1)S(1)} %get-tuple-element.11, bf16[1,192,4096]{2,1,0:T(8,128)(2,1)S(1)} %copy-done.1), kind=kOutput, calls=%fused_computation.19 | convolution fusion | flops 1610612736 | bytes 18743296 | tf_op jit(solution)/shard_map/dot_general | solution.py:76
  398.1 11.4 %add_convert_fusion = bf16[1024,4096]{1,0:T(8,128)(2,1)} fusion(f32[1024,4096]{1,0:T(8,128)} %fusion.7, bf16[1024,192]{0,1:T(8,128)(2,1)S(1)} %get-tuple-element.10, bf16[1,192,4096]{2,1,0:T(8,128)(2,1)S(1)} %copy-done), kind=kOutput, calls=%fused_computation.11 | convolution fusion | flops 1619001344 | bytes 27131904 | tf_op jit(solution)/shard_map/dot_general | solution.py:77
  409.5 0.0 reduce-scatter.2.cloned.1.call-update
  409.5 0.1 reshape.95
  409.6 7.5 %multiply_reduce_fusion.2 = (f32[]{:T(128)}, f32[192,4096]{1,0:T(8,128)}) fusion(bf16[1024,192]{0,1:T(8,128)(2,1)S(1)} %get-tuple-element.11, bf16[1024,4096]{1,0:T(8,128)(2,1)} %bitcast.10), kind=kOutput, calls=%fused_computation.18 | convolution fusion | flops 1612185600 | bytes 11927556 | tf_op jit(solution)/shard_map/dot_general | solution.py:70
  417.1 10.2 %fusion.2 = bf16[1024,4096]{1,0:T(8,128)(2,1)} fusion(bf16[16,64,4096]{2,1,0:T(8,128)(2,1)} %all-to-all-done.1, f32[1024]{0:T(1024)S(1)} %reshape.95), kind=kLoop, calls=%fused_computation.10 | loop fusion | flops 12582912 | bytes 16781312 | tf_op jit(solution)/shard_map/convert_element_type | solution.py:46
  427.4 145.9 %reduce-scatter.2.cloned.1.call-done = bf16[1024,512]{1,0:T(8,128)(2,1)} async-done(((bf16[1024,4096]{1,0:T(8,128)(2,1)}), bf16[1024,512]{1,0:T(8,128)(2,1)}) %reduce-scatter.2.cloned.1.call-update) | async-done | bytes 1048592 | tf_op jit(solution)/shard_map/reduce_scatter | solution.py:114
  573.3 7.3 %all-to-all-start.3 = ((bf16[16,64,512]{2,1,0:T(8,128)(2,1)}), bf16[16,64,512]{2,1,0:T(8,128)(2,1)S(1)}, u32[]{:S(2)}, u32[]{:S(2)}) async-start(bf16[16,64,512]{2,1,0:T(8,128)(2,1)} %bitcast.70), calls=%async_computation.4 | async-start | bytes 2097152 | tf_op jit(solution)/shard_map/all_to_all | solution.py:120
  580.6 7.4 %multiply_reduce_fusion.1 = (f32[]{:T(128)}, f32[192,4096]{1,0:T(8,128)}) fusion(bf16[1024,192]{0,1:T(8,128)(2,1)S(1)} %copy-done.3, bf16[1024,4096]{1,0:T(8,128)(2,1)} %bitcast.10), kind=kOutput, calls=%fused_computation.17 | convolution fusion | flops 1612185600 | bytes 11927556 | tf_op jit(solution)/shard_map/dot_general | solution.py:73
  588.0 0.0 copy-start.16
  589.4 7.5 %multiply_reduce_fusion = (f32[]{:T(128)}, f32[4096,192]{0,1:T(8,128)}) fusion(bf16[1024,192]{0,1:T(8,128)(2,1)S(1)} %copy-done.18, bf16[1024,4096]{1,0:T(8,128)(2,1)} %fusion.2), kind=kOutput, calls=%fused_computation.16 | convolution fusion | flops 1612185600 | bytes 11927556 | tf_op jit(solution)/shard_map/dot_general | solution.py:67
  597.6 0.7 fusion.27
  598.3 65.8 %psum.23 = f32[]{:T(128)} all-reduce(f32[]{:T(128)S(6)} %add.56), channel_id=1, replica_groups=mesh['expert'=16,'dp'=8] {'expert','dp'}, use_global_device_ids=true, to_apply=%region_18.19 | all-reduce | flops 1 | bytes 8 | tf_op jit(solution)/shard_map/psum | solution.py:146
  664.8 2.0 gather_fusion
  (44 shorter events, 0.2 us)
Async XLA Ops:
  7.2 301.2 %copy-start = (bf16[1,192,4096]{2,1,0:T(8,128)(2,1)S(1)}, bf16[1,192,4096]{2,1,0:T(8,128)(2,1)}, u32[]{:S(2)}) copy-start(bf16[1,192,4096]{2,1,0:T(8,128)(2,1)} %param.12) | copy-start | bytes 4718596
  19.6 141.4 %all-to-all-start.2 = ((bf16[16,64,4096]{2,1,0:T(8,128)(2,1)}), bf16[16,64,4096]{2,1,0:T(8,128)(2,1)}, u32[]{:S(2)}, u32[]{:S(2)}) async-start(bf16[16,64,4096]{2,1,0:T(8,128)(2,1)} %bitcast.67), calls=%async_computation.2 | async-start | bytes 16777216 | tf_op jit(solution)/shard_map/all_to_all | solution.py:96
  161.0 8.3 %copy-start.4 = (f32[256,16]{0,1:T(8,128)S(1)}, f32[256,16]{0,1:T(8,128)}, u32[]{:S(2)}) copy-start(f32[256,16]{0,1:T(8,128)} %param.9) | copy-start | bytes 49156
  161.0 140.1 %copy-start.1 = (bf16[1,192,4096]{2,1,0:T(8,128)(2,1)S(1)}, bf16[1,192,4096]{2,1,0:T(8,128)(2,1)}, u32[]{:S(2)}) copy-start(bf16[1,192,4096]{2,1,0:T(8,128)(2,1)} %param.11) | copy-start | bytes 4718596
  161.0 154.8 %all-to-all-start.1 = ((bf16[16,64,4096]{2,1,0:T(8,128)(2,1)}), bf16[16,64,4096]{2,1,0:T(8,128)(2,1)}, u32[]{:S(2)}, u32[]{:S(2)}) async-start(bf16[16,64,4096]{2,1,0:T(8,128)(2,1)} %bitcast.66), calls=%async_computation.1 | async-start | bytes 16777216 | tf_op jit(solution)/shard_map/all_to_all | solution.py:96
  169.3 190.6 %copy-start.7 = (f32[256]{0:T(256)}, f32[256]{0:T(256)S(1)}, u32[]{:S(2)}) copy-start(f32[256]{0:T(256)S(1)} %reduce_max.9) | copy-start | bytes 3076
  301.1 58.8 %copy-start.10 = (f32[256]{0:T(256)}, f32[256]{0:T(256)S(1)}, u32[]{:S(2)}) copy-start(f32[256]{0:T(256)S(1)} %fusion.30) | copy-start | bytes 3076
  301.1 58.8 %copy-start.15 = (f32[16]{0:T(128)}, f32[16]{0:T(128)S(1)}, u32[]{:S(2)}) copy-start(f32[16]{0:T(128)S(1)} %convert_multiply_fusion.1) | copy-start | bytes 196
  307.5 0.9 copy-start.19
  315.8 44.2 %copy-start.6 = (s32[256,1]{0,1:T(1,128)S(1)}, s32[256,1]{0,1:T(1,128)}, u32[]{:S(2)}) copy-start(s32[256,1]{0,1:T(1,128)} %param.10) | copy-start | bytes 3076
  338.6 19.3 %all-to-all-start.4 = ((bf16[16,1,64]{2,1,0:T(2,128)(2,1)}), bf16[16,1,64]{2,1,0:T(2,128)(2,1)S(1)}, u32[]{:S(2)}, u32[]{:S(2)}) async-start(bf16[16,1,64]{2,1,0:T(2,128)(2,1)} %all_to_all.29), calls=%async_computation.5 | async-start | bytes 16384 | tf_op jit(solution)/shard_map/all_to_all | solution.py:127
  350.9 222.4 %reduce-scatter.2.cloned.1.call-start = ((), (), s32[]{:S(2)}) async-start(), calls=%async_computation.6 | async-start | bytes 9437184 | tf_op jit(solution)/shard_map/reduce_scatter | solution.py:114
  351.0 32.1 %copy-start.9 = (s32[1024]{0:T(1024)}, s32[1024]{0:T(1024)S(1)}, u32[]{:S(2)}) copy-start(s32[1024]{0:T(1024)S(1)} %pad_clamp_fusion) | copy-start | bytes 12292
  360.0 23.1 %copy-start.12 = (f32[256]{0:T(256)}, f32[256]{0:T(256)S(1)}, u32[]{:S(2)}) copy-start(f32[256]{0:T(256)S(1)} %convert_element_type.90) | copy-start | bytes 3076
  373.0 10.1 %copy-start.17 = (bf16[1,192,4096]{2,1,0:T(8,128)(2,1)S(1)}, bf16[1,192,4096]{2,1,0:T(8,128)(2,1)}, u32[]{:S(2)}) copy-start(bf16[1,192,4096]{2,1,0:T(8,128)(2,1)} %param.13) | copy-start | bytes 4718596
  390.0 8.1 %copy-start.2 = (bf16[1024,192]{0,1:T(8,128)(2,1)}, bf16[1024,192]{0,1:T(8,128)(2,1)S(1)}, u32[]{:S(2)}) copy-start(bf16[1024,192]{0,1:T(8,128)(2,1)S(1)} %get-tuple-element.10) | copy-start | bytes 1179652
  417.1 163.5 %copy-start.3 = (bf16[1024,192]{0,1:T(8,128)(2,1)S(1)}, bf16[1024,192]{0,1:T(8,128)(2,1)}, u32[]{:S(2)}) copy-start(bf16[1024,192]{0,1:T(8,128)(2,1)} %copy-done.2) | copy-start | bytes 1179652
  427.4 162.0 %copy-start.18 = (bf16[1024,192]{0,1:T(8,128)(2,1)S(1)}, bf16[1024,192]{0,1:T(8,128)(2,1)}, u32[]{:S(2)}) copy-start(bf16[1024,192]{0,1:T(8,128)(2,1)} %get-tuple-element.14) | copy-start | bytes 1179652
  573.3 91.5 %all-to-all-start.3 = ((bf16[16,64,512]{2,1,0:T(8,128)(2,1)}), bf16[16,64,512]{2,1,0:T(8,128)(2,1)S(1)}, u32[]{:S(2)}, u32[]{:S(2)}) async-start(bf16[16,64,512]{2,1,0:T(8,128)(2,1)} %bitcast.70), calls=%async_computation.4 | async-start | bytes 2097152 | tf_op jit(solution)/shard_map/all_to_all | solution.py:120
  588.0 9.5 %copy-start.5 = (f32[256,16]{0,1:T(8,128)S(1)}, f32[256,16]{0,1:T(8,128)}, u32[]{:S(2)}) copy-start(f32[256,16]{0,1:T(8,128)} %param.9) | copy-start | bytes 49156
  588.0 9.5 %copy-start.8 = (f32[256]{0:T(256)S(1)}, f32[256]{0:T(256)}, u32[]{:S(2)}) copy-start(f32[256]{0:T(256)} %copy-done.7) | copy-start | bytes 3076
  588.0 9.5 %copy-start.11 = (f32[256]{0:T(256)S(1)}, f32[256]{0:T(256)}, u32[]{:S(2)}) copy-start(f32[256]{0:T(256)} %copy-done.10) | copy-start | bytes 3076
  588.0 9.5 %copy-start.13 = (f32[256]{0:T(256)S(1)}, f32[256]{0:T(256)}, u32[]{:S(2)}) copy-start(f32[256]{0:T(256)} %copy-done.12) | copy-start | bytes 3076
  588.0 9.5 %copy-start.14 = (f32[256]{0:T(256)S(1)}, f32[256]{0:T(256)}, u32[]{:S(2)}) copy-start(f32[256]{0:T(256)} %get-tuple-element.6) | copy-start | bytes 3076
  588.0 9.5 %copy-start.16 = (f32[16]{0:T(128)S(1)}, f32[16]{0:T(128)}, u32[]{:S(2)}) copy-start(f32[16]{0:T(128)} %copy-done.15) | copy-start | bytes 196
Sparse Core Ops, SparseCore 0:
  409.6 163.6 reduce-scatter.1
where the time goes:
time: 682 us; the launch traced here: 675 us
  waiting for transfers between devices  275 us (40%)
  blocking collectives  223 us (33%)
  matrix products  69 us (10%)
  starting transfers between devices  37.8 us (6%)
  local copies, waits for them, and re-layouts  26.7 us (4%)
  other arithmetic  24.8 us (4%)
  between operations  18.5 us (3%)
    reduce_scatter x1, waiting for transfers between devices, local(): lax.psum_scatter(input_terms.astype(jnp.bfloat16), 'dp', scatter_dimensio...  146 us
    psum x1, blocking collectives, local(): counts = lax.psum(jnp.sum(onehot, axis=0), 'expert')  132 us
    all_to_all x2, waiting for transfers between devices, local(): lax.all_to_all(as_sent(lay_out(sources, target, expert_total, capacity)),...  122 us
    psum x1, blocking collectives, local(): norm_total = lax.psum(local_squares, ('expert', 'dp'))  65.8 us
    scatter x3, local copies, waits for them, and re-layouts, place_rows(): jnp.zeros((total,) + values.shape[1:], values.dtype).at[target]  20.7 us
    convert_element_type x2, other arithmetic, expert_backward(): (gates_in.astype(jnp.float32)[:, None] * grads_in.astype(jnp.float32)).as...  20.3 us
    all_to_all x2, starting transfers between devices, local(): lax.all_to_all(as_sent(lay_out(sources, target, expert_total, capacity)),...  18.1 us
    psum x1, blocking collectives, local(): gate_sum = lax.psum(gate_terms, 'dp').astype(jnp.bfloat16)  15.7 us
  transfers between devices with their start and end apart: 5, of which 3 were waited for; matrix products, arithmetic and copies ran while one was open for 8% of the time, Pallas kernels for 0%

commit v1 on v0

v1 whole, which is shorter than its diff:
```python
import jax
import jax.numpy as jnp
from jax import lax
from jax.experimental import pallas as pl
from jax.experimental.pallas import tpu as pltpu
from jax.sharding import PartitionSpec as P

f32 = jnp.float32
bf16 = jnp.bfloat16
MESH = pl.DeviceIdType.MESH
ANY = pl.BlockSpec(memory_space=pl.ANY)
VM = pl.BlockSpec(memory_space=pltpu.VMEM)
SM = pl.BlockSpec(memory_space=pltpu.SMEM)

E = 16
NDP = 8
SLOT = 32
W = 512
ROWS = E * SLOT
LOCAL = 2 * SLOT
SLOTS = ROWS + SLOT
GW = 1280


def place():
    e = lax.axis_index("expert")
    d = lax.axis_index("dp")
    return e, d, e // 4, (e // 2) % 2, e % 2, d // 2, d % 2


def expert_at(x, zh, c):
    return (x * 2 + zh) * 2 + c


def to(e, d):
    return {"expert": e, "dp": d}


def row_facts(ids, experts):
    rows = ids.shape[1]
    onehot = (lax.broadcasted_iota(jnp.int32, (experts, rows), 0) == ids).astype(f32)
    before = lax.broadcasted_iota(jnp.int32, (rows, rows), 0) < lax.broadcasted_iota(
        jnp.int32, (rows, rows), 1
    )
    earlier = jnp.dot(onehot.astype(bf16), before.astype(bf16), preferred_element_type=f32)
    rank = jnp.sum(onehot * earlier, axis=0, keepdims=True).astype(jnp.int32)
    return onehot, rank


def soft(logits):
    top = jnp.max(logits, axis=0, keepdims=True)
    ex = jnp.exp(logits - top)
    return ex / jnp.sum(ex, axis=0, keepdims=True)


def nt(a, b):
    return lax.dot_general(a, b, (((1,), (1,)), ((), ())), preferred_element_type=f32)


def tn(a, b):
    return lax.dot_general(a, b, (((0,), (0,)), ((), ())), preferred_element_type=f32)


def slots_kernel(ids_ref, logits_ref, x_ref, dy_ref, s_ref, m_ref, perm):
    @pl.when(pl.program_id(0) == 0)
    def _():
        ids = ids_ref[...]
        onehot, rank = row_facts(ids, E)
        rows = ids.shape[1]
        target = jnp.where(rank < SLOT, ids * SLOT + rank, ROWS + rank - SLOT)
        slot = lax.broadcasted_iota(jnp.int32, (SLOTS, rows), 0)
        perm[...] = (slot == target).astype(f32).astype(bf16)
        gate = jnp.sum(soft(logits_ref[...]) * onehot, axis=0, keepdims=True).astype(bf16)
        gate = gate.astype(f32)
        lane = lax.broadcasted_iota(jnp.int32, (128, rows), 0)
        first = (lane == rank).astype(f32).astype(bf16)
        extra = (lane == rank - SLOT).astype(f32).astype(bf16)
        by_expert = (lane == ids).astype(f32).astype(bf16)
        cold = (onehot * gate * (rank < SLOT).astype(f32)).astype(bf16)
        cold = nt(cold, first)
        gate8 = jnp.broadcast_to(gate, (8, rows)).astype(bf16)
        hot = nt(gate8, extra)
        count = nt(jnp.ones((8, rows), bf16), by_expert)
        line = lax.broadcasted_iota(jnp.int32, (8, 128), 0)
        for e in range(E):
            mine = jnp.broadcast_to(cold[e : e + 1, :], (8, 128))
            m_ref[e] = jnp.where(line == 0, mine, jnp.where(line == 1, hot, count))

    p = perm[...]
    s_ref[0, 0] = jnp.dot(p, x_ref[...], preferred_element_type=f32).astype(bf16)
    s_ref[1, 0] = jnp.dot(p, dy_ref[...], preferred_element_type=f32).astype(bf16)


def lay_out(ids, logits, x, dy):
    rows = x.shape[0]
    return pl.pallas_call(
        slots_kernel,
        grid=(NDP,),
        in_specs=[
            pl.BlockSpec((1, rows), lambda j: (0, 0)),
            pl.BlockSpec((E, rows), lambda j: (0, 0)),
            pl.BlockSpec((rows, W), lambda j: (0, j)),
            pl.BlockSpec((rows, W), lambda j: (0, j)),
        ],
        out_specs=[
            pl.BlockSpec((2, 1, SLOTS, W), lambda j: (0, j, 0, 0)),
            pl.BlockSpec((E, 8, 128), lambda j: (0, 0, 0)),
        ],
        out_shape=[
            jax.ShapeDtypeStruct((2, NDP, SLOTS, W), bf16),
            jax.ShapeDtypeStruct((E, 8, 128), f32),
        ],
        scratch_shapes=[pltpu.VMEM((SLOTS, rows), bf16)],
        name="lay_out",
    )(ids, logits, x, dy)


class Gather:
    names = (
        "0oz", "0or", "0ol", "0lr", "0lz", "0rl", "0rz", "0dz", "0ez",
        "1oz", "1or", "1ol", "1zr", "1zl", "1lr", "1kr", "1rl", "1ql",
    )

    def __init__(self, own, piece, j, z, right, left, pair, ssem, rsem):
        self.own, self.piece, self.ssem, self.rsem = own, piece, ssem, rsem
        self.j, self.z = j, z
        self.jl, self.jr, self.jd = (j + 3) % 4, (j + 1) % 4, (j + 2) % 4
        self.right, self.left, self.pair = right, left, pair
        self.sent = []

    def send(self, name, src, dst, dev):
        i = self.names.index(name)
        copy = pltpu.make_async_remote_copy(
            src, dst, self.ssem.at[i], self.rsem.at[i], device_id=dev, device_id_type=MESH
        )
        copy.start()
        self.sent.append(copy)

    def pass_on(self, name, dev, *where):
        ref = self.piece(*where)
        self.send(name, ref, ref, dev)

    def got(self, name, *where):
        i = self.names.index(name)
        ref = self.piece(*where)
        pltpu.make_async_remote_copy(
            ref, ref, self.ssem.at[i], self.rsem.at[i], device_id=self.pair, device_id_type=MESH
        ).wait_recv()

    def start(self, a):
        for way, dev in (("z", self.pair), ("r", self.right), ("l", self.left)):
            self.send(f"{a}o{way}", self.own(a), self.piece(a, self.j, self.z, None), dev)

    def s2(self):
        self.got("0or", 0, self.jl, self.z, None)
        self.pass_on("0lr", self.right, 0, self.jl, self.z, 0)
        self.pass_on("0lz", self.pair, 0, self.jl, self.z, None)

    def s3(self):
        self.got("0ol", 0, self.jr, self.z, None)
        self.pass_on("0rl", self.left, 0, self.jr, self.z, 1)
        self.pass_on("0rz", self.pair, 0, self.jr, self.z, None)

    def s4(self):
        self.got("1oz", 1, self.j, 1 - self.z, None)
        self.pass_on("1zr", self.right, 1, self.j, 1 - self.z, None)
        self.pass_on("1zl", self.left, 1, self.j, 1 - self.z, None)

    def s5(self):
        self.got("1or", 1, self.jl, self.z, None)
        self.pass_on("1lr", self.right, 1, self.jl, self.z, 0)

    def s6(self):
        self.got("1ol", 1, self.jr, self.z, None)
        self.pass_on("1rl", self.left, 1, self.jr, self.z, 1)

    def s7(self):
        self.got("0lr", 0, self.jd, self.z, 0)
        self.pass_on("0dz", self.pair, 0, self.jd, self.z, 0)

    def s8(self):
        self.got("0rl", 0, self.jd, self.z, 1)
        self.pass_on("0ez", self.pair, 0, self.jd, self.z, 1)

    def s9(self):
        self.got("1zr", 1, self.jl, 1 - self.z, None)
        self.pass_on("1kr", self.right, 1, self.jl, 1 - self.z, 0)

    def s10(self):
        self.got("1zl", 1, self.jr, 1 - self.z, None)
        self.pass_on("1ql", self.left, 1, self.jr, 1 - self.z, 1)

    def end_of_1_d(self):
        self.got("1lr", 1, self.jd, self.z, 0)
        self.got("1rl", 1, self.jd, self.z, 1)

    def end_of_1_e(self):
        self.got("1kr", 1, self.jd, 1 - self.z, 0)
        self.got("1ql", 1, self.jd, 1 - self.z, 1)

    def end_of_0_d(self):
        self.got("0dz", 0, self.jd, 1 - self.z, 0)
        self.got("0ez", 0, self.jd, 1 - self.z, 1)

    def drain(self):
        for copy in self.sent:
            copy.wait_send()


def meet(partners):
    barrier = pltpu.get_barrier_semaphore()
    for dev in partners:
        pl.semaphore_signal(barrier, inc=1, device_id=dev, device_id_type=MESH)
    pl.semaphore_wait(barrier, len(partners))


def others(x, zh):
    for k in range(1, 8):
        dx, dz = k // 2, k % 2
        yield k, ((4 - dx) % 4) * 2 + dz, (x + dx) % 4, (zh + dz) % 2


def dispatch_kernel(
    s, ms, cold, extra, mr, bounce, mbounce,
    st_s, st_r, m_s, m_r, sib_s, sib_r, dp_s, dp_r, ex_s, ex_r, xs_s, xs_r, loc,
):
    e, d, x, zh, c, y, zl = place()
    dbar = y * 2 + 1 - zl
    sib = to(expert_at(x, zh, 1 - c), d)
    d_r, d_l = ((y + 1) % 4) * 2 + zl, ((y + 3) % 4) * 2 + zl
    peers = [
        (rel, back, expert_at(x2, zh2, c2), d if rel % 2 == 0 else dbar)
        for rel, back, x2, zh2 in others(x, zh)
        for c2 in (0, 1)
    ]
    x_r = to(expert_at((x + 1) % 4, zh, c), d)
    x_l = to(expert_at((x + 3) % 4, zh, c), d)
    z_p = to(expert_at(x, 1 - zh, c), dbar)
    meet([to(e2, d2) for _, _, e2, d2 in peers] + [sib, to(e, d_r), to(e, d_l), to(e, dbar)])

    sent, msent = [], []
    for a in (0, 1):
        for rel, back, e2, d2 in peers:
            copy = pltpu.make_async_remote_copy(
                s.at[a, d2, pl.ds(pl.multiple_of(e2 * SLOT, SLOT), SLOT), :],
                cold.at[a, d2, pl.ds(pl.multiple_of((back * 2 + c) * SLOT, SLOT), SLOT), :],
                st_s.at[a], st_r.at[a], device_id=to(e2, d2), device_id_type=MESH,
            )
            copy.start()
        if a == 0:
            own_in = [
                pltpu.make_async_copy(
                    s.at[:, :, pl.ds(pl.multiple_of(e * SLOT, SLOT), SLOT), :], bounce.at[0], loc.at[0]
                ),
                pltpu.make_async_copy(s.at[:, :, pl.ds(ROWS, SLOT), :], bounce.at[1], loc.at[1]),
                pltpu.make_async_copy(ms.at[e], mbounce, loc.at[2]),
            ]
            for copy in own_in:
                copy.start()
    for n, (rel, back, e2, d2) in enumerate(peers + [(0, 0, expert_at(x, zh, 1 - c), d)]):
        copy = pltpu.make_async_remote_copy(
            ms.at[e2], mr.at[back * 2 + c], m_s.at[n], m_r.at[back * 2 + c],
            device_id=to(e2, d2), device_id_type=MESH,
        )
        copy.start()
        msent.append(copy)
    sib_copy = pltpu.make_async_remote_copy(
        s.at[:, :, pl.ds(pl.multiple_of((e + 1 - 2 * c) * SLOT, SLOT), SLOT), :],
        cold.at[:, :, pl.ds(pl.multiple_of(c * SLOT, SLOT), SLOT), :],
        sib_s, sib_r, device_id=sib, device_id_type=MESH,
    )
    sib_copy.start()
    sent.append(sib_copy)
    for copy in own_in:
        copy.wait()
    own_out = [
        pltpu.make_async_copy(
            bounce.at[0], cold.at[:, :, pl.ds(pl.multiple_of(c * SLOT, SLOT), SLOT), :], loc.at[3]
        ),
        pltpu.make_async_copy(
            bounce.at[1], extra.at[:, :, pl.ds(pl.multiple_of(e * SLOT, SLOT), SLOT), :], loc.at[4]
        ),
        pltpu.make_async_copy(mbounce, mr.at[c], loc.at[5]),
    ]
    for copy in own_out:
        copy.start()

    half = (ROWS - LOCAL) // 2

    def dp_piece(a, j, z, h):
        rows = {None: (LOCAL, 2 * half), 0: (LOCAL, half), 1: (LOCAL + half, half)}[h]
        return cold.at[a, j * 2 + z, pl.ds(*rows), :]

    def ex_piece_of(core):
        def piece(a, j, z, h):
            chunks = {None: (0, NDP), 0: (0, NDP // 2), 1: (NDP // 2, NDP // 2)}[h]
            at = pl.multiple_of(expert_at(j, z, core) * SLOT, SLOT)
            return extra.at[a, pl.ds(*chunks), pl.ds(at, SLOT), :]
        return piece

    ex_piece, ex_other = ex_piece_of(c), ex_piece_of(1 - c)

    dp = Gather(
        lambda a: dp_piece(a, y, zl, None), dp_piece, y, zl,
        to(e, d_r), to(e, d_l), to(e, dbar), dp_s, dp_r,
    )
    ex = Gather(
        lambda a: s.at[a, :, pl.ds(ROWS, SLOT), :], ex_piece, x, zh, x_r, x_l, z_p, ex_s, ex_r,
    )
    shares = []

    def share(a, j, z, src=None):
        i = len(shares)
        dst = ex_piece(a, j, z, None)
        copy = pltpu.make_async_remote_copy(
            dst if src is None else src, dst, xs_s.at[i], xs_r.at[i],
            device_id=sib, device_id_type=MESH,
        )
        copy.start()
        shares.append((copy, (a, j, z)))

    def whole(a):
        ref = cold.at[a, d, pl.ds(LOCAL, ROWS - LOCAL), :]
        return pltpu.make_async_remote_copy(
            ref, ref, st_s.at[a], st_r.at[a], device_id=sib, device_id_type=MESH
        )

    whole(0).wait_recv()
    dp.start(0)
    ex.start(0)
    whole(1).wait_recv()
    dp.start(1)
    ex.start(1)
    share(0, x, zh, s.at[0, :, pl.ds(ROWS, SLOT), :])
    share(1, x, zh, s.at[1, :, pl.ds(ROWS, SLOT), :])
    ex.s2()
    ex.s3()
    dp.s2()
    dp.s3()
    ex.s4()
    ex.s5()
    ex.s6()
    for a, j, z in ((0, ex.jl, zh), (0, ex.jr, zh), (1, x, 1 - zh), (1, ex.jl, zh), (1, ex.jr, zh)):
        share(a, j, z)
    ex.s7()
    ex.s8()
    share(0, ex.jd, zh)
    dp.s4()
    dp.s5()
    dp.s6()
    ex.s9()
    ex.s10()
    share(1, ex.jl, 1 - zh)
    share(1, ex.jr, 1 - zh)
    dp.s7()
    dp.s8()
    dp.s9()
    dp.s10()
    ex.got("0oz", 0, x, 1 - zh, None)
    share(0, x, 1 - zh)
    ex.got("0lz", 0, ex.jl, 1 - zh, None)
    share(0, ex.jl, 1 - zh)
    ex.got("0rz", 0, ex.jr, 1 - zh, None)
    share(0, ex.jr, 1 - zh)
    ex.end_of_1_d()
    share(1, ex.jd, zh)
    ex.end_of_1_e()
    share(1, ex.jd, 1 - zh)
    ex.end_of_0_d()
    share(0, ex.jd, 1 - zh)
    for i, (copy, where) in enumerate(shares):
        ref = ex_other(*where, None)
        pltpu.make_async_remote_copy(
            ref, ref, xs_s.at[i], xs_r.at[i], device_id=sib, device_id_type=MESH
        ).wait_recv()
    dp.end_of_1_d()
    dp.end_of_1_e()
    dp.got("0oz", 0, y, 1 - zl, None)
    dp.got("0lz", 0, dp.jl, 1 - zl, None)
    dp.got("0rz", 0, dp.jr, 1 - zl, None)
    dp.end_of_0_d()
    for i in [1 - c] + list(range(2, E)):
        pltpu.make_async_remote_copy(
            ms.at[0], mr.at[i], m_s.at[0], m_r.at[i], device_id=sib, device_id_type=MESH
        ).wait_recv()
    for copy in sent:
        copy.wait()
    for copy in msent:
        copy.wait_send()
    whole(0).wait_send()
    whole(1).wait_send()
    for copy in own_out:
        copy.wait()
    for copy, _ in shares:
        copy.wait_send()
    dp.drain()
    ex.drain()


def dispatch(s, m):
    D = pltpu.SemaphoreType.DMA
    return pl.pallas_call(
        dispatch_kernel,
        in_specs=[ANY, ANY],
        out_specs=[ANY, ANY, ANY],
        out_shape=[
            jax.ShapeDtypeStruct((2, NDP, ROWS, W), bf16),
            jax.ShapeDtypeStruct((2, NDP, ROWS, W), bf16),
            jax.ShapeDtypeStruct((E, 8, 128), f32),
        ],
        scratch_shapes=[
            pltpu.VMEM((2, 2, NDP, SLOT, W), bf16),
            pltpu.VMEM((8, 128), f32),
            D((2,)), D((2,)), D((15,)), D((16,)), D, D,
            D((18,)), D((18,)), D((18,)), D((18,)), D((16,)), D((16,)), D((6,)),
        ],
        compiler_params=pltpu.CompilerParams(collective_id=1, has_side_effects=True),
        name="dispatch",
    )(s, m)


def sigmoid(v):
    return 1.0 / (1.0 + jnp.exp(-v))


def experts_kernel(
    hot_ref, gates_ref, cold, extra_hbm, wg, wu, wd,
    dxc, dxh, gp, gg, gu, gd,
    extra, acc, lhs, rhs, stage, sem, osem,
):
    hot = hot_ref[0] > 0
    FFL = wg.shape[0]

    @pl.when(hot)
    def _():
        pltpu.make_async_copy(extra_hbm, extra, sem).start()

    def cols(j):
        return pl.ds(pl.multiple_of(j * W, W), W)

    def forward(rows_ref, t):
        acc[...] = jnp.zeros_like(acc)

        def step(j, _):
            xj, dj = rows_ref[0, j], rows_ref[1, j]
            acc[0] += nt(wg[:, cols(j)], xj)
            acc[1] += nt(wu[:, cols(j)], xj)
            acc[2] += nt(wd[:, cols(j)], dj)
            return 0

        lax.fori_loop(0, NDP, step, 0)
        gate = gates_ref[t : t + 1, :]
        pre, up, g = acc[0], acc[1], acc[2]
        s = sigmoid(pre)
        active = pre * s
        hidden = (active * up).astype(bf16).astype(f32)
        gp[0:1, t * ROWS : (t + 1) * ROWS] = jnp.sum(hidden * g, axis=0, keepdims=True)
        gh = g * gate
        d_up = gh * active
        d_pre = gh * up * s * (1.0 + pre * (1.0 - s))
        lhs[t, 0] = d_pre.astype(bf16)
        lhs[t, 1] = d_up.astype(bf16)
        lhs[t, 2] = (hidden * gate).astype(bf16)
        rhs[t, :, 0:FFL] = d_pre.T.astype(bf16)
        rhs[t, :, FFL : 2 * FFL] = d_up.T.astype(bf16)

    forward(cold, 0)

    @pl.when(hot)
    def _():
        pltpu.make_async_copy(extra_hbm, extra, sem).wait()
        forward(extra, 1)

    @pl.when(jnp.logical_not(hot))
    def _():
        gp[0:1, ROWS : 2 * ROWS] = jnp.zeros((1, ROWS), f32)

    outs = (gg, gu, gd)

    def put(j, slot, i):
        return pltpu.make_async_copy(
            stage.at[slot, i], outs[i].at[:, cols(j)], osem.at[slot, i]
        )

    def step(j, sq):
        slot = j % 2

        @pl.when(j >= 2)
        def _():
            for i in range(3):
                put(j - 2, slot, i).wait()

        w2 = (wg[:, cols(j)], wu[:, cols(j)])

        def back(t, out):
            r = jnp.dot(rhs[t, :, 0:FFL], w2[0], preferred_element_type=f32)
            r += jnp.dot(rhs[t, :, FFL : 2 * FFL], w2[1], preferred_element_type=f32)
            out[j] = r.astype(bf16)

        back(0, dxc)
        for i in range(3):
            stage[slot, i] = jnp.dot(lhs[0, i], cold[i // 2, j], preferred_element_type=f32)

        @pl.when(hot)
        def _():
            back(1, dxh)
            for i in range(3):
                stage[slot, i] += jnp.dot(lhs[1, i], extra[i // 2, j], preferred_element_type=f32)

        @pl.when(jnp.logical_not(hot))
        def _():
            dxh[j] = jnp.zeros((ROWS, W), bf16)

        for i in range(3):
            v = stage[slot, i]
            sq = sq + jnp.sum((v * v).reshape(-1, 8, W), axis=0)
            put(j, slot, i).start()
        return sq

    sq = lax.fori_loop(0, NDP, step, jnp.zeros((8, W), f32))
    total = jnp.sum(jnp.sum(sq, axis=0, keepdims=True), axis=1, keepdims=True)
    gp[0:1, 2 * ROWS :] = jnp.broadcast_to(total, (1, GW - 2 * ROWS))
    for j in (NDP - 2, NDP - 1):
        for i in range(3):
            put(j, j % 2, i).wait()


def experts(hot, gates, cold, extra, wg, wu, wd):
    FFL, D = wg.shape
    return pl.pallas_call(
        experts_kernel,
        in_specs=[SM, VM, VM, ANY, VM, VM, VM],
        out_specs=[VM, VM, VM, ANY, ANY, ANY],
        out_shape=[
            jax.ShapeDtypeStruct((NDP, ROWS, W), bf16),
            jax.ShapeDtypeStruct((NDP, ROWS, W), bf16),
            jax.ShapeDtypeStruct((1, GW), f32),
        ]
        + [jax.ShapeDtypeStruct((FFL, D), f32)] * 3,
        scratch_shapes=[
            pltpu.VMEM((2, NDP, ROWS, W), bf16),
            pltpu.VMEM((3, FFL, ROWS), f32),
            pltpu.VMEM((2, 3, FFL, ROWS), bf16),
            pltpu.VMEM((2, ROWS, 2 * FFL), bf16),
            pltpu.VMEM((2, 3, FFL, W), f32),
            pltpu.SemaphoreType.DMA,
            pltpu.SemaphoreType.DMA((2, 3)),
        ],
        compiler_params=pltpu.CompilerParams(vmem_limit_bytes=60 * 1024 * 1024),
        name="experts",
    )(hot, gates, cold, extra, wg, wu, wd)


def add_rows(out, terms, rows):
    def step(i, _):
        r = pl.ds(pl.multiple_of(i * 32, 32), 32)
        total = terms[0][r, :].astype(f32)
        for term in terms[1:]:
            total = total + term[r, :].astype(f32)
        out[r, :] = total.astype(out.dtype)
        return 0

    lax.fori_loop(0, rows // 32, step, 0)


C_NAMES = (
    "c_rr", "c_rl", "c_dr", "c_dl", "c_sr", "c_sl", "c_z",
    "h_z2", "h_zr", "h_zl", "h_z0", "h_rr", "h_rl", "h_dr", "h_dl", "h_sr", "h_sl",
)


def combine_kernel(
    dxc, dxh, gp, back, gback,
    cr_l, cr_r, cs_r, cs_l, cf_l, cf_r, cz_s, cz_r, own,
    hz, hw, hr_l, hr_r, hf_l, hf_r, rc, rh, gall, gsum,
    ssem, rsem, g_s, g_r, b_s, b_r, gb_s, gb_r,
):
    e, d, x, zh, c, y, zl = place()
    zo = 1 - zl
    yr, yl, y2 = (y + 1) % 4, (y + 3) % 4, (y + 2) % 4
    right, left, pair = to(e, yr * 2 + zl), to(e, yl * 2 + zl), to(e, y * 2 + zo)
    peers, places, mine = [(0, expert_at(x, zh, 1 - c))], [1 - c], [c]
    for rel, seen, x2, zh2 in others(x, zh):
        for c2 in (0, 1):
            peers.append((rel, expert_at(x2, zh2, c2)))
            places.append(rel * 2 + c2)
            mine.append(seen * 2 + c)
    dps = [(d + k) % NDP for k in range(1, NDP)]
    meet([to(e2, d) for _, e2 in peers] + [to(e, d2) for d2 in dps])

    sent = []

    def send(name, src, dst, dev):
        i = C_NAMES.index(name)
        copy = pltpu.make_async_remote_copy(
            src, dst, ssem.at[i], rsem.at[i], device_id=dev, device_id_type=MESH
        )
        copy.start()
        sent.append(copy)

    def got(name, ref):
        i = C_NAMES.index(name)
        pltpu.make_async_remote_copy(
            ref, ref, ssem.at[i], rsem.at[i], device_id=pair, device_id_type=MESH
        ).wait_recv()

    H = ROWS // 2
    top, low = pl.ds(0, H), pl.ds(H, H)

    def both(j):
        return pl.ds(j * 2, 2)

    send("c_rr", dxc.at[both(y2), top], cr_l, right)
    send("c_rl", dxc.at[both(y2), low], cr_r, left)
    send("h_z2", dxh.at[y2 * 2 + zo], hz.at[y2], pair)
    send("h_zr", dxh.at[yr * 2 + zo], hz.at[yr], pair)
    send("h_zl", dxh.at[yl * 2 + zo], hz.at[yl], pair)
    send("h_z0", dxh.at[y * 2 + zo], hz.at[y], pair)
    gsends = []
    for k, d2 in enumerate(dps):
        copy = pltpu.make_async_remote_copy(
            gp, gall.at[d], g_s.at[k], g_r.at[k], device_id=to(e, d2), device_id_type=MESH
        )
        copy.start()
        gsends.append(copy)
    gall[d] = gp[...]
    send("c_dr", dxc.at[both(yr), low], cf_l.at[:, low], right)
    send("c_dl", dxc.at[both(yl), top], cf_r.at[:, top], left)

    for k in range(NDP - 1):
        src = (d + NDP - 1 - k) % NDP
        pltpu.make_async_remote_copy(
            gall.at[src], gall.at[src], g_s.at[k], g_r.at[k], device_id=pair, device_id_type=MESH
        ).wait_recv()
    total = gall[0]
    for k in range(1, NDP):
        total = total + gall[k]
    gsum[...] = total
    gback[e] = total
    for n, (_, e2) in enumerate(peers):
        copy = pltpu.make_async_remote_copy(
            gsum, gback.at[e], gb_s.at[n], gb_r.at[mine[n]], device_id=to(e2, d), device_id_type=MESH
        )
        copy.start()
        gsends.append(copy)

    got("c_rr", cr_l)
    for i in (0, 1):
        add_rows(cs_r.at[i], (dxc.at[yr * 2 + i, top], cr_l.at[i]), H)
    send("c_sr", cs_r, cf_l.at[:, top], right)
    got("c_rl", cr_r)
    for i in (0, 1):
        add_rows(cs_l.at[i], (dxc.at[yl * 2 + i, low], cr_r.at[i]), H)
    send("c_sl", cs_l, cf_r.at[:, low], left)

    got("h_z2", hz.at[y2])
    add_rows(hw.at[y2], (dxh.at[y2 * 2 + zl], hz.at[y2]), ROWS)
    send("h_rr", hw.at[y2, top], hr_l, right)
    send("h_rl", hw.at[y2, low], hr_r, left)
    got("h_zr", hz.at[yr])
    add_rows(hw.at[yr, low], (dxh.at[yr * 2 + zl, low], hz.at[yr, low]), H)
    send("h_dr", hw.at[yr, low], hf_l.at[low], right)
    got("h_zl", hz.at[yl])
    add_rows(hw.at[yl, top], (dxh.at[yl * 2 + zl, top], hz.at[yl, top]), H)
    send("h_dl", hw.at[yl, top], hf_r.at[top], left)
    got("h_rr", hr_l)
    add_rows(hw.at[yr, top], (dxh.at[yr * 2 + zl, top], hz.at[yr, top], hr_l), H)
    send("h_sr", hw.at[yr, top], hf_l.at[top], right)
    got("h_rl", hr_r)
    add_rows(hw.at[yl, low], (dxh.at[yl * 2 + zl, low], hz.at[yl, low], hr_r), H)
    send("h_sl", hw.at[yl, low], hf_r.at[low], left)

    got("c_dr", cf_l.at[:, low])
    got("c_dl", cf_r.at[:, top])
    got("c_sr", cf_l.at[:, top])
    got("c_sl", cf_r.at[:, low])
    add_rows(cz_s, (dxc.at[y * 2 + zo], cf_l.at[zo], cf_r.at[zo]), ROWS)
    send("c_z", cz_s, cz_r, pair)
    add_rows(own, (dxc.at[y * 2 + zl], cf_l.at[zl], cf_r.at[zl]), ROWS)

    def give(refs, half):
        for n, (_, e2) in enumerate(peers):
            at = places[n] if half == 0 else e2
            copy = pltpu.make_async_remote_copy(
                refs.at[pl.ds(pl.multiple_of(at * SLOT, SLOT), SLOT), :],
                back.at[e, pl.ds(half * SLOT, SLOT), :],
                b_s.at[half * 15 + n], b_r.at[half * E + mine[n]],
                device_id=to(e2, d), device_id_type=MESH,
            )
            copy.start()
            gsends.append(copy)
        at = c if half == 0 else e
        back[e, half * SLOT : (half + 1) * SLOT, :] = refs[
            pl.ds(pl.multiple_of(at * SLOT, SLOT), SLOT), :
        ]

    got("h_z0", hz.at[y])
    got("h_dr", hf_l.at[low])
    got("h_dl", hf_r.at[top])
    got("h_sr", hf_l.at[top])
    got("h_sl", hf_r.at[low])
    add_rows(rh, (dxh.at[y * 2 + zl], hz.at[y], hf_l, hf_r), ROWS)
    give(rh, 1)
    got("c_z", cz_r)
    add_rows(rc, (own, cz_r), ROWS)
    give(rc, 0)

    for i in [1 - c] + list(range(2, E)):
        for half in (0, 1):
            ref = back.at[0, pl.ds(half * SLOT, SLOT), :]
            pltpu.make_async_remote_copy(
                ref, ref, b_s.at[0], b_r.at[half * E + i], device_id=pair, device_id_type=MESH
            ).wait_recv()
        pltpu.make_async_remote_copy(
            gsum, gback.at[0], gb_s.at[0], gb_r.at[i], device_id=pair, device_id_type=MESH
        ).wait_recv()
    for copy in gsends + sent:
        copy.wait_send()


def combine(dxc, dxh, gp):
    D = pltpu.SemaphoreType.DMA
    H = ROWS // 2
    return pl.pallas_call(
        combine_kernel,
        in_specs=[VM, VM, VM],
        out_specs=[VM, VM],
        out_shape=[
            jax.ShapeDtypeStruct((E, 2 * SLOT, W), bf16),
            jax.ShapeDtypeStruct((E, 1, GW), f32),
        ],
        scratch_shapes=[
            pltpu.VMEM((2, H, W), bf16), pltpu.VMEM((2, H, W), bf16),
            pltpu.VMEM((2, H, W), bf16), pltpu.VMEM((2, H, W), bf16),
            pltpu.VMEM((2, ROWS, W), bf16), pltpu.VMEM((2, ROWS, W), bf16),
            pltpu.VMEM((ROWS, W), bf16), pltpu.VMEM((ROWS, W), bf16),
            pltpu.VMEM((ROWS, W), f32),
            pltpu.VMEM((4, ROWS, W), bf16), pltpu.VMEM((4, ROWS, W), bf16),
            pltpu.VMEM((H, W), bf16), pltpu.VMEM((H, W), bf16),
            pltpu.VMEM((ROWS, W), bf16), pltpu.VMEM((ROWS, W), bf16),
            pltpu.VMEM((ROWS, W), bf16), pltpu.VMEM((ROWS, W), bf16),
            pltpu.VMEM((NDP, 1, GW), f32), pltpu.VMEM((1, GW), f32),
            D((17,)), D((17,)), D((7,)), D((7,)), D((30,)), D((32,)), D((15,)), D((16,)),
        ],
        compiler_params=pltpu.CompilerParams(
            collective_id=2, has_side_effects=True, vmem_limit_bytes=60 * 1024 * 1024
        ),
        name="combine",
    )(dxc, dxh, gp)


def finish_kernel(ids_ref, logits_ref, back, gback, mr, rows_ref, gl_ref, norm_ref):
    e, _, x, zh, c, _, _ = place()
    ids = ids_ref[...]
    onehot, rank = row_facts(ids, E)
    probs = soft(logits_ref[...])
    n = ids.shape[1]
    slot = lax.broadcasted_iota(jnp.int32, (E * 2 * SLOT, n), 0)
    pick = (slot == ids * (2 * SLOT) + rank).astype(f32).astype(bf16)
    flat = back[...].reshape(E * 2 * SLOT, W)
    rows_ref[...] = tn(pick, flat).astype(bf16)
    rel = (((x - (ids >> 2)) & 3) * 2 + (zh ^ ((ids >> 1) & 1))) * 2 + c
    lane = jnp.where(rank < SLOT, rel * SLOT + rank, ROWS + e * SLOT + rank - SLOT)
    here = (slot == lane).astype(f32).astype(bf16)
    found = jnp.dot(gback[:, 0, 0 : 2 * ROWS].astype(bf16), here, preferred_element_type=f32)
    dgate = jnp.sum(onehot * found, axis=0, keepdims=True)
    count = jnp.sum(mr[...], axis=0)[2:3, :]
    across = lax.broadcasted_iota(jnp.int32, (E, 128), 0)
    diag = across == lax.broadcasted_iota(jnp.int32, (E, 128), 1)
    column = jnp.sum(jnp.where(diag, jnp.broadcast_to(count, (E, 128)), 0.0), axis=1, keepdims=True)
    pulls = onehot * dgate + 1.0 * E * (column / (E * n))
    gl_ref[...] = probs * (pulls - jnp.sum(probs * pulls, axis=0, keepdims=True))
    norm_ref[...] = jnp.sqrt(jnp.sum(gback[:, 0, 2 * ROWS : 2 * ROWS + 128], axis=0, keepdims=True))


def finish(ids, logits, back, gback, mr):
    n = ids.shape[1]
    return pl.pallas_call(
        finish_kernel,
        in_specs=[VM] * 5,
        out_specs=[VM] * 3,
        out_shape=[
            jax.ShapeDtypeStruct((n, W), bf16),
            jax.ShapeDtypeStruct((E, n), f32),
            jax.ShapeDtypeStruct((1, 128), f32),
        ],
        name="finish",
    )(ids, logits, back, gback, mr)


def local(rows_x, rows_dy, router_logits, expert_of, w_gate, w_up, w_down):
    e, _, x, zh, _, _, _ = place()
    ids = expert_of.reshape(1, -1)
    logits = router_logits.T
    s, m = lay_out(ids, logits, rows_x, rows_dy)
    cold, extra, mr = dispatch(s, m)
    b = jnp.arange(E, dtype=jnp.int32)
    rel = (((b >> 2) - x) & 3) * 4 + (((b >> 1) & 1) ^ zh) * 2 + (b & 1)
    order = (rel[:, None] == jnp.arange(E, dtype=jnp.int32)[None, :]).astype(f32)
    gates = jnp.stack(
        [mr[:, 0, :SLOT].reshape(ROWS), jnp.dot(order, mr[:, 1, :SLOT]).reshape(ROWS)]
    )
    hot = (m[e, 2, e] > SLOT).astype(jnp.int32).reshape(1)
    dxc, dxh, gp, gg, gu, gd = experts(hot, gates, cold, extra, w_gate[0], w_up[0], w_down[0])
    back, gback = combine(dxc, dxh, gp)
    grad_rows, grad_logits, norm = finish(ids, logits, back, gback, mr)
    return grad_rows, grad_logits.T, gg[None], gu[None], gd[None], norm[0, 0]


def solution(mesh):
    rows = P("expert", None)
    weights = P("expert", "dp", None)
    return jax.shard_map(
        local,
        mesh=mesh,
        in_specs=(rows, rows, rows, rows, weights, weights, weights),
        out_specs=(P("expert", "dp"), rows, weights, weights, weights, P()),
        check_vma=False,
    )
```

time: 682 us -> 222 us (0.33)
  waiting for transfers between devices: 275 us -> 0 us
  blocking collectives: 223 us -> 0 us
  Pallas kernels: 0 us -> 216 us
  matrix products: 69 us -> 0.19 us
  starting transfers between devices: 37.8 us -> 0 us
  local copies, waits for them, and re-layouts: 26.7 us -> 1.11 us
  other arithmetic: 24.8 us -> 1.88 us
  between operations: 18.5 us -> 1.36 us
    pallas_call x0 -> x5, Pallas kernels: none -> 216 us  [the longest x1 112 us: combine(): pl.pallas_call(combine_kernel, in_specs=[VM, VM, VM], out_specs=[VM, VM],...]
    psum x3 -> x0, blocking collectives: 213 us -> none  [the longest x1 132 us: local(): counts = lax.psum(jnp.sum(onehot, axis=0), 'expert')]
    reduce_scatter x1 -> x0, waiting for transfers between devices: 146 us -> none  [local(): lax.psum_scatter(input_terms.astype(jnp.bfloat16), 'dp', scatter_dimensio...]
    all_to_all x4 -> x0, waiting for transfers between devices: 129 us -> none  [the longest x2 122 us: local(): lax.all_to_all(as_sent(lay_out(sources, target, expert_total, capacity)),...]
    dot_general x9 -> x1, matrix products: 69 us -> 0.19 us  [local(): jnp.dot(order, mr[:, 1, :SLOT]).reshape(ROWS)]
    all_to_all x4 -> x0, starting transfers between devices: 37.7 us -> none  [the longest x2 18.1 us: local(): lax.all_to_all(as_sent(lay_out(sources, target, expert_total, capacity)),...]
    convert_element_type x6 -> x0, other arithmetic: 21.2 us -> none  [the longest x2 20.3 us: expert_backward(): (gates_in.astype(jnp.float32)[:, None] * grads_in.astype(jnp.float32)).as...]
    scatter x3 -> x0, local copies, waits for them, and re-layouts: 20.7 us -> none  [place_rows(): jnp.zeros((total,) + values.shape[1:], values.dtype).at[target]]
  transfers between devices with their start and end apart: 5 -> 0, of which waited for: 3 -> 0; matrix products, arithmetic and copies ran while one was open for 8% -> 0% of each run, Pallas kernels for 0% -> 0%
where the time goes in v1:
time: 222 us; the launch traced here: 220 us
  Pallas kernels  216 us (97%)
    pallas_call x1, Pallas kernels, combine(): pl.pallas_call(combine_kernel, in_specs=[VM, VM, VM], out_specs=[VM, VM],...  112 us
    pallas_call x1, Pallas kernels, dispatch(): pl.pallas_call(dispatch_kernel, in_specs=[ANY, ANY], out_specs=[ANY, ANY,...  69.6 us
    pallas_call x1, Pallas kernels, experts(): pl.pallas_call(experts_kernel, in_specs=[SM, VM, VM, ANY, VM, VM, VM], ou...  22.2 us
    pallas_call x1, Pallas kernels, lay_out(): pl.pallas_call(slots_kernel, grid=(NDP,), in_specs=[pl.BlockSpec((1, rows...  9.38 us

profile of v1, /device:TPU:1, one launch (start us, length us, event | category | flops | bytes accessed | tf_op | source)
XLA Modules:
  0.0 220.2 jit_solution(18129631920410505107)
XLA Ops:
  0.7 9.4 %lay_out.1 = (bf16[2,8,544,512]{3,2,1,0:T(8,128)(2,1)}, f32[16,8,128]{2,1,0:T(8,128)}) custom-call(s32[1,256]{1,0:T(1,128)} %bitcast.20, f32[16,256]{1,0:T(8,128)} %bitcast.17, bf16[256,4096]{1,0:T(8,128)(2,1)} %x_ref.1, bf16[256,4096]{1,0:T(8,128)(2,1)} %dy_ref.1), custom_call_target="tpu_custom_call" | custom-call | tf_op jit(solution)/shard_map/lay_out/pallas_call | solution.py:96
  10.1 1.3 fusion.2
  12.0 69.6 %dispatch.1 = (bf16[2,8,512,512]{3,2,1,0:T(8,128)(2,1)}, bf16[2,8,512,512]{3,2,1,0:T(8,128)(2,1)}, f32[16,8,128]{2,1,0:T(8,128)}) custom-call(bf16[2,8,544,512]{3,2,1,0:T(8,128)(2,1)} %get-tuple-element.23.s, f32[16,8,128]{2,1,0:T(8,128)} %get-tuple-element.22.ms), custom_call_target="tpu_custom_call" | custom-call | tf_op jit(solution)/shard_map/dispatch/pallas_call | solution.py:402
  81.6 0.9 slice_reduce_fusion
  82.5 0.1 stack_reshape_squeeze.3
  82.6 0.2 fusion
  82.8 0.1 stack_reshape.3
  82.9 0.6 pad_maximum_fusion.gates_ref
  83.5 22.2 %experts.1 = (bf16[8,512,512]{2,1,0:T(8,128)(2,1)}, bf16[8,512,512]{2,1,0:T(8,128)(2,1)}, f32[1,1280]{1,0:T(1,128)}, f32[192,4096]{1,0:T(8,128)}, f32[192,4096]{1,0:T(8,128)}, /*index=5*/f32[192,4096]{1,0:T(8,128)}) custom-call(s32[1]{0:T(128)} %bitcast.2.hot_ref, f32[2,512]{1,0:T(2,128)} %pad_maximum_fusion.gates_ref, ...), custom_call_target="tpu_custom_call" | custom-call | tf_op jit(solution)/shard_map/experts/pallas_call | solution.py:530
  105.6 111.8 %combine.1 = (bf16[16,64,512]{2,1,0:T(8,128)(2,1)}, f32[16,1,1280]{2,1,0:T(1,128)}) custom-call(bf16[8,512,512]{2,1,0:T(8,128)(2,1)} %get-tuple-element.27.dxc, bf16[8,512,512]{2,1,0:T(8,128)(2,1)} %get-tuple-element.28.dxh, f32[1,1280]{1,0:T(1,128)} %get-tuple-element.29.gp), custom_call_target="tpu_custom_call" | custom-call | tf_op jit(solution)/shard_map/combine/pallas_call | solution.py:724
  217.5 2.7 %finish.1 = (bf16[256,512]{1,0:T(8,128)(2,1)}, f32[16,256]{1,0:T(8,128)}, f32[1,128]{1,0:T(1,128)}) custom-call(s32[1,256]{1,0:T(1,128)} %bitcast.21, f32[16,256]{1,0:T(8,128)} %bitcast.18, bf16[16,64,512]{2,1,0:T(8,128)(2,1)} %get-tuple-element.30.back, f32[16,1,1280]{2,1,0:T(1,128)} %get-tuple-element.31.gback, f32[16,8,128]{2,1,0:T(8,128)} %get-tuple-element.24.mr), custom_call_target="tpu_custom_call" | custom-call | tf_op jit(solution)/shard_map/finish/pallas_call | solution.py:778
  (1 shorter events, 0.0 us)

commit v2 on v1

--- a/solution.py
+++ b/solution.py
@@ -18,7 +18,6 @@
 W = 512
 ROWS = E * SLOT
 LOCAL = 2 * SLOT
-SLOTS = ROWS + SLOT
 GW = 1280
 
 
@@ -61,56 +60,63 @@
     return lax.dot_general(a, b, (((0,), (0,)), ((), ())), preferred_element_type=f32)
 
 
-def slots_kernel(ids_ref, logits_ref, x_ref, dy_ref, s_ref, m_ref, perm):
-    @pl.when(pl.program_id(0) == 0)
-    def _():
-        ids = ids_ref[...]
-        onehot, rank = row_facts(ids, E)
-        rows = ids.shape[1]
-        target = jnp.where(rank < SLOT, ids * SLOT + rank, ROWS + rank - SLOT)
-        slot = lax.broadcasted_iota(jnp.int32, (SLOTS, rows), 0)
-        perm[...] = (slot == target).astype(f32).astype(bf16)
-        gate = jnp.sum(soft(logits_ref[...]) * onehot, axis=0, keepdims=True).astype(bf16)
-        gate = gate.astype(f32)
-        lane = lax.broadcasted_iota(jnp.int32, (128, rows), 0)
-        first = (lane == rank).astype(f32).astype(bf16)
-        extra = (lane == rank - SLOT).astype(f32).astype(bf16)
-        by_expert = (lane == ids).astype(f32).astype(bf16)
-        cold = (onehot * gate * (rank < SLOT).astype(f32)).astype(bf16)
-        cold = nt(cold, first)
-        gate8 = jnp.broadcast_to(gate, (8, rows)).astype(bf16)
-        hot = nt(gate8, extra)
-        count = nt(jnp.ones((8, rows), bf16), by_expert)
-        line = lax.broadcasted_iota(jnp.int32, (8, 128), 0)
-        for e in range(E):
-            mine = jnp.broadcast_to(cold[e : e + 1, :], (8, 128))
-            m_ref[e] = jnp.where(line == 0, mine, jnp.where(line == 1, hot, count))
-
-    p = perm[...]
-    s_ref[0, 0] = jnp.dot(p, x_ref[...], preferred_element_type=f32).astype(bf16)
-    s_ref[1, 0] = jnp.dot(p, dy_ref[...], preferred_element_type=f32).astype(bf16)
+def seen_from(ids, x, zh, c):
+    return (((x - (ids >> 2)) & 3) * 2 + (zh ^ ((ids >> 1) & 1))) * 2 + c
+
+
+def slots_kernel(ids_ref, logits_ref, x_ref, dy_ref, s1_ref, s2_ref, m_ref):
+    e, d, x, zh, c, y, zl = place()
+    ids = ids_ref[...]
+    onehot, rank = row_facts(ids, E)
+    rows = ids.shape[1]
+    none = -1
+
+    def perm(slots, target):
+        slot = lax.broadcasted_iota(jnp.int32, (slots, rows), 0)
+        return (slot == target).astype(f32).astype(bf16)
+
+    far = (zh ^ ((ids >> 1) & 1)) == 1
+    first = rank < SLOT
+    chip = ((ids >> 2) * 2 + (ids & 1)) * SLOT + rank
+    for g, ours in ((0, jnp.logical_not(far)), (1, far)):
+        p = perm(ROWS // 2, jnp.where(first & ours, chip, none))
+        at = pl.ds(pl.multiple_of((d if g == 0 else y * 2 + 1 - zl) * W, W), W)
+        s1_ref[0, g] = jnp.dot(p, x_ref[:, at], preferred_element_type=f32).astype(bf16)
+        s1_ref[1, g] = jnp.dot(p, dy_ref[:, at], preferred_element_type=f32).astype(bf16)
+    home = jnp.where(ids == e, rank, jnp.where(ids == e + 1 - 2 * c, SLOT + rank, none))
+    p = perm(3 * SLOT, jnp.where(first, home, SLOT + rank))
+    for j in range(NDP):
+        at = slice(j * W, (j + 1) * W)
+        s2_ref[0, j] = jnp.dot(p, x_ref[:, at], preferred_element_type=f32).astype(bf16)
+        s2_ref[1, j] = jnp.dot(p, dy_ref[:, at], preferred_element_type=f32).astype(bf16)
+
+    gate = jnp.sum(soft(logits_ref[...]) * onehot, axis=0, keepdims=True).astype(bf16).astype(f32)
+    lane = lax.broadcasted_iota(jnp.int32, (128, rows), 0)
+    spot = (seen_from(ids, x, zh, c) & 3) * SLOT + rank
+    cold = (onehot * gate * first.astype(f32)).astype(bf16)
+    cold = nt(cold, (lane == spot).astype(f32).astype(bf16))
+    gate8 = jnp.broadcast_to(gate, (8, rows)).astype(bf16)
+    spot = jnp.where(first, none, (e & 3) * SLOT + rank - SLOT)
+    hot = nt(gate8, (lane == spot).astype(f32).astype(bf16))
+    count = nt(jnp.ones((8, rows), bf16), (lane == ids).astype(f32).astype(bf16))
+    line = lax.broadcasted_iota(jnp.int32, (8, 128), 0)
+    for k in range(E):
+        mine = jnp.broadcast_to(cold[k : k + 1, :], (8, 128))
+        busy = (jnp.sum(onehot[k : k + 1, :], axis=1, keepdims=True) > SLOT).astype(f32)
+        rest = jnp.where(line == 2, count, jnp.broadcast_to(busy, (8, 128)))
+        m_ref[k] = jnp.where(line == 0, mine, jnp.where(line == 1, hot, rest))
 
 
 def lay_out(ids, logits, x, dy):
-    rows = x.shape[0]
     return pl.pallas_call(
         slots_kernel,
-        grid=(NDP,),
-        in_specs=[
-            pl.BlockSpec((1, rows), lambda j: (0, 0)),
-            pl.BlockSpec((E, rows), lambda j: (0, 0)),
-            pl.BlockSpec((rows, W), lambda j: (0, j)),
-            pl.BlockSpec((rows, W), lambda j: (0, j)),
-        ],
-        out_specs=[
-            pl.BlockSpec((2, 1, SLOTS, W), lambda j: (0, j, 0, 0)),
-            pl.BlockSpec((E, 8, 128), lambda j: (0, 0, 0)),
-        ],
+        in_specs=[VM] * 4,
+        out_specs=[VM] * 3,
         out_shape=[
-            jax.ShapeDtypeStruct((2, NDP, SLOTS, W), bf16),
+            jax.ShapeDtypeStruct((2, 2, ROWS // 2, W), bf16),
+            jax.ShapeDtypeStruct((2, NDP, 3 * SLOT, W), bf16),
             jax.ShapeDtypeStruct((E, 8, 128), f32),
         ],
-        scratch_shapes=[pltpu.VMEM((SLOTS, rows), bf16)],
         name="lay_out",
     )(ids, logits, x, dy)
 
@@ -221,7 +227,7 @@
 
 
 def dispatch_kernel(
-    s, ms, cold, extra, mr, bounce, mbounce,
+    s1, s2, ms, cold, extra, mr, bounce, mbounce,
     st_s, st_r, m_s, m_r, sib_s, sib_r, dp_s, dp_r, ex_s, ex_r, xs_s, xs_r, loc,
 ):
     e, d, x, zh, c, y, zl = place()
@@ -229,35 +235,33 @@
     sib = to(expert_at(x, zh, 1 - c), d)
     d_r, d_l = ((y + 1) % 4) * 2 + zl, ((y + 3) % 4) * 2 + zl
     peers = [
-        (rel, back, expert_at(x2, zh2, c2), d if rel % 2 == 0 else dbar)
+        (rel, back, expert_at(x2, zh2, c2), d if rel % 2 == 0 else dbar, x2 * 2 + c2)
         for rel, back, x2, zh2 in others(x, zh)
         for c2 in (0, 1)
     ]
     x_r = to(expert_at((x + 1) % 4, zh, c), d)
     x_l = to(expert_at((x + 3) % 4, zh, c), d)
     z_p = to(expert_at(x, 1 - zh, c), dbar)
-    meet([to(e2, d2) for _, _, e2, d2 in peers] + [sib, to(e, d_r), to(e, d_l), to(e, dbar)])
+    meet([to(p[2], p[3]) for p in peers] + [sib, to(e, d_r), to(e, d_l), to(e, dbar)])
 
     sent, msent = [], []
     for a in (0, 1):
-        for rel, back, e2, d2 in peers:
+        for rel, back, e2, d2, q in peers:
             copy = pltpu.make_async_remote_copy(
-                s.at[a, d2, pl.ds(pl.multiple_of(e2 * SLOT, SLOT), SLOT), :],
+                s1.at[a, rel % 2, pl.ds(pl.multiple_of(q * SLOT, SLOT), SLOT), :],
                 cold.at[a, d2, pl.ds(pl.multiple_of((back * 2 + c) * SLOT, SLOT), SLOT), :],
                 st_s.at[a], st_r.at[a], device_id=to(e2, d2), device_id_type=MESH,
             )
             copy.start()
         if a == 0:
             own_in = [
-                pltpu.make_async_copy(
-                    s.at[:, :, pl.ds(pl.multiple_of(e * SLOT, SLOT), SLOT), :], bounce.at[0], loc.at[0]
-                ),
-                pltpu.make_async_copy(s.at[:, :, pl.ds(ROWS, SLOT), :], bounce.at[1], loc.at[1]),
+                pltpu.make_async_copy(s2.at[:, :, 0:SLOT, :], bounce.at[0], loc.at[0]),
+                pltpu.make_async_copy(s2.at[:, :, 2 * SLOT :, :], bounce.at[1], loc.at[1]),
                 pltpu.make_async_copy(ms.at[e], mbounce, loc.at[2]),
             ]
             for copy in own_in:
                 copy.start()
-    for n, (rel, back, e2, d2) in enumerate(peers + [(0, 0, expert_at(x, zh, 1 - c), d)]):
+    for n, (_, back, e2, d2, _) in enumerate(peers + [(0, 0, expert_at(x, zh, 1 - c), d, 0)]):
         copy = pltpu.make_async_remote_copy(
             ms.at[e2], mr.at[back * 2 + c], m_s.at[n], m_r.at[back * 2 + c],
             device_id=to(e2, d2), device_id_type=MESH,
@@ -265,7 +269,7 @@
         copy.start()
         msent.append(copy)
     sib_copy = pltpu.make_async_remote_copy(
-        s.at[:, :, pl.ds(pl.multiple_of((e + 1 - 2 * c) * SLOT, SLOT), SLOT), :],
+        s2.at[:, :, SLOT : 2 * SLOT, :],
         cold.at[:, :, pl.ds(pl.multiple_of(c * SLOT, SLOT), SLOT), :],
         sib_s, sib_r, device_id=sib, device_id_type=MESH,
     )
@@ -305,7 +309,7 @@
         to(e, d_r), to(e, d_l), to(e, dbar), dp_s, dp_r,
     )
     ex = Gather(
-        lambda a: s.at[a, :, pl.ds(ROWS, SLOT), :], ex_piece, x, zh, x_r, x_l, z_p, ex_s, ex_r,
+        lambda a: s2.at[a, :, 2 * SLOT :, :], ex_piece, x, zh, x_r, x_l, z_p, ex_s, ex_r,
     )
     shares = []
 
@@ -331,8 +335,8 @@
     whole(1).wait_recv()
     dp.start(1)
     ex.start(1)
-    share(0, x, zh, s.at[0, :, pl.ds(ROWS, SLOT), :])
-    share(1, x, zh, s.at[1, :, pl.ds(ROWS, SLOT), :])
+    share(0, x, zh, s2.at[0, :, 2 * SLOT :, :])
+    share(1, x, zh, s2.at[1, :, 2 * SLOT :, :])
     ex.s2()
     ex.s3()
     dp.s2()
@@ -397,11 +401,11 @@
     ex.drain()
 
 
-def dispatch(s, m):
+def dispatch(s1, s2, m):
     D = pltpu.SemaphoreType.DMA
     return pl.pallas_call(
         dispatch_kernel,
-        in_specs=[ANY, ANY],
+        in_specs=[ANY, ANY, ANY],
         out_specs=[ANY, ANY, ANY],
         out_shape=[
             jax.ShapeDtypeStruct((2, NDP, ROWS, W), bf16),
@@ -416,15 +420,27 @@
         ],
         compiler_params=pltpu.CompilerParams(collective_id=1, has_side_effects=True),
         name="dispatch",
-    )(s, m)
+    )(s1, s2, m)
 
 
 def sigmoid(v):
     return 1.0 / (1.0 + jnp.exp(-v))
 
 
+def gate_row(mr, t):
+    _, _, x, _, c, _, _ = place()
+    parts = []
+    for g in range(E // 4):
+        at = g * 4 if t == 0 else ((g - x) & 3) * 4
+        part = mr[at, t : t + 1, :]
+        for i in range(1, 4):
+            part = part + mr[at + i, t : t + 1, :]
+        parts.append(part if t == 0 else part * mr[c, 3:4, :])
+    return jnp.concatenate(parts, axis=1)
+
+
 def experts_kernel(
-    hot_ref, gates_ref, cold, extra_hbm, wg, wu, wd,
+    hot_ref, mr, cold, extra_hbm, wg, wu, wd,
     dxc, dxh, gp, gg, gu, gd,
     extra, acc, lhs, rhs, stage, sem, osem,
 ):
@@ -449,7 +465,7 @@
             return 0
 
         lax.fori_loop(0, NDP, step, 0)
-        gate = gates_ref[t : t + 1, :]
+        gate = gate_row(mr, t)
         pre, up, g = acc[0], acc[1], acc[2]
         s = sigmoid(pre)
         active = pre * s
@@ -525,7 +541,7 @@
             put(j, j % 2, i).wait()
 
 
-def experts(hot, gates, cold, extra, wg, wu, wd):
+def experts(hot, mr, cold, extra, wg, wu, wd):
     FFL, D = wg.shape
     return pl.pallas_call(
         experts_kernel,
@@ -548,199 +564,293 @@
         ],
         compiler_params=pltpu.CompilerParams(vmem_limit_bytes=60 * 1024 * 1024),
         name="experts",
-    )(hot, gates, cold, extra, wg, wu, wd)
-
-
-def add_rows(out, terms, rows):
-    def step(i, _):
-        r = pl.ds(pl.multiple_of(i * 32, 32), 32)
-        total = terms[0][r, :].astype(f32)
-        for term in terms[1:]:
-            total = total + term[r, :].astype(f32)
-        out[r, :] = total.astype(out.dtype)
-        return 0
-
-    lax.fori_loop(0, rows // 32, step, 0)
-
-
-C_NAMES = (
-    "c_rr", "c_rl", "c_dr", "c_dl", "c_sr", "c_sl", "c_z",
-    "h_z2", "h_zr", "h_zl", "h_z0", "h_rr", "h_rl", "h_dr", "h_dl", "h_sr", "h_sl",
-)
-
-
-def combine_kernel(
-    dxc, dxh, gp, back, gback,
-    cr_l, cr_r, cs_r, cs_l, cf_l, cf_r, cz_s, cz_r, own,
-    hz, hw, hr_l, hr_r, hf_l, hf_r, rc, rh, gall, gsum,
-    ssem, rsem, g_s, g_r, b_s, b_r, gb_s, gb_r,
-):
+    )(hot, mr, cold, extra, wg, wu, wd)
+
+
+def add_into(out, *terms):
+    n, rows, _ = out.shape
+    step_rows = min(rows, 64)
+    for i in range(n):
+
+        def step(k, _):
+            r = pl.ds(pl.multiple_of(k * step_rows, step_rows), step_rows)
+            total = terms[0][i, r, :].astype(f32)
+            for term in terms[1:]:
+                total = total + term[i, r, :].astype(f32)
+            out[i, r, :] = total.astype(out.dtype)
+            return 0
+
+        if rows == step_rows:
+            step(0, 0)
+        else:
+            lax.fori_loop(0, rows // step_rows, step, 0)
+
+
+class Scatter:
+    names = (
+        "ar0", "ar1", "al0", "al1", "br0", "br1", "bl0", "bl1", "cr0", "cr1", "cl0", "cl1", "p",
+        "zd", "zr", "zl", "z0", "hr", "hl", "ir", "il", "kr", "kl",
+    )
+
+    @staticmethod
+    def scratch(piece, half):
+        V = pltpu.VMEM
+        return [
+            V((2,) + half, bf16), V((2,) + half, bf16), V((2,) + half, bf16), V((2,) + half, bf16),
+            V((2,) + piece, bf16), V((2,) + piece, bf16),
+            V(piece, bf16), V(piece, bf16), V(piece, f32),
+            V((4,) + piece, bf16), V((4,) + piece, bf16),
+            V(half, bf16), V(half, bf16), V(piece, bf16), V(piece, bf16),
+            pltpu.SemaphoreType.DMA((23,)), pltpu.SemaphoreType.DMA((23,)),
+        ]
+
+    def __init__(self, chunk, cut, j, z, right, left, pair, refs):
+        self.chunk, self.cut, self.j, self.z = chunk, cut, j, z
+        self.jl, self.jr, self.jd = (j + 3) % 4, (j + 1) % 4, (j + 2) % 4
+        self.right, self.left, self.pair = right, left, pair
+        (
+            self.rl, self.rr, self.tr, self.tl, self.fl, self.fr, self.zs, self.zin, self.own,
+            self.hz, self.hw, self.hrl, self.hrr, self.hfl, self.hfr, self.ssem, self.rsem,
+        ) = refs
+        self.sent = []
+
+    def send(self, name, src, dst, dev):
+        i = self.names.index(name)
+        copy = pltpu.make_async_remote_copy(
+            src, dst, self.ssem.at[i], self.rsem.at[i], device_id=dev, device_id_type=MESH
+        )
+        copy.start()
+        self.sent.append(copy)
+
+    def got(self, name, ref):
+        i = self.names.index(name)
+        pltpu.make_async_remote_copy(
+            ref, ref, self.ssem.at[i], self.rsem.at[i], device_id=self.pair, device_id_type=MESH
+        ).wait_recv()
+
+    def start0_far(self):
+        for k in (0, 1):
+            far = self.chunk(0, self.jd, k)
+            self.send(f"ar{k}", self.cut(far, 0), self.rl.at[k], self.right)
+            self.send(f"al{k}", self.cut(far, 1), self.rr.at[k], self.left)
+
+    def start0_near(self):
+        for k in (0, 1):
+            right, left = self.chunk(0, self.jr, k), self.chunk(0, self.jl, k)
+            self.send(f"br{k}", self.cut(right, 1), self.cut(self.fl.at[k], 1), self.right)
+            self.send(f"bl{k}", self.cut(left, 0), self.cut(self.fr.at[k], 0), self.left)
+
+    def start1(self):
+        for way, j in (("d", self.jd), ("r", self.jr), ("l", self.jl), ("0", self.j)):
+            self.send("z" + way, self.chunk(1, j, 1 - self.z), self.hz.at[j], self.pair)
+
+    def relay0(self):
+        for k in (0, 1):
+            self.got(f"ar{k}", self.rl.at[k])
+            add_into(self.tr.at[k], self.cut(self.chunk(0, self.jr, k), 0), self.rl.at[k])
+            self.send(f"cr{k}", self.tr.at[k], self.cut(self.fl.at[k], 0), self.right)
+            self.got(f"al{k}", self.rr.at[k])
+            add_into(self.tl.at[k], self.cut(self.chunk(0, self.jl, k), 1), self.rr.at[k])
+            self.send(f"cl{k}", self.tl.at[k], self.cut(self.fr.at[k], 1), self.left)
+
+    def pair0(self):
+        for k in (0, 1):
+            for n, ref, h in (("br", self.fl, 1), ("bl", self.fr, 0), ("cr", self.fl, 0), ("cl", self.fr, 1)):
+                self.got(f"{n}{k}", self.cut(ref.at[k], h))
+        k = 1 - self.z
+        add_into(self.zs, self.chunk(0, self.j, k), self.fl.at[k], self.fr.at[k])
+        self.send("p", self.zs, self.zin, self.pair)
+        k = self.z
+        add_into(self.own, self.chunk(0, self.j, k), self.fl.at[k], self.fr.at[k])
+
+    def end0(self, out):
+        self.got("p", self.zin)
+        add_into(out, self.own, self.zin)
+
+    def relay1_far(self):
+        self.got("zd", self.hz.at[self.jd])
+        w = self.hw.at[self.jd]
+        add_into(w, self.chunk(1, self.jd, self.z), self.hz.at[self.jd])
+        self.send("hr", self.cut(w, 0), self.hrl, self.right)
+        self.send("hl", self.cut(w, 1), self.hrr, self.left)
+
+    def relay1_near(self):
+        for way, j, h, ref, dev in (
+            ("r", self.jr, 1, self.hfl, self.right), ("l", self.jl, 0, self.hfr, self.left)
+        ):
+            self.got("z" + way, self.hz.at[j])
+            w = self.cut(self.hw.at[j], h)
+            add_into(w, self.cut(self.chunk(1, j, self.z), h), self.cut(self.hz.at[j], h))
+            self.send("i" + way, w, self.cut(ref, h), dev)
+
+    def relay1_last(self):
+        for way, j, h, inp, ref, dev in (
+            ("r", self.jr, 0, self.hrl, self.hfl, self.right),
+            ("l", self.jl, 1, self.hrr, self.hfr, self.left),
+        ):
+            self.got("h" + way, inp)
+            w = self.cut(self.hw.at[j], h)
+            add_into(w, self.cut(self.chunk(1, j, self.z), h), self.cut(self.hz.at[j], h), inp)
+            self.send("k" + way, w, self.cut(ref, h), dev)
+
+    def end1(self, out):
+        self.got("z0", self.hz.at[self.j])
+        self.got("ir", self.cut(self.hfl, 1))
+        self.got("il", self.cut(self.hfr, 0))
+        self.got("kr", self.cut(self.hfl, 0))
+        self.got("kl", self.cut(self.hfr, 1))
+        add_into(out, self.chunk(1, self.j, self.z), self.hz.at[self.j], self.hfl, self.hfr)
+
+    def drain(self):
+        for copy in self.sent:
+            copy.wait_send()
+
+
+HR = ROWS // 2
+C_PIECE, C_HALF = (1, HR, W), (1, HR // 2, W)
+H_PIECE, H_HALF = (NDP // 2, SLOT, W), (NDP // 4, SLOT, W)
+
+
+def combine_kernel(dxc, dxh, gp, back, backh, gback, *refs):
     e, d, x, zh, c, y, zl = place()
-    zo = 1 - zl
-    yr, yl, y2 = (y + 1) % 4, (y + 3) % 4, (y + 2) % 4
-    right, left, pair = to(e, yr * 2 + zl), to(e, yl * 2 + zl), to(e, y * 2 + zo)
-    peers, places, mine = [(0, expert_at(x, zh, 1 - c))], [1 - c], [c]
+    c_refs, refs = refs[:17], refs[17:]
+    h_refs, refs = refs[:17], refs[17:]
+    rc, hs, hin, outh, hp, gall, gsum, g_s, g_r, b_s, b_r, gb_s, gb_r, x_s, x_r, q_s, q_r = refs
+    dbar = y * 2 + 1 - zl
+    sib = to(expert_at(x, zh, 1 - c), d)
+    peers, places, mine = [expert_at(x, zh, 1 - c)], [1 - c], [c]
     for rel, seen, x2, zh2 in others(x, zh):
         for c2 in (0, 1):
-            peers.append((rel, expert_at(x2, zh2, c2)))
+            peers.append(expert_at(x2, zh2, c2))
             places.append(rel * 2 + c2)
             mine.append(seen * 2 + c)
     dps = [(d + k) % NDP for k in range(1, NDP)]
-    meet([to(e2, d) for _, e2 in peers] + [to(e, d2) for d2 in dps])
-
-    sent = []
-
-    def send(name, src, dst, dev):
-        i = C_NAMES.index(name)
+    z_p = to(expert_at(x, 1 - zh, c), dbar)
+    meet([to(e2, d) for e2 in peers] + [to(e, d2) for d2 in dps] + [z_p])
+
+    C = Scatter(
+        lambda a, j, z: dxc.at[pl.ds(j * 2 + z, 1), pl.ds(a * HR, HR)],
+        lambda ref, h: ref.at[:, pl.ds(h * (HR // 2), HR // 2)],
+        y, zl, to(e, ((y + 1) % 4) * 2 + zl), to(e, ((y + 3) % 4) * 2 + zl), to(e, dbar), c_refs,
+    )
+    X = Scatter(
+        lambda a, j, z: hs.at[j * 2 + z, pl.ds(a * (NDP // 2), NDP // 2)],
+        lambda ref, h: ref.at[pl.ds(h * (NDP // 4), NDP // 4)],
+        x, zh, to(expert_at((x + 1) % 4, zh, c), d), to(expert_at((x + 3) % 4, zh, c), d), z_p,
+        h_refs,
+    )
+    far = [X.jd * 2, X.jd * 2 + 1, X.jr * 2, X.jl * 2, X.jr * 2 + 1, X.jl * 2 + 1, x * 2, x * 2 + 1]
+
+    def h_rows(chip, core):
+        return pl.ds(pl.multiple_of((chip * 2 + core) * SLOT, SLOT), SLOT)
+
+    rest = []
+
+    def send(src, dst, ssem, rsem, dev):
         copy = pltpu.make_async_remote_copy(
-            src, dst, ssem.at[i], rsem.at[i], device_id=dev, device_id_type=MESH
+            src, dst, ssem, rsem, device_id=dev, device_id_type=MESH
         )
         copy.start()
-        sent.append(copy)
-
-    def got(name, ref):
-        i = C_NAMES.index(name)
+        rest.append(copy)
+
+    def wait(ref, ssem, rsem):
         pltpu.make_async_remote_copy(
-            ref, ref, ssem.at[i], rsem.at[i], device_id=pair, device_id_type=MESH
+            ref, ref, ssem, rsem, device_id=sib, device_id_type=MESH
         ).wait_recv()
 
-    H = ROWS // 2
-    top, low = pl.ds(0, H), pl.ds(H, H)
-
-    def both(j):
-        return pl.ds(j * 2, 2)
-
-    send("c_rr", dxc.at[both(y2), top], cr_l, right)
-    send("c_rl", dxc.at[both(y2), low], cr_r, left)
-    send("h_z2", dxh.at[y2 * 2 + zo], hz.at[y2], pair)
-    send("h_zr", dxh.at[yr * 2 + zo], hz.at[yr], pair)
-    send("h_zl", dxh.at[yl * 2 + zo], hz.at[yl], pair)
-    send("h_z0", dxh.at[y * 2 + zo], hz.at[y], pair)
-    gsends = []
+    C.start0_far()
+    C.start1()
+    for i, chip in enumerate(far):
+        send(dxh.at[:, h_rows(chip, 1 - c)], hin.at[chip], x_s.at[i], x_r.at[i], sib)
+    C.start0_near()
     for k, d2 in enumerate(dps):
-        copy = pltpu.make_async_remote_copy(
-            gp, gall.at[d], g_s.at[k], g_r.at[k], device_id=to(e, d2), device_id_type=MESH
-        )
-        copy.start()
-        gsends.append(copy)
+        send(gp, gall.at[d], g_s.at[k], g_r.at[k], to(e, d2))
     gall[d] = gp[...]
-    send("c_dr", dxc.at[both(yr), low], cf_l.at[:, low], right)
-    send("c_dl", dxc.at[both(yl), top], cf_r.at[:, top], left)
+    for i, chip in enumerate(far):
+        wait(hin.at[chip], x_s.at[i], x_r.at[i])
+        add_into(hs.at[chip], dxh.at[:, h_rows(chip, c)], hin.at[chip])
+        if i == 1:
+            X.start0_far()
+        if i == 5:
+            X.start0_near()
+    X.start1()
 
     for k in range(NDP - 1):
-        src = (d + NDP - 1 - k) % NDP
-        pltpu.make_async_remote_copy(
-            gall.at[src], gall.at[src], g_s.at[k], g_r.at[k], device_id=pair, device_id_type=MESH
-        ).wait_recv()
+        wait(gall.at[(d + NDP - 1 - k) % NDP], g_s.at[k], g_r.at[k])
     total = gall[0]
     for k in range(1, NDP):
         total = total + gall[k]
     gsum[...] = total
     gback[e] = total
-    for n, (_, e2) in enumerate(peers):
-        copy = pltpu.make_async_remote_copy(
-            gsum, gback.at[e], gb_s.at[n], gb_r.at[mine[n]], device_id=to(e2, d), device_id_type=MESH
-        )
-        copy.start()
-        gsends.append(copy)
-
-    got("c_rr", cr_l)
-    for i in (0, 1):
-        add_rows(cs_r.at[i], (dxc.at[yr * 2 + i, top], cr_l.at[i]), H)
-    send("c_sr", cs_r, cf_l.at[:, top], right)
-    got("c_rl", cr_r)
-    for i in (0, 1):
-        add_rows(cs_l.at[i], (dxc.at[yl * 2 + i, low], cr_r.at[i]), H)
-    send("c_sl", cs_l, cf_r.at[:, low], left)
-
-    got("h_z2", hz.at[y2])
-    add_rows(hw.at[y2], (dxh.at[y2 * 2 + zl], hz.at[y2]), ROWS)
-    send("h_rr", hw.at[y2, top], hr_l, right)
-    send("h_rl", hw.at[y2, low], hr_r, left)
-    got("h_zr", hz.at[yr])
-    add_rows(hw.at[yr, low], (dxh.at[yr * 2 + zl, low], hz.at[yr, low]), H)
-    send("h_dr", hw.at[yr, low], hf_l.at[low], right)
-    got("h_zl", hz.at[yl])
-    add_rows(hw.at[yl, top], (dxh.at[yl * 2 + zl, top], hz.at[yl, top]), H)
-    send("h_dl", hw.at[yl, top], hf_r.at[top], left)
-    got("h_rr", hr_l)
-    add_rows(hw.at[yr, top], (dxh.at[yr * 2 + zl, top], hz.at[yr, top], hr_l), H)
-    send("h_sr", hw.at[yr, top], hf_l.at[top], right)
-    got("h_rl", hr_r)
-    add_rows(hw.at[yl, low], (dxh.at[yl * 2 + zl, low], hz.at[yl, low], hr_r), H)
-    send("h_sl", hw.at[yl, low], hf_r.at[low], left)
-
-    got("c_dr", cf_l.at[:, low])
-    got("c_dl", cf_r.at[:, top])
-    got("c_sr", cf_l.at[:, top])
-    got("c_sl", cf_r.at[:, low])
-    add_rows(cz_s, (dxc.at[y * 2 + zo], cf_l.at[zo], cf_r.at[zo]), ROWS)
-    send("c_z", cz_s, cz_r, pair)
-    add_rows(own, (dxc.at[y * 2 + zl], cf_l.at[zl], cf_r.at[zl]), ROWS)
-
-    def give(refs, half):
-        for n, (_, e2) in enumerate(peers):
-            at = places[n] if half == 0 else e2
-            copy = pltpu.make_async_remote_copy(
-                refs.at[pl.ds(pl.multiple_of(at * SLOT, SLOT), SLOT), :],
-                back.at[e, pl.ds(half * SLOT, SLOT), :],
-                b_s.at[half * 15 + n], b_r.at[half * E + mine[n]],
-                device_id=to(e2, d), device_id_type=MESH,
-            )
-            copy.start()
-            gsends.append(copy)
-        at = c if half == 0 else e
-        back[e, half * SLOT : (half + 1) * SLOT, :] = refs[
-            pl.ds(pl.multiple_of(at * SLOT, SLOT), SLOT), :
-        ]
-
-    got("h_z0", hz.at[y])
-    got("h_dr", hf_l.at[low])
-    got("h_dl", hf_r.at[top])
-    got("h_sr", hf_l.at[top])
-    got("h_sl", hf_r.at[low])
-    add_rows(rh, (dxh.at[y * 2 + zl], hz.at[y], hf_l, hf_r), ROWS)
-    give(rh, 1)
-    got("c_z", cz_r)
-    add_rows(rc, (own, cz_r), ROWS)
-    give(rc, 0)
+    for n, e2 in enumerate(peers):
+        send(gsum, gback.at[e], gb_s.at[n], gb_r.at[mine[n]], to(e2, d))
+
+    C.relay0()
+    C.relay1_far()
+    X.relay0()
+    X.relay1_far()
+    X.relay1_near()
+    C.relay1_near()
+    X.relay1_last()
+    X.pair0()
+    C.relay1_last()
+    C.pair0()
+    X.end1(outh.at[pl.ds(NDP // 2, NDP // 2)])
+    X.end0(outh.at[pl.ds(0, NDP // 2)])
+    for k, d2 in enumerate(dps):
+        send(outh.at[d2], hp.at[d], q_s.at[k], q_r.at[k], to(e, d2))
+    hp[d] = outh[d]
+
+    def give(a):
+        for n, e2 in enumerate(peers):
+            if (n >= 7) == (a == 1):
+                send(
+                    rc.at[0, pl.ds(pl.multiple_of(places[n] * SLOT, SLOT), SLOT), :],
+                    back.at[e], b_s.at[n], b_r.at[mine[n]], to(e2, d),
+                )
+
+    C.end1(rc.at[:, pl.ds(HR, HR)])
+    give(1)
+    C.end0(rc.at[:, pl.ds(0, HR)])
+    give(0)
+    back[e] = rc[0, pl.ds(pl.multiple_of(c * SLOT, SLOT), SLOT), :]
+    for k in range(NDP - 1):
+        wait(hp.at[(d + NDP - 1 - k) % NDP], q_s.at[k], q_r.at[k])
+    total = hp[0].astype(f32)
+    for k in range(1, NDP):
+        total = total + hp[k].astype(f32)
+    backh[...] = total.astype(bf16)
 
     for i in [1 - c] + list(range(2, E)):
-        for half in (0, 1):
-            ref = back.at[0, pl.ds(half * SLOT, SLOT), :]
-            pltpu.make_async_remote_copy(
-                ref, ref, b_s.at[0], b_r.at[half * E + i], device_id=pair, device_id_type=MESH
-            ).wait_recv()
-        pltpu.make_async_remote_copy(
-            gsum, gback.at[0], gb_s.at[0], gb_r.at[i], device_id=pair, device_id_type=MESH
-        ).wait_recv()
-    for copy in gsends + sent:
+        wait(back.at[0], b_s.at[0], b_r.at[i])
+        wait(gback.at[0], gb_s.at[0], gb_r.at[i])
+    for copy in rest:
         copy.wait_send()
+    C.drain()
+    X.drain()
 
 
 def combine(dxc, dxh, gp):
     D = pltpu.SemaphoreType.DMA
-    H = ROWS // 2
+    V = pltpu.VMEM
     return pl.pallas_call(
         combine_kernel,
         in_specs=[VM, VM, VM],
-        out_specs=[VM, VM],
+        out_specs=[VM, VM, VM],
         out_shape=[
-            jax.ShapeDtypeStruct((E, 2 * SLOT, W), bf16),
+            jax.ShapeDtypeStruct((E, SLOT, W), bf16),
+            jax.ShapeDtypeStruct((SLOT, W), bf16),
             jax.ShapeDtypeStruct((E, 1, GW), f32),
         ],
-        scratch_shapes=[
-            pltpu.VMEM((2, H, W), bf16), pltpu.VMEM((2, H, W), bf16),
-            pltpu.VMEM((2, H, W), bf16), pltpu.VMEM((2, H, W), bf16),
-            pltpu.VMEM((2, ROWS, W), bf16), pltpu.VMEM((2, ROWS, W), bf16),
-            pltpu.VMEM((ROWS, W), bf16), pltpu.VMEM((ROWS, W), bf16),
-            pltpu.VMEM((ROWS, W), f32),
-            pltpu.VMEM((4, ROWS, W), bf16), pltpu.VMEM((4, ROWS, W), bf16),
-            pltpu.VMEM((H, W), bf16), pltpu.VMEM((H, W), bf16),
-            pltpu.VMEM((ROWS, W), bf16), pltpu.VMEM((ROWS, W), bf16),
-            pltpu.VMEM((ROWS, W), bf16), pltpu.VMEM((ROWS, W), bf16),
-            pltpu.VMEM((NDP, 1, GW), f32), pltpu.VMEM((1, GW), f32),
-            D((17,)), D((17,)), D((7,)), D((7,)), D((30,)), D((32,)), D((15,)), D((16,)),
+        scratch_shapes=Scatter.scratch(C_PIECE, C_HALF)
+        + Scatter.scratch(H_PIECE, H_HALF)
+        + [
+            V((1, ROWS, W), bf16),
+            V((NDP, NDP, SLOT, W), bf16), V((NDP, NDP, SLOT, W), bf16),
+            V((NDP, SLOT, W), bf16), V((NDP, SLOT, W), bf16),
+            V((NDP, 1, GW), f32), V((1, GW), f32),
+            D((7,)), D((7,)), D((15,)), D((16,)), D((15,)), D((16,)),
+            D((8,)), D((8,)), D((7,)), D((7,)),
         ],
         compiler_params=pltpu.CompilerParams(
             collective_id=2, has_side_effects=True, vmem_limit_bytes=60 * 1024 * 1024
@@ -749,18 +859,22 @@
     )(dxc, dxh, gp)
 
 
-def finish_kernel(ids_ref, logits_ref, back, gback, mr, rows_ref, gl_ref, norm_ref):
+def finish_kernel(ids_ref, logits_ref, back, backh, gback, mr, rows_ref, gl_ref, norm_ref):
     e, _, x, zh, c, _, _ = place()
     ids = ids_ref[...]
     onehot, rank = row_facts(ids, E)
     probs = soft(logits_ref[...])
     n = ids.shape[1]
-    slot = lax.broadcasted_iota(jnp.int32, (E * 2 * SLOT, n), 0)
-    pick = (slot == ids * (2 * SLOT) + rank).astype(f32).astype(bf16)
-    flat = back[...].reshape(E * 2 * SLOT, W)
-    rows_ref[...] = tn(pick, flat).astype(bf16)
-    rel = (((x - (ids >> 2)) & 3) * 2 + (zh ^ ((ids >> 1) & 1))) * 2 + c
-    lane = jnp.where(rank < SLOT, rel * SLOT + rank, ROWS + e * SLOT + rank - SLOT)
+    first = rank < SLOT
+    slot = lax.broadcasted_iota(jnp.int32, (ROWS, n), 0)
+    pick = (slot == jnp.where(first, ids * SLOT + rank, -1)).astype(f32).astype(bf16)
+    slot = lax.broadcasted_iota(jnp.int32, (SLOT, n), 0)
+    pickh = (slot == rank - SLOT).astype(f32).astype(bf16)
+    got = tn(pick, back[...].reshape(ROWS, W)) + tn(pickh, backh[...])
+    rows_ref[...] = got.astype(bf16)
+    rel = seen_from(ids, x, zh, c)
+    lane = jnp.where(first, rel * SLOT + rank, ROWS + e * SLOT + rank - SLOT)
+    slot = lax.broadcasted_iota(jnp.int32, (2 * ROWS, n), 0)
     here = (slot == lane).astype(f32).astype(bf16)
     found = jnp.dot(gback[:, 0, 0 : 2 * ROWS].astype(bf16), here, preferred_element_type=f32)
     dgate = jnp.sum(onehot * found, axis=0, keepdims=True)
@@ -773,11 +887,11 @@
     norm_ref[...] = jnp.sqrt(jnp.sum(gback[:, 0, 2 * ROWS : 2 * ROWS + 128], axis=0, keepdims=True))
 
 
-def finish(ids, logits, back, gback, mr):
+def finish(ids, logits, back, backh, gback, mr):
     n = ids.shape[1]
     return pl.pallas_call(
         finish_kernel,
-        in_specs=[VM] * 5,
+        in_specs=[VM] * 6,
         out_specs=[VM] * 3,
         out_shape=[
             jax.ShapeDtypeStruct((n, W), bf16),
@@ -785,25 +899,19 @@
             jax.ShapeDtypeStruct((1, 128), f32),
         ],
         name="finish",
-    )(ids, logits, back, gback, mr)
+    )(ids, logits, back, backh, gback, mr)
 
 
 def local(rows_x, rows_dy, router_logits, expert_of, w_gate, w_up, w_down):
-    e, _, x, zh, _, _, _ = place()
+    c = place()[4]
     ids = expert_of.reshape(1, -1)
     logits = router_logits.T
-    s, m = lay_out(ids, logits, rows_x, rows_dy)
-    cold, extra, mr = dispatch(s, m)
-    b = jnp.arange(E, dtype=jnp.int32)
-    rel = (((b >> 2) - x) & 3) * 4 + (((b >> 1) & 1) ^ zh) * 2 + (b & 1)
-    order = (rel[:, None] == jnp.arange(E, dtype=jnp.int32)[None, :]).astype(f32)
-    gates = jnp.stack(
-        [mr[:, 0, :SLOT].reshape(ROWS), jnp.dot(order, mr[:, 1, :SLOT]).reshape(ROWS)]
-    )
-    hot = (m[e, 2, e] > SLOT).astype(jnp.int32).reshape(1)
-    dxc, dxh, gp, gg, gu, gd = experts(hot, gates, cold, extra, w_gate[0], w_up[0], w_down[0])
-    back, gback = combine(dxc, dxh, gp)
-    grad_rows, grad_logits, norm = finish(ids, logits, back, gback, mr)
+    s1, s2, m = lay_out(ids, logits, rows_x, rows_dy)
+    cold, extra, mr = dispatch(s1, s2, m)
+    hot = mr[c, 3, 0].astype(jnp.int32).reshape(1)
+    dxc, dxh, gp, gg, gu, gd = experts(hot, mr, cold, extra, w_gate[0], w_up[0], w_down[0])
+    back, backh, gback = combine(dxc, dxh, gp)
+    grad_rows, grad_logits, norm = finish(ids, logits, back, backh, gback, mr)
     return grad_rows, grad_logits.T, gg[None], gu[None], gd[None], norm[0, 0]
 
 

time: 222 us -> 177 us (0.80)
  Pallas kernels: 216 us -> 174 us
    pallas_call x4, Pallas kernels: 193 us -> 151 us  [the longest x1 74.9 us: combine(): pl.pallas_call(combine_kernel, in_specs=[VM, VM, VM], out_specs=[VM, VM,...]
where the time goes in v2:
time: 177 us; the launch traced here: 176 us
  Pallas kernels  174 us (98%)
    pallas_call x1, Pallas kernels, combine(): pl.pallas_call(combine_kernel, in_specs=[VM, VM, VM], out_specs=[VM, VM,...  74.9 us
    pallas_call x1, Pallas kernels, dispatch(): pl.pallas_call(dispatch_kernel, in_specs=[ANY, ANY, ANY], out_specs=[ANY,...  69.3 us
    pallas_call x1, Pallas kernels, experts(): pl.pallas_call(experts_kernel, in_specs=[SM, VM, VM, ANY, VM, VM, VM], ou...  22.8 us
    pallas_call x1, Pallas kernels, lay_out(): pl.pallas_call(slots_kernel, in_specs=[VM] * 4, out_specs=[VM] * 3, out_s...  4.65 us

profile of v2, /device:TPU:1, one launch (start us, length us, event | category | flops | bytes accessed | tf_op | source)
XLA Modules:
  0.0 176.0 jit_solution(3373087401636248102)
XLA Ops:
  0.6 4.6 %lay_out.1 = (bf16[2,2,256,512]{3,2,1,0:T(8,128)(2,1)}, bf16[2,8,96,512]{3,2,1,0:T(8,128)(2,1)}, f32[16,8,128]{2,1,0:T(8,128)}) custom-call(s32[1,256]{1,0:T(1,128)} %bitcast.17, f32[16,256]{1,0:T(8,128)} %bitcast.15, bf16[256,4096]{1,0:T(8,128)(2,1)} %x_ref.1, bf16[256,4096]{1,0:T(8,128)(2,1)} %dy_ref.1), custom_call_target="tpu_custom_call" | custom-call | tf_op jit(solution)/shard_map/lay_out/pallas_call | solution.py:111
  5.3 69.3 %dispatch.1 = (bf16[2,8,512,512]{3,2,1,0:T(8,128)(2,1)}, bf16[2,8,512,512]{3,2,1,0:T(8,128)(2,1)}, f32[16,8,128]{2,1,0:T(8,128)}) custom-call(bf16[2,2,256,512]{3,2,1,0:T(8,128)(2,1)} %get-tuple-element.24.s1, bf16[2,8,96,512]{3,2,1,0:T(8,128)(2,1)} %get-tuple-element.25.s2, f32[16,8,128]{2,1,0:T(8,128)} %get-tuple-element.26.ms), custom_call_target="tpu_custom_call" | custom-call | tf_op jit(solution)/shard_map/dispatch/pallas_call | solution.py:406
  74.6 1.2 fusion
  75.8 22.8 %experts.1 = (bf16[8,512,512]{2,1,0:T(8,128)(2,1)}, bf16[8,512,512]{2,1,0:T(8,128)(2,1)}, f32[1,1280]{1,0:T(1,128)}, f32[192,4096]{1,0:T(8,128)}, f32[192,4096]{1,0:T(8,128)}, /*index=5*/f32[192,4096]{1,0:T(8,128)}) custom-call(s32[1]{0:T(128)} %bitcast.2.hot_ref, f32[16,8,128]{2,1,0:T(8,128)} %get-tuple-element.27.mr, ...), custom_call_target="tpu_custom_call" | custom-call | tf_op jit(solution)/shard_map/experts/pallas_call | solution.py:546
  98.6 74.9 %combine.1 = (bf16[16,32,512]{2,1,0:T(8,128)(2,1)}, bf16[32,512]{1,0:T(8,128)(2,1)}, f32[16,1,1280]{2,1,0:T(1,128)}) custom-call(bf16[8,512,512]{2,1,0:T(8,128)(2,1)} %get-tuple-element.30.dxc, bf16[8,512,512]{2,1,0:T(8,128)(2,1)} %get-tuple-element.31.dxh, f32[1,1280]{1,0:T(1,128)} %get-tuple-element.32.gp), custom_call_target="tpu_custom_call" | custom-call | tf_op jit(solution)/shard_map/combine/pallas_call | solution.py:836
  173.6 2.4 %finish.1 = (bf16[256,512]{1,0:T(8,128)(2,1)}, f32[16,256]{1,0:T(8,128)}, f32[1,128]{1,0:T(1,128)}) custom-call(s32[1,256]{1,0:T(1,128)} %bitcast.18, f32[16,256]{1,0:T(8,128)} %bitcast.16, bf16[16,32,512]{2,1,0:T(8,128)(2,1)} %get-tuple-element.33.back, bf16[32,512]{1,0:T(8,128)(2,1)} %get-tuple-element.34.backh, f32[16,1,1280]{2,1,0:T(1,128)} %get-tuple-element.35.gback, ...), custom_call_target="tpu_custom_call" | custom-call | tf_op jit(solution)/shard_map/finish/pallas_call | solution.py:892

commit v3 on v2

v3 whole, which is shorter than its diff:
```python
import jax
import jax.numpy as jnp
from jax import lax
from jax.experimental import pallas as pl
from jax.experimental.pallas import tpu as pltpu
from jax.sharding import PartitionSpec as P

f32 = jnp.float32
bf16 = jnp.bfloat16
MESH = pl.DeviceIdType.MESH
ANY = pl.BlockSpec(memory_space=pl.ANY)
VM = pl.BlockSpec(memory_space=pltpu.VMEM)
SM = pl.BlockSpec(memory_space=pltpu.SMEM)

E = 16
NDP = 8
SLOT = 32
W = 512
ROWS = E * SLOT
LOCAL = 2 * SLOT
GW = 1280


def place():
    e = lax.axis_index("expert")
    d = lax.axis_index("dp")
    return e, d, e // 4, (e // 2) % 2, e % 2, d // 2, d % 2


def expert_at(x, zh, c):
    return (x * 2 + zh) * 2 + c


def to(e, d):
    return {"expert": e, "dp": d}


def row_facts(ids, experts):
    rows = ids.shape[1]
    onehot = (lax.broadcasted_iota(jnp.int32, (experts, rows), 0) == ids).astype(f32)
    before = lax.broadcasted_iota(jnp.int32, (rows, rows), 0) < lax.broadcasted_iota(
        jnp.int32, (rows, rows), 1
    )
    earlier = jnp.dot(onehot.astype(bf16), before.astype(bf16), preferred_element_type=f32)
    rank = jnp.sum(onehot * earlier, axis=0, keepdims=True).astype(jnp.int32)
    return onehot, rank


def soft(logits):
    top = jnp.max(logits, axis=0, keepdims=True)
    ex = jnp.exp(logits - top)
    return ex / jnp.sum(ex, axis=0, keepdims=True)


def nt(a, b):
    return lax.dot_general(a, b, (((1,), (1,)), ((), ())), preferred_element_type=f32)


def tn(a, b):
    return lax.dot_general(a, b, (((0,), (0,)), ((), ())), preferred_element_type=f32)


def seen_from(ids, x, zh, c):
    return (((x - (ids >> 2)) & 3) * 2 + (zh ^ ((ids >> 1) & 1))) * 2 + c


def slots_kernel(ids_ref, logits_ref, x_ref, dy_ref, s1_ref, s2_ref, m_ref):
    e, d, x, zh, c, y, zl = place()
    ids = ids_ref[...]
    onehot, rank = row_facts(ids, E)
    rows = ids.shape[1]
    none = -1

    def perm(slots, target):
        slot = lax.broadcasted_iota(jnp.int32, (slots, rows), 0)
        return (slot == target).astype(f32).astype(bf16)

    far = (zh ^ ((ids >> 1) & 1)) == 1
    first = rank < SLOT
    chip = ((ids >> 2) * 2 + (ids & 1)) * SLOT + rank
    for g, ours in ((0, jnp.logical_not(far)), (1, far)):
        p = perm(ROWS // 2, jnp.where(first & ours, chip, none))
        at = pl.ds(pl.multiple_of((d if g == 0 else y * 2 + 1 - zl) * W, W), W)
        s1_ref[0, g] = jnp.dot(p, x_ref[:, at], preferred_element_type=f32).astype(bf16)
        s1_ref[1, g] = jnp.dot(p, dy_ref[:, at], preferred_element_type=f32).astype(bf16)
    home = jnp.where(ids == e, rank, jnp.where(ids == e + 1 - 2 * c, SLOT + rank, none))
    p = perm(3 * SLOT, jnp.where(first, home, SLOT + rank))
    for j in range(NDP):
        at = slice(j * W, (j + 1) * W)
        s2_ref[0, j] = jnp.dot(p, x_ref[:, at], preferred_element_type=f32).astype(bf16)
        s2_ref[1, j] = jnp.dot(p, dy_ref[:, at], preferred_element_type=f32).astype(bf16)

    gate = jnp.sum(soft(logits_ref[...]) * onehot, axis=0, keepdims=True).astype(bf16).astype(f32)
    lane = lax.broadcasted_iota(jnp.int32, (128, rows), 0)
    spot = (seen_from(ids, x, zh, c) & 3) * SLOT + rank
    cold = (onehot * gate * first.astype(f32)).astype(bf16)
    cold = nt(cold, (lane == spot).astype(f32).astype(bf16))
    gate8 = jnp.broadcast_to(gate, (8, rows)).astype(bf16)
    spot = jnp.where(first, none, (e & 3) * SLOT + rank - SLOT)
    hot = nt(gate8, (lane == spot).astype(f32).astype(bf16))
    count = nt(jnp.ones((8, rows), bf16), (lane == ids).astype(f32).astype(bf16))
    line = lax.broadcasted_iota(jnp.int32, (8, 128), 0)
    for k in range(E):
        mine = jnp.broadcast_to(cold[k : k + 1, :], (8, 128))
        busy = (jnp.sum(onehot[k : k + 1, :], axis=1, keepdims=True) > SLOT).astype(f32)
        rest = jnp.where(line == 2, count, jnp.broadcast_to(busy, (8, 128)))
        m_ref[k] = jnp.where(line == 0, mine, jnp.where(line == 1, hot, rest))


def lay_out(ids, logits, x, dy):
    return pl.pallas_call(
        slots_kernel,
        in_specs=[VM] * 4,
        out_specs=[VM] * 3,
        out_shape=[
            jax.ShapeDtypeStruct((2, 2, ROWS // 2, W), bf16),
            jax.ShapeDtypeStruct((2, NDP, 3 * SLOT, W), bf16),
            jax.ShapeDtypeStruct((E, 8, 128), f32),
        ],
        name="lay_out",
    )(ids, logits, x, dy)


class Gather:
    names = (
        "0oz", "0or", "0ol", "0lr", "0lz", "0rl", "0rz", "0dz", "0ez",
        "1oz", "1or", "1ol", "1zr", "1zl", "1lr", "1kr", "1rl", "1ql",
    )

    def __init__(self, own, piece, j, z, right, left, pair, ssem, rsem):
        self.own, self.piece, self.ssem, self.rsem = own, piece, ssem, rsem
        self.j, self.z = j, z
        self.jl, self.jr, self.jd = (j + 3) % 4, (j + 1) % 4, (j + 2) % 4
        self.right, self.left, self.pair = right, left, pair
        self.sent = []

    def send(self, name, src, dst, dev):
        i = self.names.index(name)
        copy = pltpu.make_async_remote_copy(
            src, dst, self.ssem.at[i], self.rsem.at[i], device_id=dev, device_id_type=MESH
        )
        copy.start()
        self.sent.append(copy)

    def pass_on(self, name, dev, *where):
        ref = self.piece(*where)
        self.send(name, ref, ref, dev)

    def got(self, name, *where):
        i = self.names.index(name)
        ref = self.piece(*where)
        pltpu.make_async_remote_copy(
            ref, ref, self.ssem.at[i], self.rsem.at[i], device_id=self.pair, device_id_type=MESH
        ).wait_recv()

    def start(self, a):
        for way, dev in (("z", self.pair), ("r", self.right), ("l", self.left)):
            self.send(f"{a}o{way}", self.own(a), self.piece(a, self.j, self.z, None), dev)

    def s2(self):
        self.got("0or", 0, self.jl, self.z, None)
        self.pass_on("0lr", self.right, 0, self.jl, self.z, 0)
        self.pass_on("0lz", self.pair, 0, self.jl, self.z, None)

    def s3(self):
        self.got("0ol", 0, self.jr, self.z, None)
        self.pass_on("0rl", self.left, 0, self.jr, self.z, 1)
        self.pass_on("0rz", self.pair, 0, self.jr, self.z, None)

    def s4(self):
        self.got("1oz", 1, self.j, 1 - self.z, None)
        self.pass_on("1zr", self.right, 1, self.j, 1 - self.z, None)
        self.pass_on("1zl", self.left, 1, self.j, 1 - self.z, None)

    def s5(self):
        self.got("1or", 1, self.jl, self.z, None)
        self.pass_on("1lr", self.right, 1, self.jl, self.z, 0)

    def s6(self):
        self.got("1ol", 1, self.jr, self.z, None)
        self.pass_on("1rl", self.left, 1, self.jr, self.z, 1)

    def s7(self):
        self.got("0lr", 0, self.jd, self.z, 0)
        self.pass_on("0dz", self.pair, 0, self.jd, self.z, 0)

    def s8(self):
        self.got("0rl", 0, self.jd, self.z, 1)
        self.pass_on("0ez", self.pair, 0, self.jd, self.z, 1)

    def s9(self):
        self.got("1zr", 1, self.jl, 1 - self.z, None)
        self.pass_on("1kr", self.right, 1, self.jl, 1 - self.z, 0)

    def s10(self):
        self.got("1zl", 1, self.jr, 1 - self.z, None)
        self.pass_on("1ql", self.left, 1, self.jr, 1 - self.z, 1)

    def end_of_1_d(self):
        self.got("1lr", 1, self.jd, self.z, 0)
        self.got("1rl", 1, self.jd, self.z, 1)

    def end_of_1_e(self):
        self.got("1kr", 1, self.jd, 1 - self.z, 0)
        self.got("1ql", 1, self.jd, 1 - self.z, 1)

    def end_of_0_d(self):
        self.got("0dz", 0, self.jd, 1 - self.z, 0)
        self.got("0ez", 0, self.jd, 1 - self.z, 1)

    def drain(self):
        for copy in self.sent:
            copy.wait_send()


def meet(partners):
    barrier = pltpu.get_barrier_semaphore()
    for dev in partners:
        pl.semaphore_signal(barrier, inc=1, device_id=dev, device_id_type=MESH)
    pl.semaphore_wait(barrier, len(partners))


def others(x, zh):
    for k in range(1, 8):
        dx, dz = k // 2, k % 2
        yield k, ((4 - dx) % 4) * 2 + dz, (x + dx) % 4, (zh + dz) % 2


def sigmoid(v):
    return 1.0 / (1.0 + jnp.exp(-v))


def gate_row(mr, t):
    _, _, x, _, c, _, _ = place()
    parts = []
    for g in range(E // 4):
        at = g * 4 if t == 0 else ((g - x) & 3) * 4
        part = mr[at, t : t + 1, :]
        for i in range(1, 4):
            part = part + mr[at + i, t : t + 1, :]
        parts.append(part if t == 0 else part * mr[c, 3:4, :])
    return jnp.concatenate(parts, axis=1)


def add_into(out, *terms):
    n, rows, _ = out.shape
    step_rows = min(rows, 64)
    for i in range(n):

        def step(k, _):
            r = pl.ds(pl.multiple_of(k * step_rows, step_rows), step_rows)
            total = terms[0][i, r, :].astype(f32)
            for term in terms[1:]:
                total = total + term[i, r, :].astype(f32)
            out[i, r, :] = total.astype(out.dtype)
            return 0

        if rows == step_rows:
            step(0, 0)
        else:
            lax.fori_loop(0, rows // step_rows, step, 0)


class Scatter:
    names = (
        "ar0", "ar1", "al0", "al1", "br0", "br1", "bl0", "bl1", "cr0", "cr1", "cl0", "cl1", "p",
        "zd", "zr", "zl", "z0", "hr", "hl", "ir", "il", "kr", "kl",
    )

    @staticmethod
    def scratch(piece, half):
        V = pltpu.VMEM
        return [
            V((2,) + half, bf16), V((2,) + half, bf16), V((2,) + half, bf16), V((2,) + half, bf16),
            V((2,) + piece, bf16), V((2,) + piece, bf16),
            V(piece, bf16), V(piece, bf16), V(piece, f32),
            V((4,) + piece, bf16), V((4,) + piece, bf16),
            V(half, bf16), V(half, bf16), V(piece, bf16), V(piece, bf16),
            pltpu.SemaphoreType.DMA((23,)), pltpu.SemaphoreType.DMA((23,)),
        ]

    def __init__(self, chunk, cut, j, z, right, left, pair, refs):
        self.chunk, self.cut, self.j, self.z = chunk, cut, j, z
        self.jl, self.jr, self.jd = (j + 3) % 4, (j + 1) % 4, (j + 2) % 4
        self.right, self.left, self.pair = right, left, pair
        (
            self.rl, self.rr, self.tr, self.tl, self.fl, self.fr, self.zs, self.zin, self.own,
            self.hz, self.hw, self.hrl, self.hrr, self.hfl, self.hfr, self.ssem, self.rsem,
        ) = refs
        self.sent = []

    def send(self, name, src, dst, dev):
        i = self.names.index(name)
        copy = pltpu.make_async_remote_copy(
            src, dst, self.ssem.at[i], self.rsem.at[i], device_id=dev, device_id_type=MESH
        )
        copy.start()
        self.sent.append(copy)

    def got(self, name, ref):
        i = self.names.index(name)
        pltpu.make_async_remote_copy(
            ref, ref, self.ssem.at[i], self.rsem.at[i], device_id=self.pair, device_id_type=MESH
        ).wait_recv()

    def start0_far(self):
        for k in (0, 1):
            far = self.chunk(0, self.jd, k)
            self.send(f"ar{k}", self.cut(far, 0), self.rl.at[k], self.right)
            self.send(f"al{k}", self.cut(far, 1), self.rr.at[k], self.left)

    def start0_right(self):
        for k in (0, 1):
            right = self.chunk(0, self.jr, k)
            self.send(f"br{k}", self.cut(right, 1), self.cut(self.fl.at[k], 1), self.right)

    def start0_left(self):
        for k in (0, 1):
            left = self.chunk(0, self.jl, k)
            self.send(f"bl{k}", self.cut(left, 0), self.cut(self.fr.at[k], 0), self.left)

    def start1(self, way):
        j = {"d": self.jd, "r": self.jr, "l": self.jl, "0": self.j}[way]
        self.send("z" + way, self.chunk(1, j, 1 - self.z), self.hz.at[j], self.pair)

    def relay0(self):
        for k in (0, 1):
            self.got(f"ar{k}", self.rl.at[k])
            add_into(self.tr.at[k], self.cut(self.chunk(0, self.jr, k), 0), self.rl.at[k])
            self.send(f"cr{k}", self.tr.at[k], self.cut(self.fl.at[k], 0), self.right)
            self.got(f"al{k}", self.rr.at[k])
            add_into(self.tl.at[k], self.cut(self.chunk(0, self.jl, k), 1), self.rr.at[k])
            self.send(f"cl{k}", self.tl.at[k], self.cut(self.fr.at[k], 1), self.left)

    def pair0(self):
        for k in (0, 1):
            for n, ref, h in (("br", self.fl, 1), ("bl", self.fr, 0), ("cr", self.fl, 0), ("cl", self.fr, 1)):
                self.got(f"{n}{k}", self.cut(ref.at[k], h))
        k = 1 - self.z
        add_into(self.zs, self.chunk(0, self.j, k), self.fl.at[k], self.fr.at[k])
        self.send("p", self.zs, self.zin, self.pair)
        k = self.z
        add_into(self.own, self.chunk(0, self.j, k), self.fl.at[k], self.fr.at[k])

    def end0(self, out):
        self.got("p", self.zin)
        add_into(out, self.own, self.zin)

    def relay1_far(self):
        self.got("zd", self.hz.at[self.jd])
        w = self.hw.at[self.jd]
        add_into(w, self.chunk(1, self.jd, self.z), self.hz.at[self.jd])
        self.send("hr", self.cut(w, 0), self.hrl, self.right)
        self.send("hl", self.cut(w, 1), self.hrr, self.left)

    def relay1_near(self):
        for way, j, h, ref, dev in (
            ("r", self.jr, 1, self.hfl, self.right), ("l", self.jl, 0, self.hfr, self.left)
        ):
            self.got("z" + way, self.hz.at[j])
            w = self.cut(self.hw.at[j], h)
            add_into(w, self.cut(self.chunk(1, j, self.z), h), self.cut(self.hz.at[j], h))
            self.send("i" + way, w, self.cut(ref, h), dev)

    def relay1_last(self):
        for way, j, h, inp, ref, dev in (
            ("r", self.jr, 0, self.hrl, self.hfl, self.right),
            ("l", self.jl, 1, self.hrr, self.hfr, self.left),
        ):
            self.got("h" + way, inp)
            w = self.cut(self.hw.at[j], h)
            add_into(w, self.cut(self.chunk(1, j, self.z), h), self.cut(self.hz.at[j], h), inp)
            self.send("k" + way, w, self.cut(ref, h), dev)

    def end1(self, out):
        self.got("z0", self.hz.at[self.j])
        self.got("ir", self.cut(self.hfl, 1))
        self.got("il", self.cut(self.hfr, 0))
        self.got("kr", self.cut(self.hfl, 0))
        self.got("kl", self.cut(self.hfr, 1))
        add_into(out, self.chunk(1, self.j, self.z), self.hz.at[self.j], self.hfl, self.hfr)

    def drain(self):
        for copy in self.sent:
            copy.wait_send()


HR = ROWS // 2
C_PIECE, C_HALF = (1, HR, W), (1, HR // 2, W)
H_PIECE, H_HALF = (NDP // 2, SLOT, W), (NDP // 4, SLOT, W)


def moe_kernel(
    s1, s2, ms, wg_hbm, wu_hbm, wd_hbm,
    back, backh, gback, mr, gg, gu, gd,
    *refs,
):
    e, d, x, zh, c, y, zl = place()
    c_refs, refs = refs[:17], refs[17:]
    h_refs, refs = refs[:17], refs[17:]
    (
        cold, extra, weights, acc, lhs, rhs, stage, dxc, dxh, gp,
        rc, hs, hin, outh, hp, gall, gsum,
        st_s, st_r, m_s, m_r, sib_s, sib_r, dp_s, dp_r, ex_s, ex_r, xs_s, xs_r, loc, osem,
        g_s, g_r, b_s, b_r, gb_s, gb_r, x_s, x_r, q_s, q_r,
    ) = refs
    wg, wu, wd = weights.at[0], weights.at[1], weights.at[2]
    FFL = weights.shape[1]
    dbar = y * 2 + 1 - zl
    sib = to(expert_at(x, zh, 1 - c), d)
    right, left, pair = to(e, ((y + 1) % 4) * 2 + zl), to(e, ((y + 3) % 4) * 2 + zl), to(e, dbar)
    x_r_dev, x_l_dev = to(expert_at((x + 1) % 4, zh, c), d), to(expert_at((x + 3) % 4, zh, c), d)
    z_p = to(expert_at(x, 1 - zh, c), dbar)
    peers, places, mine = [expert_at(x, zh, 1 - c)], [1 - c], [c]
    row_peers = []
    for rel, seen, x2, zh2 in others(x, zh):
        for c2 in (0, 1):
            peers.append(expert_at(x2, zh2, c2))
            places.append(rel * 2 + c2)
            mine.append(seen * 2 + c)
            d2 = d if rel % 2 == 0 else dbar
            row_peers.append((rel, seen, expert_at(x2, zh2, c2), d2, x2 * 2 + c2))
    dps = [(d + k) % NDP for k in range(1, NDP)]

    own_in = [
        pltpu.make_async_copy(s2.at[:, :, 0:SLOT, :], cold.at[:, :, pl.ds(pl.multiple_of(c * SLOT, SLOT), SLOT), :], loc.at[0]),
        pltpu.make_async_copy(s2.at[:, :, 2 * SLOT :, :], extra.at[:, :, pl.ds(pl.multiple_of(e * SLOT, SLOT), SLOT), :], loc.at[1]),
        pltpu.make_async_copy(ms.at[e], mr.at[c], loc.at[2]),
        pltpu.make_async_copy(wg_hbm, wg, loc.at[3]),
        pltpu.make_async_copy(wu_hbm, wu, loc.at[4]),
        pltpu.make_async_copy(wd_hbm, wd, loc.at[5]),
    ]
    for copy in own_in:
        copy.start()
    meet(
        [to(e2, d) for e2 in peers] + [to(e, d2) for d2 in dps]
        + [to(p[2], dbar) for p in row_peers if p[0] % 2]
    )

    rest = []

    def send(src, dst, ssem, rsem, dev):
        copy = pltpu.make_async_remote_copy(
            src, dst, ssem, rsem, device_id=dev, device_id_type=MESH
        )
        copy.start()
        rest.append(copy)

    def wait(ref, ssem, rsem):
        pltpu.make_async_remote_copy(
            ref, ref, ssem, rsem, device_id=sib, device_id_type=MESH
        ).wait_recv()

    def slots_at(n):
        return pl.ds(pl.multiple_of(n * SLOT, SLOT), SLOT)

    for a in (0, 1):
        for rel, seen, e2, d2, q in row_peers:
            pltpu.make_async_remote_copy(
                s1.at[a, rel % 2, slots_at(q), :], cold.at[a, d2, slots_at(seen * 2 + c), :],
                st_s.at[a], st_r.at[a], device_id=to(e2, d2), device_id_type=MESH,
            ).start()
    meta_peers = row_peers + [(0, 0, expert_at(x, zh, 1 - c), d, 0)]
    for n, (_, seen, e2, d2, _) in enumerate(meta_peers):
        send(ms.at[e2], mr.at[seen * 2 + c], m_s.at[n], m_r.at[seen * 2 + c], to(e2, d2))
    send(s2.at[:, :, SLOT : 2 * SLOT, :], cold.at[:, :, slots_at(c), :], sib_s, sib_r, sib)

    half = (ROWS - LOCAL) // 2

    def dp_piece(a, j, z, h):
        rows = {None: (LOCAL, 2 * half), 0: (LOCAL, half), 1: (LOCAL + half, half)}[h]
        return cold.at[a, j * 2 + z, pl.ds(*rows), :]

    def ex_piece_of(core):
        def piece(a, j, z, h):
            chunks = {None: (0, NDP), 0: (0, NDP // 2), 1: (NDP // 2, NDP // 2)}[h]
            return extra.at[a, pl.ds(*chunks), slots_at(expert_at(j, z, core)), :]
        return piece

    ex_piece, ex_other = ex_piece_of(c), ex_piece_of(1 - c)
    dp = Gather(
        lambda a: dp_piece(a, y, zl, None), dp_piece, y, zl, right, left, pair, dp_s, dp_r
    )
    ex = Gather(
        lambda a: s2.at[a, :, 2 * SLOT :, :], ex_piece, x, zh, x_r_dev, x_l_dev, z_p, ex_s, ex_r
    )
    C = Scatter(
        lambda a, j, z: dxc.at[pl.ds(j * 2 + z, 1), pl.ds(a * HR, HR)],
        lambda ref, h: ref.at[:, pl.ds(h * (HR // 2), HR // 2)],
        y, zl, right, left, pair, c_refs,
    )
    X = Scatter(
        lambda a, j, z: hs.at[j * 2 + z, pl.ds(a * (NDP // 2), NDP // 2)],
        lambda ref, h: ref.at[pl.ds(h * (NDP // 4), NDP // 4)],
        x, zh, x_r_dev, x_l_dev, z_p, h_refs,
    )
    shares = []

    def share(a, j, z, src=None):
        i = len(shares)
        dst = ex_piece(a, j, z, None)
        send(dst if src is None else src, dst, xs_s.at[i], xs_r.at[i], sib)
        shares.append((a, j, z))

    def whole(a):
        ref = cold.at[a, d, pl.ds(LOCAL, ROWS - LOCAL), :]
        return pltpu.make_async_remote_copy(
            ref, ref, st_s.at[a], st_r.at[a], device_id=sib, device_id_type=MESH
        )

    def cols(j):
        return pl.ds(pl.multiple_of(j * W, W), W)

    def forward_x(rows, t, at, n):
        def step(i, _):
            j = at(i)
            xj = rows[0, j]
            acc[t, 0] += nt(wg[:, cols(j)], xj)
            acc[t, 1] += nt(wu[:, cols(j)], xj)
            return 0

        lax.fori_loop(0, n, step, 0)

    def forward_dy(rows, t, at, n):
        def step(i, _):
            j = at(i)
            acc[t, 2] += nt(wd[:, cols(j)], rows[1, j])
            return 0

        lax.fori_loop(0, n, step, 0)

    def between(t):
        gate = gate_row(mr, t)
        pre, up, g = acc[t, 0], acc[t, 1], acc[t, 2]
        s = sigmoid(pre)
        active = pre * s
        hidden = (active * up).astype(bf16).astype(f32)
        gp[0:1, t * ROWS : (t + 1) * ROWS] = jnp.sum(hidden * g, axis=0, keepdims=True)
        gh = g * gate
        d_up = gh * active
        d_pre = gh * up * s * (1.0 + pre * (1.0 - s))
        lhs[t, 0] = d_pre.astype(bf16)
        lhs[t, 1] = d_up.astype(bf16)
        lhs[t, 2] = (hidden * gate).astype(bf16)
        rhs[t, :, 0:FFL] = d_pre.T.astype(bf16)
        rhs[t, :, FFL : 2 * FFL] = d_up.T.astype(bf16)

    def rows_back(t, out, at, n):
        def step(i, _):
            j = at(i)
            r = jnp.dot(rhs[t, :, 0:FFL], wg[:, cols(j)], preferred_element_type=f32)
            r += jnp.dot(rhs[t, :, FFL : 2 * FFL], wu[:, cols(j)], preferred_element_type=f32)
            out[j] = r.astype(bf16)
            return 0

        lax.fori_loop(0, n, step, 0)

    outs = (gg, gu, gd)

    def put(j, slot, i):
        return pltpu.make_async_copy(
            stage.at[slot, i], outs[i].at[:, cols(j)], osem.at[slot, i]
        )

    def weights_back(first, sq, fresh):
        def step(j, sq):
            slot = j % 2
            if not fresh:
                for i in range(3):
                    put(j - 2, slot, i).wait()
            for i in range(3):
                v = jnp.dot(lhs[0, i], cold[i // 2, j], preferred_element_type=f32)
                v += jnp.dot(lhs[1, i], extra[i // 2, j], preferred_element_type=f32)
                stage[slot, i] = v
                sq = sq + jnp.sum((v * v).reshape(-1, 8, W), axis=0)
                put(j, slot, i).start()
            return sq

        return lax.fori_loop(first, first + 2, step, sq)

    acc[...] = jnp.zeros_like(acc)
    for copy in own_in[2:]:
        copy.wait()
    own_in[0].wait()
    wait(cold.at[:, :, slots_at(1 - c), :], sib_s, sib_r)
    whole(0).wait_recv()
    dp.start(0)
    ex.start(0)
    forward_x(cold, 0, lambda i: d, 1)
    whole(1).wait_recv()
    dp.start(1)
    ex.start(1)
    own_in[1].wait()
    share(0, x, zh, s2.at[0, :, 2 * SLOT :, :])
    share(1, x, zh, s2.at[1, :, 2 * SLOT :, :])
    forward_dy(cold, 0, lambda i: d, 1)
    ex.s2()
    ex.s3()
    dp.s2()
    dp.s3()
    ex.s4()
    ex.s5()
    ex.s6()
    for a, j, z in ((0, ex.jl, zh), (0, ex.jr, zh), (1, x, 1 - zh), (1, ex.jl, zh), (1, ex.jr, zh)):
        share(a, j, z)
    forward_x(cold, 0, lambda i: ((y + 1 + 2 * i) % 4) * 2 + zl, 2)
    ex.s7()
    ex.s8()
    share(0, ex.jd, zh)
    dp.s4()
    dp.s5()
    dp.s6()
    forward_dy(cold, 0, lambda i: ((y + 1 + 2 * i) % 4) * 2 + zl, 2)
    forward_dy(cold, 0, lambda i: dbar, 1)
    ex.s9()
    ex.s10()
    share(1, ex.jl, 1 - zh)
    share(1, ex.jr, 1 - zh)
    dp.s7()
    dp.s8()
    dp.got("0oz", 0, y, 1 - zl, None)
    forward_x(cold, 0, lambda i: i * (dp.jd * 2 + zl) + (1 - i) * dbar, 2)
    ex.got("0oz", 0, x, 1 - zh, None)
    share(0, x, 1 - zh)
    ex.got("0lz", 0, ex.jl, 1 - zh, None)
    share(0, ex.jl, 1 - zh)
    ex.got("0rz", 0, ex.jr, 1 - zh, None)
    share(0, ex.jr, 1 - zh)
    ex.end_of_1_d()
    share(1, ex.jd, zh)
    ex.end_of_1_e()
    share(1, ex.jd, 1 - zh)
    ex.end_of_0_d()
    share(0, ex.jd, 1 - zh)
    dp.s9()
    dp.s10()
    forward_dy(cold, 0, lambda i: ((y + 1 + 2 * i) % 4) * 2 + 1 - zl, 2)
    for i in [1 - c] + list(range(2, E)):
        wait(mr.at[i], m_s.at[0], m_r.at[i])
    for i, where in enumerate(shares):
        wait(ex_other(*where, None), xs_s.at[i], xs_r.at[i])
    forward_x(extra, 1, lambda i: i, NDP)
    forward_dy(extra, 1, lambda i: i, NDP)
    between(1)
    rows_back(1, dxh, lambda i: i, NDP)
    far = [X.jd * 2, X.jd * 2 + 1, X.jr * 2, X.jl * 2, X.jr * 2 + 1, X.jl * 2 + 1, x * 2, x * 2 + 1]

    def h_rows(chip, core):
        return slots_at(chip * 2 + core)

    for i, chip in enumerate(far):
        send(dxh.at[:, h_rows(chip, 1 - c)], hin.at[chip], x_s.at[i], x_r.at[i], sib)
    dp.end_of_1_d()
    forward_dy(cold, 0, lambda i: dp.jd * 2 + zl, 1)
    for i, chip in enumerate(far):
        wait(hin.at[chip], x_s.at[i], x_r.at[i])
        add_into(hs.at[chip], dxh.at[:, h_rows(chip, c)], hin.at[chip])
        if i == 1:
            X.start0_far()
        if i == 5:
            X.start0_right()
            X.start0_left()
    for way in ("d", "r", "l", "0"):
        X.start1(way)
    dp.got("0lz", 0, dp.jl, 1 - zl, None)
    dp.got("0rz", 0, dp.jr, 1 - zl, None)
    forward_x(cold, 0, lambda i: ((y + 1 + 2 * i) % 4) * 2 + 1 - zl, 2)
    dp.end_of_1_e()
    forward_dy(cold, 0, lambda i: dp.jd * 2 + 1 - zl, 1)
    dp.end_of_0_d()
    forward_x(cold, 0, lambda i: dp.jd * 2 + 1 - zl, 1)
    between(0)

    rows_back(0, dxc, lambda i: C.jd * 2 + i, 2)
    C.start0_far()
    C.start1("d")
    rows_back(0, dxc, lambda i: C.jr * 2 + i, 2)
    C.start0_right()
    C.start1("r")
    rows_back(0, dxc, lambda i: C.jl * 2 + i, 2)
    C.start0_left()
    C.start1("l")
    rows_back(0, dxc, lambda i: y * 2 + i, 2)
    C.start1("0")
    X.relay0()
    X.relay1_far()
    X.relay1_near()
    sq = weights_back(0, jnp.zeros((8, W), f32), True)
    C.relay0()
    C.relay1_far()
    X.relay1_last()
    X.pair0()
    sq = weights_back(2, sq, False)
    C.relay1_near()
    sq = weights_back(4, sq, False)
    C.relay1_last()
    sq = weights_back(6, sq, False)
    total = jnp.sum(jnp.sum(sq, axis=0, keepdims=True), axis=1, keepdims=True)
    gp[0:1, 2 * ROWS :] = jnp.broadcast_to(total, (1, GW - 2 * ROWS))
    for k, d2 in enumerate(dps):
        send(gp, gall.at[d], g_s.at[k], g_r.at[k], to(e, d2))
    gall[d] = gp[...]
    C.pair0()
    X.end1(outh.at[pl.ds(NDP // 2, NDP // 2)])
    X.end0(outh.at[pl.ds(0, NDP // 2)])
    for k, d2 in enumerate(dps):
        send(outh.at[d2], hp.at[d], q_s.at[k], q_r.at[k], to(e, d2))
    hp[d] = outh[d]

    def give(a):
        for n, e2 in enumerate(peers):
            if (n >= 7) == (a == 1):
                send(
                    rc.at[0, slots_at(places[n]), :],
                    back.at[e], b_s.at[n], b_r.at[mine[n]], to(e2, d),
                )

    C.end1(rc.at[:, pl.ds(HR, HR)])
    give(1)
    for k in range(NDP - 1):
        wait(gall.at[(d + NDP - 1 - k) % NDP], g_s.at[k], g_r.at[k])
    total = gall[0]
    for k in range(1, NDP):
        total = total + gall[k]
    gsum[...] = total
    gback[e] = total
    for n, e2 in enumerate(peers):
        send(gsum, gback.at[e], gb_s.at[n], gb_r.at[mine[n]], to(e2, d))
    C.end0(rc.at[:, pl.ds(0, HR)])
    give(0)
    back[e] = rc[0, slots_at(c), :]
    for k in range(NDP - 1):
        wait(hp.at[(d + NDP - 1 - k) % NDP], q_s.at[k], q_r.at[k])
    total = hp[0].astype(f32)
    for k in range(1, NDP):
        total = total + hp[k].astype(f32)
    backh[...] = total.astype(bf16)

    for i in [1 - c] + list(range(2, E)):
        wait(back.at[0], b_s.at[0], b_r.at[i])
        wait(gback.at[0], gb_s.at[0], gb_r.at[i])
    for j in (NDP - 2, NDP - 1):
        for i in range(3):
            put(j, j % 2, i).wait()
    whole(0).wait_send()
    whole(1).wait_send()
    for copy in rest:
        copy.wait_send()
    dp.drain()
    ex.drain()
    C.drain()
    X.drain()


def moe(s1, s2, m, wg, wu, wd):
    FFL, width = wg.shape
    D = pltpu.SemaphoreType.DMA
    V = pltpu.VMEM
    return pl.pallas_call(
        moe_kernel,
        in_specs=[ANY] * 6,
        out_specs=[VM] * 4 + [ANY] * 3,
        out_shape=[
            jax.ShapeDtypeStruct((E, SLOT, W), bf16),
            jax.ShapeDtypeStruct((SLOT, W), bf16),
            jax.ShapeDtypeStruct((E, 1, GW), f32),
            jax.ShapeDtypeStruct((E, 8, 128), f32),
        ]
        + [jax.ShapeDtypeStruct((FFL, width), f32)] * 3,
        scratch_shapes=Scatter.scratch(C_PIECE, C_HALF)
        + Scatter.scratch(H_PIECE, H_HALF)
        + [
            V((2, NDP, ROWS, W), bf16), V((2, NDP, ROWS, W), bf16),
            V((3, FFL, width), bf16),
            V((2, 3, FFL, ROWS), f32), V((2, 3, FFL, ROWS), bf16), V((2, ROWS, 2 * FFL), bf16),
            V((2, 3, FFL, W), f32),
            V((NDP, ROWS, W), bf16), V((NDP, ROWS, W), bf16), V((1, GW), f32),
            V((1, ROWS, W), bf16),
            V((NDP, NDP, SLOT, W), bf16), V((NDP, NDP, SLOT, W), bf16),
            V((NDP, SLOT, W), bf16), V((NDP, SLOT, W), bf16),
            V((NDP, 1, GW), f32), V((1, GW), f32),
            D((2,)), D((2,)), D((15,)), D((16,)), D, D,
            D((18,)), D((18,)), D((18,)), D((18,)), D((16,)), D((16,)), D((6,)), D((2, 3)),
            D((7,)), D((7,)), D((15,)), D((16,)), D((15,)), D((16,)),
            D((8,)), D((8,)), D((7,)), D((7,)),
        ],
        compiler_params=pltpu.CompilerParams(
            collective_id=1, has_side_effects=True, vmem_limit_bytes=62 * 1024 * 1024
        ),
        name="moe",
    )(s1, s2, m, wg, wu, wd)


def finish_kernel(ids_ref, logits_ref, back, backh, gback, mr, rows_ref, gl_ref, norm_ref):
    e, _, x, zh, c, _, _ = place()
    ids = ids_ref[...]
    onehot, rank = row_facts(ids, E)
    probs = soft(logits_ref[...])
    n = ids.shape[1]
    first = rank < SLOT
    slot = lax.broadcasted_iota(jnp.int32, (ROWS, n), 0)
    pick = (slot == jnp.where(first, ids * SLOT + rank, -1)).astype(f32).astype(bf16)
    slot = lax.broadcasted_iota(jnp.int32, (SLOT, n), 0)
    pickh = (slot == rank - SLOT).astype(f32).astype(bf16)
    got = tn(pick, back[...].reshape(ROWS, W)) + tn(pickh, backh[...])
    rows_ref[...] = got.astype(bf16)
    rel = seen_from(ids, x, zh, c)
    lane = jnp.where(first, rel * SLOT + rank, ROWS + e * SLOT + rank - SLOT)
    slot = lax.broadcasted_iota(jnp.int32, (2 * ROWS, n), 0)
    here = (slot == lane).astype(f32).astype(bf16)
    found = jnp.dot(gback[:, 0, 0 : 2 * ROWS].astype(bf16), here, preferred_element_type=f32)
    dgate = jnp.sum(onehot * found, axis=0, keepdims=True)
    count = jnp.sum(mr[...], axis=0)[2:3, :]
    across = lax.broadcasted_iota(jnp.int32, (E, 128), 0)
    diag = across == lax.broadcasted_iota(jnp.int32, (E, 128), 1)
    column = jnp.sum(jnp.where(diag, jnp.broadcast_to(count, (E, 128)), 0.0), axis=1, keepdims=True)
    pulls = onehot * dgate + 1.0 * E * (column / (E * n))
    gl_ref[...] = probs * (pulls - jnp.sum(probs * pulls, axis=0, keepdims=True))
    norm_ref[...] = jnp.sqrt(jnp.sum(gback[:, 0, 2 * ROWS : 2 * ROWS + 128], axis=0, keepdims=True))


def finish(ids, logits, back, backh, gback, mr):
    n = ids.shape[1]
    return pl.pallas_call(
        finish_kernel,
        in_specs=[VM] * 6,
        out_specs=[VM] * 3,
        out_shape=[
            jax.ShapeDtypeStruct((n, W), bf16),
            jax.ShapeDtypeStruct((E, n), f32),
            jax.ShapeDtypeStruct((1, 128), f32),
        ],
        name="finish",
    )(ids, logits, back, backh, gback, mr)


def local(rows_x, rows_dy, router_logits, expert_of, w_gate, w_up, w_down):
    ids = expert_of.reshape(1, -1)
    logits = router_logits.T
    s1, s2, m = lay_out(ids, logits, rows_x, rows_dy)
    back, backh, gback, mr, gg, gu, gd = moe(s1, s2, m, w_gate[0], w_up[0], w_down[0])
    grad_rows, grad_logits, norm = finish(ids, logits, back, backh, gback, mr)
    return grad_rows, grad_logits.T, gg[None], gu[None], gd[None], norm[0, 0]


def solution(mesh):
    rows = P("expert", None)
    weights = P("expert", "dp", None)
    return jax.shard_map(
        local,
        mesh=mesh,
        in_specs=(rows, rows, rows, rows, weights, weights, weights),
        out_specs=(P("expert", "dp"), rows, weights, weights, weights, P()),
        check_vma=False,
    )
```

time: 177 us -> 138 us (0.78)
  Pallas kernels: 174 us -> 129 us
  local copies, waits for them, and re-layouts: 0 us -> 8.7 us
    pallas_call x3 -> x1, Pallas kernels: 167 us -> 122 us  [moe(): pl.pallas_call(moe_kernel, in_specs=[ANY] * 6, out_specs=[VM] * 4 + [ANY]...]
    unnamed x0 -> x7, local copies, waits for them, and re-layouts: none -> 8.7 us
where the time goes in v3:
time: 138 us
  Pallas kernels  129 us (93%)
  local copies, waits for them, and re-layouts  8.7 us (6%)
    pallas_call x1, Pallas kernels, moe(): pl.pallas_call(moe_kernel, in_specs=[ANY] * 6, out_specs=[VM] * 4 + [ANY]...  122 us
    unnamed x7, local copies, waits for them, and re-layouts  8.7 us
    pallas_call x1, Pallas kernels, lay_out(): pl.pallas_call(slots_kernel, in_specs=[VM] * 4, out_specs=[VM] * 3, out_s...  4.64 us

profile of v3, /device:TPU:1, one launch (start us, length us, event | category | flops | bytes accessed | tf_op | source)
XLA Modules:
  0.0 138.2 jit_solution(4661692656720384116)
XLA Ops:
  0.6 4.6 %lay_out.1 = (bf16[2,2,256,512]{3,2,1,0:T(8,128)(2,1)}, bf16[2,8,96,512]{3,2,1,0:T(8,128)(2,1)}, f32[16,8,128]{2,1,0:T(8,128)}) custom-call(s32[1,256]{1,0:T(1,128)} %bitcast.19, f32[16,256]{1,0:T(8,128)} %bitcast.17, bf16[256,4096]{1,0:T(8,128)(2,1)} %x_ref.1, bf16[256,4096]{1,0:T(8,128)(2,1)} %dy_ref.1), custom_call_target="tpu_custom_call" | custom-call | tf_op jit(solution)/shard_map/lay_out/pallas_call | solution.py:111
  5.3 121.8 %moe.1 = (bf16[16,32,512]{2,1,0:T(8,128)(2,1)}, bf16[32,512]{1,0:T(8,128)(2,1)}, f32[16,1,1280]{2,1,0:T(1,128)}, f32[16,8,128]{2,1,0:T(8,128)}, f32[192,4096]{1,...) custom-call(bf16[2,2,256,512]{3,2,1,0:T(8,128)(2,1)} %get-tuple-element.19.s1, ...), custom_call_target="tpu_custom_call" | custom-call | tf_op jit(solution)/shard_map/moe/pallas_call | solution.py:759
  127.1 2.4 %finish.1 = (bf16[256,512]{1,0:T(8,128)(2,1)}, f32[16,256]{1,0:T(8,128)}, f32[1,128]{1,0:T(1,128)}) custom-call(s32[1,256]{1,0:T(1,128)} %bitcast.20, f32[16,256]{1,0:T(8,128)} %bitcast.18, bf16[16,32,512]{2,1,0:T(8,128)(2,1)} %get-tuple-element.22.back, bf16[32,512]{1,0:T(8,128)(2,1)} %get-tuple-element.23.backh, f32[16,1,1280]{2,1,0:T(1,128)} %get-tuple-element.24.gback, ...), custom_call_target="tpu_custom_call" | custom-call | tf_op jit(solution)/shard_map/finish/pallas_call | solution.py:824
  129.5 0.0 copy-start.1
  129.5 4.0 %copy.16 = f32[1,192,4096]{2,1,0:T(8,128)} copy(f32[1,192,4096]{2,1,0:T(8,128)} %bitcast.13) | data formatting | bytes 6291456
  133.5 0.0 copy-done.1
  133.5 0.0 copy-start
  133.5 1.7 %copy.17 = f32[1,192,4096]{2,1,0:T(8,128)} copy(f32[1,192,4096]{2,1,0:T(8,128)S(1)} %bitcast.12) | data formatting | bytes 6291456
  135.2 1.4 copy-done
  136.6 1.7 %copy.18 = f32[1,192,4096]{2,1,0:T(8,128)} copy(f32[1,192,4096]{2,1,0:T(8,128)S(1)} %bitcast.11) | data formatting | bytes 6291456
Async XLA Ops:
  129.5 4.0 %copy-start.1 = (f32[192,4096]{1,0:T(8,128)S(1)}, f32[192,4096]{1,0:T(8,128)}, u32[]{:S(2)}) copy-start(f32[192,4096]{1,0:T(8,128)} %get-tuple-element.29) | copy-start | bytes 9437188
  133.5 3.0 %copy-start = (f32[192,4096]{1,0:T(8,128)S(1)}, f32[192,4096]{1,0:T(8,128)}, u32[]{:S(2)}) copy-start(f32[192,4096]{1,0:T(8,128)} %get-tuple-element.30) | copy-start | bytes 9437188

commit v4 on v3

--- a/solution.py
+++ b/solution.py
@@ -61,10 +61,11 @@
 
 
 def seen_from(ids, x, zh, c):
-    return (((x - (ids >> 2)) & 3) * 2 + (zh ^ ((ids >> 1) & 1))) * 2 + c
-
-
-def slots_kernel(ids_ref, logits_ref, x_ref, dy_ref, s1_ref, s2_ref, m_ref):
+    dx = (x - (ids >> 2)) & 3
+    return ((dx ^ (dx >> 1)) + 4 * (zh ^ ((ids >> 1) & 1))) * 2 + c
+
+
+def slots_kernel(ids_ref, logits_ref, x_ref, dy_ref, s1_ref, s2_ref, s3_ref, m_ref):
     e, d, x, zh, c, y, zl = place()
     ids = ids_ref[...]
     onehot, rank = row_facts(ids, E)
@@ -84,11 +85,16 @@
         s1_ref[0, g] = jnp.dot(p, x_ref[:, at], preferred_element_type=f32).astype(bf16)
         s1_ref[1, g] = jnp.dot(p, dy_ref[:, at], preferred_element_type=f32).astype(bf16)
     home = jnp.where(ids == e, rank, jnp.where(ids == e + 1 - 2 * c, SLOT + rank, none))
-    p = perm(3 * SLOT, jnp.where(first, home, SLOT + rank))
+    dx = ((ids >> 2) - x) & 3
+    side = (3 + (dx & 2) + (ids & 1)) * SLOT + rank
+    home = jnp.where(((dx & 1) == 1) & jnp.logical_not(far), side, home)
+    p = perm(7 * SLOT, jnp.where(first, home, SLOT + rank))
     for j in range(NDP):
         at = slice(j * W, (j + 1) * W)
-        s2_ref[0, j] = jnp.dot(p, x_ref[:, at], preferred_element_type=f32).astype(bf16)
-        s2_ref[1, j] = jnp.dot(p, dy_ref[:, at], preferred_element_type=f32).astype(bf16)
+        got = jnp.dot(p, x_ref[:, at], preferred_element_type=f32).astype(bf16)
+        s2_ref[0, j] = got[: 3 * SLOT]
+        s3_ref[j] = got[3 * SLOT :]
+        s2_ref[1, j] = jnp.dot(p[: 3 * SLOT], dy_ref[:, at], preferred_element_type=f32).astype(bf16)
 
     gate = jnp.sum(soft(logits_ref[...]) * onehot, axis=0, keepdims=True).astype(bf16).astype(f32)
     lane = lax.broadcasted_iota(jnp.int32, (128, rows), 0)
@@ -111,10 +117,11 @@
     return pl.pallas_call(
         slots_kernel,
         in_specs=[VM] * 4,
-        out_specs=[VM] * 3,
+        out_specs=[VM] * 4,
         out_shape=[
             jax.ShapeDtypeStruct((2, 2, ROWS // 2, W), bf16),
             jax.ShapeDtypeStruct((2, NDP, 3 * SLOT, W), bf16),
+            jax.ShapeDtypeStruct((NDP, 4 * SLOT, W), bf16),
             jax.ShapeDtypeStruct((E, 8, 128), f32),
         ],
         name="lay_out",
@@ -221,9 +228,10 @@
 
 
 def others(x, zh):
+    order = (0, 1, 3, 2)
     for k in range(1, 8):
         dx, dz = k // 2, k % 2
-        yield k, ((4 - dx) % 4) * 2 + dz, (x + dx) % 4, (zh + dz) % 2
+        yield order[dx] + 4 * dz, order[(4 - dx) % 4] + 4 * dz, (x + dx) % 4, (zh + dz) % 2
 
 
 def sigmoid(v):
@@ -234,9 +242,10 @@
     _, _, x, _, c, _, _ = place()
     parts = []
     for g in range(E // 4):
-        at = g * 4 if t == 0 else ((g - x) & 3) * 4
+        dx = (g + 4 - x) % 4
+        at = g * 4 if t == 0 else (dx + dx // 2 - 2 * (dx // 3)) * 2
         part = mr[at, t : t + 1, :]
-        for i in range(1, 4):
+        for i in (1, 2, 3) if t == 0 else (1, 8, 9):
             part = part + mr[at + i, t : t + 1, :]
         parts.append(part if t == 0 else part * mr[c, 3:4, :])
     return jnp.concatenate(parts, axis=1)
@@ -391,7 +400,7 @@
 
 
 def moe_kernel(
-    s1, s2, ms, wg_hbm, wu_hbm, wd_hbm,
+    s1, s2, s3, ms, wg_hbm, wu_hbm, wd_hbm,
     back, backh, gback, mr, gg, gu, gd,
     *refs,
 ):
@@ -401,7 +410,7 @@
     (
         cold, extra, weights, acc, lhs, rhs, stage, dxc, dxh, gp,
         rc, hs, hin, outh, hp, gall, gsum,
-        st_s, st_r, m_s, m_r, sib_s, sib_r, dp_s, dp_r, ex_s, ex_r, xs_s, xs_r, loc, osem,
+        st_s, st_r, sd_s, sd_r, m_s, m_r, sib_s, sib_r, dp_s, dp_r, ex_s, ex_r, xs_s, xs_r, loc, osem,
         g_s, g_r, b_s, b_r, gb_s, gb_r, x_s, x_r, q_s, q_r,
     ) = refs
     wg, wu, wd = weights.at[0], weights.at[1], weights.at[2]
@@ -411,15 +420,16 @@
     right, left, pair = to(e, ((y + 1) % 4) * 2 + zl), to(e, ((y + 3) % 4) * 2 + zl), to(e, dbar)
     x_r_dev, x_l_dev = to(expert_at((x + 1) % 4, zh, c), d), to(expert_at((x + 3) % 4, zh, c), d)
     z_p = to(expert_at(x, 1 - zh, c), dbar)
-    peers, places, mine = [expert_at(x, zh, 1 - c)], [1 - c], [c]
+    peers, places, mine, parts = [expert_at(x, zh, 1 - c)], [1 - c], [c], [0]
     row_peers = []
-    for rel, seen, x2, zh2 in others(x, zh):
+    for here, seen, x2, zh2 in others(x, zh):
         for c2 in (0, 1):
             peers.append(expert_at(x2, zh2, c2))
-            places.append(rel * 2 + c2)
+            places.append(here * 2 + c2)
             mine.append(seen * 2 + c)
-            d2 = d if rel % 2 == 0 else dbar
-            row_peers.append((rel, seen, expert_at(x2, zh2, c2), d2, x2 * 2 + c2))
+            parts.append(here // 4)
+            d2 = d if here < 4 else dbar
+            row_peers.append((here, seen, expert_at(x2, zh2, c2), d2, x2 * 2 + c2))
     dps = [(d + k) % NDP for k in range(1, NDP)]
 
     own_in = [
@@ -434,7 +444,7 @@
         copy.start()
     meet(
         [to(e2, d) for e2 in peers] + [to(e, d2) for d2 in dps]
-        + [to(p[2], dbar) for p in row_peers if p[0] % 2]
+        + [to(p[2], dbar) for p in row_peers if p[0] >= 4]
     )
 
     rest = []
@@ -455,9 +465,11 @@
         return pl.ds(pl.multiple_of(n * SLOT, SLOT), SLOT)
 
     for a in (0, 1):
-        for rel, seen, e2, d2, q in row_peers:
+        for here, seen, e2, d2, q in row_peers:
+            if a == 0 and here in (1, 2):
+                continue
             pltpu.make_async_remote_copy(
-                s1.at[a, rel % 2, slots_at(q), :], cold.at[a, d2, slots_at(seen * 2 + c), :],
+                s1.at[a, here // 4, slots_at(q), :], cold.at[a, d2, slots_at(seen * 2 + c), :],
                 st_s.at[a], st_r.at[a], device_id=to(e2, d2), device_id_type=MESH,
             ).start()
     meta_peers = row_peers + [(0, 0, expert_at(x, zh, 1 - c), d, 0)]
@@ -465,10 +477,10 @@
         send(ms.at[e2], mr.at[seen * 2 + c], m_s.at[n], m_r.at[seen * 2 + c], to(e2, d2))
     send(s2.at[:, :, SLOT : 2 * SLOT, :], cold.at[:, :, slots_at(c), :], sib_s, sib_r, sib)
 
-    half = (ROWS - LOCAL) // 2
-
     def dp_piece(a, j, z, h):
-        rows = {None: (LOCAL, 2 * half), 0: (LOCAL, half), 1: (LOCAL + half, half)}[h]
+        start = (3 if a == 0 else 1) * 2 * SLOT
+        half = (ROWS - start) // 2
+        rows = {None: (start, 2 * half), 0: (start, half), 1: (start + half, half)}[h]
         return cold.at[a, j * 2 + z, pl.ds(*rows), :]
 
     def ex_piece_of(core):
@@ -503,7 +515,7 @@
         shares.append((a, j, z))
 
     def whole(a):
-        ref = cold.at[a, d, pl.ds(LOCAL, ROWS - LOCAL), :]
+        ref = dp_piece(a, y, zl, None)
         return pltpu.make_async_remote_copy(
             ref, ref, st_s.at[a], st_r.at[a], device_id=sib, device_id_type=MESH
         )
@@ -578,21 +590,25 @@
 
         return lax.fori_loop(first, first + 2, step, sq)
 
+    ex.start(1)
+    ex.start(0)
+    for i, (x2, seen) in enumerate((((x + 1) % 4, 2), ((x + 3) % 4, 1))):
+        for c2 in (0, 1):
+            send(
+                s3.at[:, pl.ds((i * 2 + c2) * SLOT, SLOT), :],
+                cold.at[0, :, slots_at(seen * 2 + c), :],
+                sd_s.at[i * 2 + c2], sd_r.at[(seen - 1) * 2 + c], to(expert_at(x2, zh, c2), d),
+            )
+    share(0, x, zh, s2.at[0, :, 2 * SLOT :, :])
+    share(1, x, zh, s2.at[1, :, 2 * SLOT :, :])
     acc[...] = jnp.zeros_like(acc)
-    for copy in own_in[2:]:
-        copy.wait()
-    own_in[0].wait()
-    wait(cold.at[:, :, slots_at(1 - c), :], sib_s, sib_r)
     whole(0).wait_recv()
     dp.start(0)
-    ex.start(0)
-    forward_x(cold, 0, lambda i: d, 1)
     whole(1).wait_recv()
     dp.start(1)
-    ex.start(1)
-    own_in[1].wait()
-    share(0, x, zh, s2.at[0, :, 2 * SLOT :, :])
-    share(1, x, zh, s2.at[1, :, 2 * SLOT :, :])
+    for copy in own_in:
+        copy.wait()
+    wait(cold.at[:, :, slots_at(1 - c), :], sib_s, sib_r)
     forward_dy(cold, 0, lambda i: d, 1)
     ex.s2()
     ex.s3()
@@ -603,21 +619,26 @@
     ex.s6()
     for a, j, z in ((0, ex.jl, zh), (0, ex.jr, zh), (1, x, 1 - zh), (1, ex.jl, zh), (1, ex.jr, zh)):
         share(a, j, z)
-    forward_x(cold, 0, lambda i: ((y + 1 + 2 * i) % 4) * 2 + zl, 2)
+    dp.s4()
+    dp.s5()
+    dp.s6()
+    for i in range(4):
+        wait(cold.at[0, :, pl.ds((2 + i) * SLOT, SLOT), :], sd_s.at[0], sd_r.at[i])
     ex.s7()
     ex.s8()
     share(0, ex.jd, zh)
-    dp.s4()
-    dp.s5()
-    dp.s6()
-    forward_dy(cold, 0, lambda i: ((y + 1 + 2 * i) % 4) * 2 + zl, 2)
-    forward_dy(cold, 0, lambda i: dbar, 1)
+    dp.s7()
+    dp.s8()
+    forward_x(cold, 0, lambda i: d, 1)
+    forward_x(cold, 0, lambda i: ((y + 1 + 2 * i) % 4) * 2 + zl, 2)
     ex.s9()
     ex.s10()
     share(1, ex.jl, 1 - zh)
     share(1, ex.jr, 1 - zh)
-    dp.s7()
-    dp.s8()
+    dp.s9()
+    dp.s10()
+    forward_dy(cold, 0, lambda i: ((y + 1 + 2 * i) % 4) * 2 + zl, 2)
+    forward_dy(cold, 0, lambda i: dbar, 1)
     dp.got("0oz", 0, y, 1 - zl, None)
     forward_x(cold, 0, lambda i: i * (dp.jd * 2 + zl) + (1 - i) * dbar, 2)
     ex.got("0oz", 0, x, 1 - zh, None)
@@ -632,36 +653,11 @@
     share(1, ex.jd, 1 - zh)
     ex.end_of_0_d()
     share(0, ex.jd, 1 - zh)
-    dp.s9()
-    dp.s10()
     forward_dy(cold, 0, lambda i: ((y + 1 + 2 * i) % 4) * 2 + 1 - zl, 2)
     for i in [1 - c] + list(range(2, E)):
         wait(mr.at[i], m_s.at[0], m_r.at[i])
-    for i, where in enumerate(shares):
-        wait(ex_other(*where, None), xs_s.at[i], xs_r.at[i])
-    forward_x(extra, 1, lambda i: i, NDP)
-    forward_dy(extra, 1, lambda i: i, NDP)
-    between(1)
-    rows_back(1, dxh, lambda i: i, NDP)
-    far = [X.jd * 2, X.jd * 2 + 1, X.jr * 2, X.jl * 2, X.jr * 2 + 1, X.jl * 2 + 1, x * 2, x * 2 + 1]
-
-    def h_rows(chip, core):
-        return slots_at(chip * 2 + core)
-
-    for i, chip in enumerate(far):
-        send(dxh.at[:, h_rows(chip, 1 - c)], hin.at[chip], x_s.at[i], x_r.at[i], sib)
     dp.end_of_1_d()
     forward_dy(cold, 0, lambda i: dp.jd * 2 + zl, 1)
-    for i, chip in enumerate(far):
-        wait(hin.at[chip], x_s.at[i], x_r.at[i])
-        add_into(hs.at[chip], dxh.at[:, h_rows(chip, c)], hin.at[chip])
-        if i == 1:
-            X.start0_far()
-        if i == 5:
-            X.start0_right()
-            X.start0_left()
-    for way in ("d", "r", "l", "0"):
-        X.start1(way)
     dp.got("0lz", 0, dp.jl, 1 - zl, None)
     dp.got("0rz", 0, dp.jr, 1 - zl, None)
     forward_x(cold, 0, lambda i: ((y + 1 + 2 * i) % 4) * 2 + 1 - zl, 2)
@@ -682,41 +678,67 @@
     C.start1("l")
     rows_back(0, dxc, lambda i: y * 2 + i, 2)
     C.start1("0")
+    for i, where in enumerate(shares):
+        wait(ex_other(*where, None), xs_s.at[i], xs_r.at[i])
+    forward_x(extra, 1, lambda i: i, NDP)
+    forward_dy(extra, 1, lambda i: i, NDP)
+    C.relay0()
+    C.relay1_far()
+    between(1)
+    far = [X.jd * 2, X.jd * 2 + 1, X.jr * 2, X.jl * 2, X.jr * 2 + 1, X.jl * 2 + 1, x * 2, x * 2 + 1]
+    rows_back(1, dxh, lambda i: i, NDP)
+
+    def h_rows(chip, core):
+        return slots_at(chip * 2 + core)
+
+    for i, chip in enumerate(far):
+        send(dxh.at[:, h_rows(chip, 1 - c)], hin.at[chip], x_s.at[i], x_r.at[i], sib)
+    C.relay1_near()
+    for i, chip in enumerate(far):
+        wait(hin.at[chip], x_s.at[i], x_r.at[i])
+        add_into(hs.at[chip], dxh.at[:, h_rows(chip, c)], hin.at[chip])
+        if i == 1:
+            X.start0_far()
+        if i == 5:
+            X.start0_right()
+            X.start0_left()
+    for way in ("d", "r", "l", "0"):
+        X.start1(way)
+    C.relay1_last()
+    sq = weights_back(0, jnp.zeros((8, W), f32), True)
     X.relay0()
     X.relay1_far()
     X.relay1_near()
-    sq = weights_back(0, jnp.zeros((8, W), f32), True)
-    C.relay0()
-    C.relay1_far()
+    C.pair0()
+    sq = weights_back(2, sq, False)
     X.relay1_last()
     X.pair0()
-    sq = weights_back(2, sq, False)
-    C.relay1_near()
     sq = weights_back(4, sq, False)
-    C.relay1_last()
+
+    def give(a):
+        for n, e2 in enumerate(peers):
+            if parts[n] == a:
+                send(
+                    rc.at[0, slots_at(places[n]), :],
+                    back.at[e], b_s.at[n], b_r.at[mine[n]], to(e2, d),
+                )
+
+    C.end1(rc.at[:, pl.ds(HR, HR)])
+    give(1)
     sq = weights_back(6, sq, False)
     total = jnp.sum(jnp.sum(sq, axis=0, keepdims=True), axis=1, keepdims=True)
     gp[0:1, 2 * ROWS :] = jnp.broadcast_to(total, (1, GW - 2 * ROWS))
     for k, d2 in enumerate(dps):
         send(gp, gall.at[d], g_s.at[k], g_r.at[k], to(e, d2))
     gall[d] = gp[...]
-    C.pair0()
+    C.end0(rc.at[:, pl.ds(0, HR)])
+    give(0)
+    back[e] = rc[0, slots_at(c), :]
     X.end1(outh.at[pl.ds(NDP // 2, NDP // 2)])
     X.end0(outh.at[pl.ds(0, NDP // 2)])
     for k, d2 in enumerate(dps):
         send(outh.at[d2], hp.at[d], q_s.at[k], q_r.at[k], to(e, d2))
     hp[d] = outh[d]
-
-    def give(a):
-        for n, e2 in enumerate(peers):
-            if (n >= 7) == (a == 1):
-                send(
-                    rc.at[0, slots_at(places[n]), :],
-                    back.at[e], b_s.at[n], b_r.at[mine[n]], to(e2, d),
-                )
-
-    C.end1(rc.at[:, pl.ds(HR, HR)])
-    give(1)
     for k in range(NDP - 1):
         wait(gall.at[(d + NDP - 1 - k) % NDP], g_s.at[k], g_r.at[k])
     total = gall[0]
@@ -726,9 +748,6 @@
     gback[e] = total
     for n, e2 in enumerate(peers):
         send(gsum, gback.at[e], gb_s.at[n], gb_r.at[mine[n]], to(e2, d))
-    C.end0(rc.at[:, pl.ds(0, HR)])
-    give(0)
-    back[e] = rc[0, slots_at(c), :]
     for k in range(NDP - 1):
         wait(hp.at[(d + NDP - 1 - k) % NDP], q_s.at[k], q_r.at[k])
     total = hp[0].astype(f32)
@@ -752,13 +771,13 @@
     X.drain()
 
 
-def moe(s1, s2, m, wg, wu, wd):
+def moe(s1, s2, s3, m, wg, wu, wd):
     FFL, width = wg.shape
     D = pltpu.SemaphoreType.DMA
     V = pltpu.VMEM
     return pl.pallas_call(
         moe_kernel,
-        in_specs=[ANY] * 6,
+        in_specs=[ANY] * 7,
         out_specs=[VM] * 4 + [ANY] * 3,
         out_shape=[
             jax.ShapeDtypeStruct((E, SLOT, W), bf16),
@@ -779,7 +798,7 @@
             V((NDP, NDP, SLOT, W), bf16), V((NDP, NDP, SLOT, W), bf16),
             V((NDP, SLOT, W), bf16), V((NDP, SLOT, W), bf16),
             V((NDP, 1, GW), f32), V((1, GW), f32),
-            D((2,)), D((2,)), D((15,)), D((16,)), D, D,
+            D((2,)), D((2,)), D((4,)), D((4,)), D((15,)), D((16,)), D, D,
             D((18,)), D((18,)), D((18,)), D((18,)), D((16,)), D((16,)), D((6,)), D((2, 3)),
             D((7,)), D((7,)), D((15,)), D((16,)), D((15,)), D((16,)),
             D((8,)), D((8,)), D((7,)), D((7,)),
@@ -788,10 +807,38 @@
             collective_id=1, has_side_effects=True, vmem_limit_bytes=62 * 1024 * 1024
         ),
         name="moe",
-    )(s1, s2, m, wg, wu, wd)
-
-
-def finish_kernel(ids_ref, logits_ref, back, backh, gback, mr, rows_ref, gl_ref, norm_ref):
+    )(s1, s2, s3, m, wg, wu, wd)
+
+
+GRAD_CUTS = 4
+
+
+def finish_kernel(
+    ids_ref, logits_ref, back, backh, gback, mr, g1, g2, g3,
+    rows_ref, gl_ref, norm_ref, o1, o2, o3, held, isem, osem,
+):
+    cuts = [(i, k) for i in range(3) for k in range(GRAD_CUTS)]
+    n = g1.shape[0] // GRAD_CUTS
+
+    def load(i, k):
+        r = pl.ds(k * n, n)
+        return pltpu.make_async_copy((g1, g2, g3)[i].at[r], held.at[i, r], isem.at[i, k])
+
+    def store(i, k):
+        r = pl.ds(k * n, n)
+        return pltpu.make_async_copy(held.at[i, r], (o1, o2, o3)[i].at[r], osem.at[i, k])
+
+    for cut in cuts:
+        load(*cut).start()
+    for cut in cuts:
+        load(*cut).wait()
+        store(*cut).start()
+    finish_rows(ids_ref, logits_ref, back, backh, gback, mr, rows_ref, gl_ref, norm_ref)
+    for cut in cuts:
+        store(*cut).wait()
+
+
+def finish_rows(ids_ref, logits_ref, back, backh, gback, mr, rows_ref, gl_ref, norm_ref):
     e, _, x, zh, c, _, _ = place()
     ids = ids_ref[...]
     onehot, rank = row_facts(ids, E)
@@ -819,27 +866,37 @@
     norm_ref[...] = jnp.sqrt(jnp.sum(gback[:, 0, 2 * ROWS : 2 * ROWS + 128], axis=0, keepdims=True))
 
 
-def finish(ids, logits, back, backh, gback, mr):
+def finish(ids, logits, back, backh, gback, mr, *grads):
     n = ids.shape[1]
     return pl.pallas_call(
         finish_kernel,
-        in_specs=[VM] * 6,
-        out_specs=[VM] * 3,
+        in_specs=[VM] * 6 + [ANY] * 3,
+        out_specs=[VM] * 3 + [ANY] * 3,
         out_shape=[
             jax.ShapeDtypeStruct((n, W), bf16),
             jax.ShapeDtypeStruct((E, n), f32),
             jax.ShapeDtypeStruct((1, 128), f32),
+        ]
+        + [jax.ShapeDtypeStruct(g.shape, f32) for g in grads],
+        scratch_shapes=[
+            pltpu.VMEM((3,) + grads[0].shape, f32),
+            pltpu.SemaphoreType.DMA((3, GRAD_CUTS)),
+            pltpu.SemaphoreType.DMA((3, GRAD_CUTS)),
         ],
         name="finish",
-    )(ids, logits, back, backh, gback, mr)
+    )(ids, logits, back, backh, gback, mr, *grads)
 
 
 def local(rows_x, rows_dy, router_logits, expert_of, w_gate, w_up, w_down):
     ids = expert_of.reshape(1, -1)
     logits = router_logits.T
-    s1, s2, m = lay_out(ids, logits, rows_x, rows_dy)
-    back, backh, gback, mr, gg, gu, gd = moe(s1, s2, m, w_gate[0], w_up[0], w_down[0])
-    grad_rows, grad_logits, norm = finish(ids, logits, back, backh, gback, mr)
+    s1, s2, s3, m = lay_out(ids, logits, rows_x, rows_dy)
+    back, backh, gback, mr, gg, gu, gd = moe(
+        s1, s2, s3, m, w_gate[0], w_up[0], w_down[0]
+    )
+    grad_rows, grad_logits, norm, gg, gu, gd = finish(
+        ids, logits, back, backh, gback, mr, gg, gu, gd
+    )
     return grad_rows, grad_logits.T, gg[None], gu[None], gd[None], norm[0, 0]
 
 

time: 138 us -> 131 us (0.949)
  local copies, waits for them, and re-layouts: 8.7 us -> 0 us
  Pallas kernels: 129 us -> 131 us
    unnamed x7 -> x0, local copies, waits for them, and re-layouts: 8.7 us -> none
    pallas_call x3, Pallas kernels: 129 us -> 131 us  [the longest x1 116 us: moe(): pl.pallas_call(moe_kernel, in_specs=[ANY] * 7, out_specs=[VM] * 4 + [ANY]...]
where the time goes in v4:
time: 131 us
  Pallas kernels  131 us (100%)
    pallas_call x1, Pallas kernels, moe(): pl.pallas_call(moe_kernel, in_specs=[ANY] * 7, out_specs=[VM] * 4 + [ANY]...  116 us
    pallas_call x1, Pallas kernels, finish(): pl.pallas_call(finish_kernel, in_specs=[VM] * 6 + [ANY] * 3, out_specs=[V...  9.13 us
    pallas_call x1, Pallas kernels, lay_out(): pl.pallas_call(slots_kernel, in_specs=[VM] * 4, out_specs=[VM] * 4, out_s...  5.19 us

profile of v4, /device:TPU:1, one launch (start us, length us, event | category | flops | bytes accessed | tf_op | source)
XLA Modules:
  0.0 131.3 jit_solution(614793189974793112)
XLA Ops:
  0.6 5.2 %lay_out.1 = (bf16[2,2,256,512]{3,2,1,0:T(8,128)(2,1)}, bf16[2,8,96,512]{3,2,1,0:T(8,128)(2,1)}, bf16[8,128,512]{2,1,0:T(8,128)(2,1)}, f32[16,8,128]{2,1,0:T(8,128)}) custom-call(s32[1,256]{1,0:T(1,128)} %bitcast.16, f32[16,256]{1,0:T(8,128)} %bitcast.14, bf16[256,4096]{1,0:T(8,128)(2,1)} %x_ref.1, bf16[256,4096]{1,0:T(8,128)(2,1)} %dy_ref.1), custom_call_target="tpu_custom_call" | custom-call | tf_op jit(solution)/shard_map/lay_out/pallas_call | solution.py:117
  5.8 116.2 %moe.1 = (bf16[16,32,512]{2,1,0:T(8,128)(2,1)}, bf16[32,512]{1,0:T(8,128)(2,1)}, f32[16,1,1280]{2,1,0:T(1,128)}, f32[16,8,128]{2,1,0:T(8,128)}, f32[192,4096]{1,...) custom-call(bf16[2,2,256,512]{3,2,1,0:T(8,128)(2,1)} %get-tuple-element.23.s1, ...), custom_call_target="tpu_custom_call" | custom-call | tf_op jit(solution)/shard_map/moe/pallas_call | solution.py:778
  122.1 9.1 %finish.1 = (bf16[256,512]{1,0:T(8,128)(2,1)}, f32[16,256]{1,0:T(8,128)}, f32[1,128]{1,0:T(1,128)}, f32[192,4096]{1,0:T(8,128)}, f32[192,4096]{1,0:T(8,128)}, /*index=5*/f32[192,4096]{1,0:T(8,128)}) custom-call(s32[1,256]{1,0:T(1,128)} %bitcast.17, f32[16,256]{1,0:T(8,128)} %bitcast.15, bf16[16,32,512]{2,1,0:T(8,128)(2,1)} %get-tuple-element.27.back, ...), custom_call_target="tpu_custom_call" | custom-call | tf_op jit(solution)/shard_map/finish/pallas_call | solution.py:871

commit v5 on v4

--- a/solution.py
+++ b/solution.py
@@ -408,9 +408,9 @@
     c_refs, refs = refs[:17], refs[17:]
     h_refs, refs = refs[:17], refs[17:]
     (
-        cold, extra, weights, acc, lhs, rhs, stage, dxc, dxh, gp,
+        cold, extra, weights, acc, lhs, rhs, dxc, dxh, gp,
         rc, hs, hin, outh, hp, gall, gsum,
-        st_s, st_r, sd_s, sd_r, m_s, m_r, sib_s, sib_r, dp_s, dp_r, ex_s, ex_r, xs_s, xs_r, loc, osem,
+        st_s, st_r, sd_s, sd_r, m_s, m_r, sib_s, sib_r, dp_s, dp_r, ex_s, ex_r, xs_s, xs_r, loc,
         g_s, g_r, b_s, b_r, gb_s, gb_r, x_s, x_r, q_s, q_r,
     ) = refs
     wg, wu, wd = weights.at[0], weights.at[1], weights.at[2]
@@ -569,23 +569,13 @@
 
     outs = (gg, gu, gd)
 
-    def put(j, slot, i):
-        return pltpu.make_async_copy(
-            stage.at[slot, i], outs[i].at[:, cols(j)], osem.at[slot, i]
-        )
-
-    def weights_back(first, sq, fresh):
+    def weights_back(first, sq):
         def step(j, sq):
-            slot = j % 2
-            if not fresh:
-                for i in range(3):
-                    put(j - 2, slot, i).wait()
             for i in range(3):
                 v = jnp.dot(lhs[0, i], cold[i // 2, j], preferred_element_type=f32)
                 v += jnp.dot(lhs[1, i], extra[i // 2, j], preferred_element_type=f32)
-                stage[slot, i] = v
+                outs[i][:, cols(j)] = v
                 sq = sq + jnp.sum((v * v).reshape(-1, 8, W), axis=0)
-                put(j, slot, i).start()
             return sq
 
         return lax.fori_loop(first, first + 2, step, sq)
@@ -704,16 +694,16 @@
             X.start0_left()
     for way in ("d", "r", "l", "0"):
         X.start1(way)
+    C.pair0()
     C.relay1_last()
-    sq = weights_back(0, jnp.zeros((8, W), f32), True)
+    sq = weights_back(0, jnp.zeros((8, W), f32))
     X.relay0()
     X.relay1_far()
     X.relay1_near()
-    C.pair0()
-    sq = weights_back(2, sq, False)
+    sq = weights_back(2, sq)
     X.relay1_last()
     X.pair0()
-    sq = weights_back(4, sq, False)
+    sq = weights_back(4, sq)
 
     def give(a):
         for n, e2 in enumerate(peers):
@@ -723,14 +713,14 @@
                     back.at[e], b_s.at[n], b_r.at[mine[n]], to(e2, d),
                 )
 
-    C.end1(rc.at[:, pl.ds(HR, HR)])
-    give(1)
-    sq = weights_back(6, sq, False)
+    sq = weights_back(6, sq)
     total = jnp.sum(jnp.sum(sq, axis=0, keepdims=True), axis=1, keepdims=True)
     gp[0:1, 2 * ROWS :] = jnp.broadcast_to(total, (1, GW - 2 * ROWS))
     for k, d2 in enumerate(dps):
         send(gp, gall.at[d], g_s.at[k], g_r.at[k], to(e, d2))
     gall[d] = gp[...]
+    C.end1(rc.at[:, pl.ds(HR, HR)])
+    give(1)
     C.end0(rc.at[:, pl.ds(0, HR)])
     give(0)
     back[e] = rc[0, slots_at(c), :]
@@ -758,9 +748,6 @@
     for i in [1 - c] + list(range(2, E)):
         wait(back.at[0], b_s.at[0], b_r.at[i])
         wait(gback.at[0], gb_s.at[0], gb_r.at[i])
-    for j in (NDP - 2, NDP - 1):
-        for i in range(3):
-            put(j, j % 2, i).wait()
     whole(0).wait_send()
     whole(1).wait_send()
     for copy in rest:
@@ -778,64 +765,50 @@
     return pl.pallas_call(
         moe_kernel,
         in_specs=[ANY] * 7,
-        out_specs=[VM] * 4 + [ANY] * 3,
+        out_specs=[VM] * 7,
         out_shape=[
-            jax.ShapeDtypeStruct((E, SLOT, W), bf16),
-            jax.ShapeDtypeStruct((SLOT, W), bf16),
-            jax.ShapeDtypeStruct((E, 1, GW), f32),
-            jax.ShapeDtypeStruct((E, 8, 128), f32),
+            pltpu.VMEM((E, SLOT, W), bf16),
+            pltpu.VMEM((SLOT, W), bf16),
+            pltpu.VMEM((E, 1, GW), f32),
+            pltpu.VMEM((E, 8, 128), f32),
         ]
-        + [jax.ShapeDtypeStruct((FFL, width), f32)] * 3,
+        + [pltpu.VMEM((FFL, width), f32)] * 3,
         scratch_shapes=Scatter.scratch(C_PIECE, C_HALF)
         + Scatter.scratch(H_PIECE, H_HALF)
         + [
             V((2, NDP, ROWS, W), bf16), V((2, NDP, ROWS, W), bf16),
             V((3, FFL, width), bf16),
             V((2, 3, FFL, ROWS), f32), V((2, 3, FFL, ROWS), bf16), V((2, ROWS, 2 * FFL), bf16),
-            V((2, 3, FFL, W), f32),
             V((NDP, ROWS, W), bf16), V((NDP, ROWS, W), bf16), V((1, GW), f32),
             V((1, ROWS, W), bf16),
             V((NDP, NDP, SLOT, W), bf16), V((NDP, NDP, SLOT, W), bf16),
             V((NDP, SLOT, W), bf16), V((NDP, SLOT, W), bf16),
             V((NDP, 1, GW), f32), V((1, GW), f32),
             D((2,)), D((2,)), D((4,)), D((4,)), D((15,)), D((16,)), D, D,
-            D((18,)), D((18,)), D((18,)), D((18,)), D((16,)), D((16,)), D((6,)), D((2, 3)),
+            D((18,)), D((18,)), D((18,)), D((18,)), D((16,)), D((16,)), D((6,)),
             D((7,)), D((7,)), D((15,)), D((16,)), D((15,)), D((16,)),
             D((8,)), D((8,)), D((7,)), D((7,)),
         ],
         compiler_params=pltpu.CompilerParams(
-            collective_id=1, has_side_effects=True, vmem_limit_bytes=62 * 1024 * 1024
+            collective_id=1, has_side_effects=True, vmem_limit_bytes=54 * 1024 * 1024
         ),
         name="moe",
     )(s1, s2, s3, m, wg, wu, wd)
 
 
-GRAD_CUTS = 4
-
-
 def finish_kernel(
     ids_ref, logits_ref, back, backh, gback, mr, g1, g2, g3,
-    rows_ref, gl_ref, norm_ref, o1, o2, o3, held, isem, osem,
+    rows_ref, gl_ref, norm_ref, o1, o2, o3, osem,
 ):
-    cuts = [(i, k) for i in range(3) for k in range(GRAD_CUTS)]
-    n = g1.shape[0] // GRAD_CUTS
-
-    def load(i, k):
-        r = pl.ds(k * n, n)
-        return pltpu.make_async_copy((g1, g2, g3)[i].at[r], held.at[i, r], isem.at[i, k])
-
-    def store(i, k):
-        r = pl.ds(k * n, n)
-        return pltpu.make_async_copy(held.at[i, r], (o1, o2, o3)[i].at[r], osem.at[i, k])
-
-    for cut in cuts:
-        load(*cut).start()
-    for cut in cuts:
-        load(*cut).wait()
-        store(*cut).start()
+    stores = [
+        pltpu.make_async_copy(g, o, osem.at[i])
+        for i, (g, o) in enumerate(((g1, o1), (g2, o2), (g3, o3)))
+    ]
+    for copy in stores:
+        copy.start()
     finish_rows(ids_ref, logits_ref, back, backh, gback, mr, rows_ref, gl_ref, norm_ref)
-    for cut in cuts:
-        store(*cut).wait()
+    for copy in stores:
+        copy.wait()
 
 
 def finish_rows(ids_ref, logits_ref, back, backh, gback, mr, rows_ref, gl_ref, norm_ref):
@@ -870,7 +843,7 @@
     n = ids.shape[1]
     return pl.pallas_call(
         finish_kernel,
-        in_specs=[VM] * 6 + [ANY] * 3,
+        in_specs=[VM] * 9,
         out_specs=[VM] * 3 + [ANY] * 3,
         out_shape=[
             jax.ShapeDtypeStruct((n, W), bf16),
@@ -879,10 +852,9 @@
         ]
         + [jax.ShapeDtypeStruct(g.shape, f32) for g in grads],
         scratch_shapes=[
-            pltpu.VMEM((3,) + grads[0].shape, f32),
-            pltpu.SemaphoreType.DMA((3, GRAD_CUTS)),
-            pltpu.SemaphoreType.DMA((3, GRAD_CUTS)),
+            pltpu.SemaphoreType.DMA((3,)),
         ],
+        compiler_params=pltpu.CompilerParams(vmem_limit_bytes=20 * 1024 * 1024),
         name="finish",
     )(ids, logits, back, backh, gback, mr, *grads)
 
@@ -894,9 +866,9 @@
     back, backh, gback, mr, gg, gu, gd = moe(
         s1, s2, s3, m, w_gate[0], w_up[0], w_down[0]
     )
-    grad_rows, grad_logits, norm, gg, gu, gd = finish(
-        ids, logits, back, backh, gback, mr, gg, gu, gd
-    )
+    held = (back, backh, gback, mr, gg, gu, gd)
+    held = [pltpu.with_memory_space_constraint(v, pltpu.VMEM) for v in held]
+    grad_rows, grad_logits, norm, gg, gu, gd = finish(ids, logits, *held)
     return grad_rows, grad_logits.T, gg[None], gu[None], gd[None], norm[0, 0]
 
 

time: 131 us -> 123 us (0.939)
  Pallas kernels: 131 us -> 122 us
    pallas_call x2, Pallas kernels: 125 us -> 117 us  [the longest x1 112 us: moe(): pl.pallas_call(moe_kernel, in_specs=[ANY] * 7, out_specs=[VM] * 7, out_sh...]
where the time goes in v5:
time: 123 us
  Pallas kernels  122 us (99%)
    pallas_call x1, Pallas kernels, moe(): pl.pallas_call(moe_kernel, in_specs=[ANY] * 7, out_specs=[VM] * 7, out_sh...  112 us
    pallas_call x1, Pallas kernels, lay_out(): pl.pallas_call(slots_kernel, in_specs=[VM] * 4, out_specs=[VM] * 4, out_s...  5.19 us
    pallas_call x1, Pallas kernels, finish(): pl.pallas_call(finish_kernel, in_specs=[VM] * 9, out_specs=[VM] * 3 + [AN...  4.87 us

profile of v5, /device:TPU:1, one launch (start us, length us, event | category | flops | bytes accessed | tf_op | source)
XLA Modules:
  0.0 123.2 jit_solution(4991425558259107221)
XLA Ops:
  0.6 5.2 %lay_out.1 = (bf16[2,2,256,512]{3,2,1,0:T(8,128)(2,1)}, bf16[2,8,96,512]{3,2,1,0:T(8,128)(2,1)}, bf16[8,128,512]{2,1,0:T(8,128)(2,1)}, f32[16,8,128]{2,1,0:T(8,128)}) custom-call(s32[1,256]{1,0:T(1,128)} %bitcast.13, f32[16,256]{1,0:T(8,128)} %bitcast.11, bf16[256,4096]{1,0:T(8,128)(2,1)} %x_ref.1, bf16[256,4096]{1,0:T(8,128)(2,1)} %dy_ref.1), custom_call_target="tpu_custom_call" | custom-call | tf_op jit(solution)/shard_map/lay_out/pallas_call | solution.py:117
  5.8 0.0 copy-start
  5.8 0.0 copy-start.1
  5.8 112.3 %moe.1 = (bf16[16,32,512]{2,1,0:T(8,128)(2,1)S(1)}, bf16[32,512]{1,0:T(8,128)(2,1)S(1)}, f32[16,1,1280]{2,1,0:T(1,128)S(1)}, f32[16,8,128]{2,1,0:T(8,128)S(1)}, ...) custom-call(bf16[2,2,256,512]{3,2,1,0:T(8,128)(2,1)} %get-tuple-element.23.s1, ...), custom_call_target="tpu_custom_call" | custom-call | tf_op jit(solution)/shard_map/moe/pallas_call | solution.py:765
  118.1 0.0 copy-done
  118.1 0.0 copy-done.1
  118.1 4.9 %finish.1 = (bf16[256,512]{1,0:T(8,128)(2,1)}, f32[16,256]{1,0:T(8,128)}, f32[1,128]{1,0:T(1,128)}, f32[192,4096]{1,0:T(8,128)}, f32[192,4096]{1,0:T(8,128)}, /*index=5*/f32[192,4096]{1,0:T(8,128)}) custom-call(s32[1,256]{1,0:T(1,128)S(1)} %bitcast.14, f32[16,256]{1,0:T(8,128)S(1)} %bitcast.12, bf16[16,32,512]{2,1,0:T(8,128)(2,1)S(1)} %get-tuple-element.27.back, ...), custom_call_target="tpu_custom_call" | custom-call | tf_op jit(solution)/shard_map/finish/pallas_call | solution.py:844
Async XLA Ops:
  5.8 112.3 %copy-start = (f32[256,16]{0,1:T(8,128)S(1)}, f32[256,16]{0,1:T(8,128)}, u32[]{:S(2)}) copy-start(f32[256,16]{0,1:T(8,128)} %param.9) | copy-start | bytes 49156
  5.8 112.3 %copy-start.1 = (s32[256,1]{0,1:T(1,128)S(1)}, s32[256,1]{0,1:T(1,128)}, u32[]{:S(2)}) copy-start(s32[256,1]{0,1:T(1,128)} %param.10) | copy-start | bytes 3076

commit v6 on v5

--- a/solution.py
+++ b/solution.py
@@ -65,44 +65,36 @@
     return ((dx ^ (dx >> 1)) + 4 * (zh ^ ((ids >> 1) & 1))) * 2 + c
 
 
-def slots_kernel(ids_ref, logits_ref, x_ref, dy_ref, s1_ref, s2_ref, s3_ref, m_ref):
-    e, d, x, zh, c, y, zl = place()
-    ids = ids_ref[...]
-    onehot, rank = row_facts(ids, E)
-    rows = ids.shape[1]
-    none = -1
-
-    def perm(slots, target):
-        slot = lax.broadcasted_iota(jnp.int32, (slots, rows), 0)
-        return (slot == target).astype(f32).astype(bf16)
-
+def permute(slots, target):
+    slot = lax.broadcasted_iota(jnp.int32, (slots, target.shape[1]), 0)
+    return (slot == target).astype(f32).astype(bf16)
+
+
+def slot_maps(ids, rank):
+    e, _, x, zh, c, _, _ = place()
     far = (zh ^ ((ids >> 1) & 1)) == 1
+    near = jnp.logical_not(far)
     first = rank < SLOT
     chip = ((ids >> 2) * 2 + (ids & 1)) * SLOT + rank
-    for g, ours in ((0, jnp.logical_not(far)), (1, far)):
-        p = perm(ROWS // 2, jnp.where(first & ours, chip, none))
-        at = pl.ds(pl.multiple_of((d if g == 0 else y * 2 + 1 - zl) * W, W), W)
-        s1_ref[0, g] = jnp.dot(p, x_ref[:, at], preferred_element_type=f32).astype(bf16)
-        s1_ref[1, g] = jnp.dot(p, dy_ref[:, at], preferred_element_type=f32).astype(bf16)
-    home = jnp.where(ids == e, rank, jnp.where(ids == e + 1 - 2 * c, SLOT + rank, none))
+    maps = [permute(ROWS // 2, jnp.where(first & ours, chip, -1)) for ours in (near, far)]
+    home = jnp.where(ids == e, rank, jnp.where(ids == e + 1 - 2 * c, SLOT + rank, -1))
     dx = ((ids >> 2) - x) & 3
     side = (3 + (dx & 2) + (ids & 1)) * SLOT + rank
-    home = jnp.where(((dx & 1) == 1) & jnp.logical_not(far), side, home)
-    p = perm(7 * SLOT, jnp.where(first, home, SLOT + rank))
-    for j in range(NDP):
-        at = slice(j * W, (j + 1) * W)
-        got = jnp.dot(p, x_ref[:, at], preferred_element_type=f32).astype(bf16)
-        s2_ref[0, j] = got[: 3 * SLOT]
-        s3_ref[j] = got[3 * SLOT :]
-        s2_ref[1, j] = jnp.dot(p[: 3 * SLOT], dy_ref[:, at], preferred_element_type=f32).astype(bf16)
-
-    gate = jnp.sum(soft(logits_ref[...]) * onehot, axis=0, keepdims=True).astype(bf16).astype(f32)
+    home = jnp.where(((dx & 1) == 1) & near, side, home)
+    return maps + [permute(7 * SLOT, jnp.where(first, home, SLOT + rank))]
+
+
+def fill_meta(m_ref, ids, logits, onehot, rank):
+    e, _, x, zh, c, _, _ = place()
+    rows = ids.shape[1]
+    first = rank < SLOT
+    gate = jnp.sum(soft(logits) * onehot, axis=0, keepdims=True).astype(bf16).astype(f32)
     lane = lax.broadcasted_iota(jnp.int32, (128, rows), 0)
     spot = (seen_from(ids, x, zh, c) & 3) * SLOT + rank
     cold = (onehot * gate * first.astype(f32)).astype(bf16)
     cold = nt(cold, (lane == spot).astype(f32).astype(bf16))
     gate8 = jnp.broadcast_to(gate, (8, rows)).astype(bf16)
-    spot = jnp.where(first, none, (e & 3) * SLOT + rank - SLOT)
+    spot = jnp.where(first, -1, (e & 3) * SLOT + rank - SLOT)
     hot = nt(gate8, (lane == spot).astype(f32).astype(bf16))
     count = nt(jnp.ones((8, rows), bf16), (lane == ids).astype(f32).astype(bf16))
     line = lax.broadcasted_iota(jnp.int32, (8, 128), 0)
@@ -113,21 +105,6 @@
         m_ref[k] = jnp.where(line == 0, mine, jnp.where(line == 1, hot, rest))
 
 
-def lay_out(ids, logits, x, dy):
-    return pl.pallas_call(
-        slots_kernel,
-        in_specs=[VM] * 4,
-        out_specs=[VM] * 4,
-        out_shape=[
-            jax.ShapeDtypeStruct((2, 2, ROWS // 2, W), bf16),
-            jax.ShapeDtypeStruct((2, NDP, 3 * SLOT, W), bf16),
-            jax.ShapeDtypeStruct((NDP, 4 * SLOT, W), bf16),
-            jax.ShapeDtypeStruct((E, 8, 128), f32),
-        ],
-        name="lay_out",
-    )(ids, logits, x, dy)
-
-
 class Gather:
     names = (
         "0oz", "0or", "0ol", "0lr", "0lz", "0rl", "0rz", "0dz", "0ez",
@@ -218,13 +195,6 @@
     def drain(self):
         for copy in self.sent:
             copy.wait_send()
-
-
-def meet(partners):
-    barrier = pltpu.get_barrier_semaphore()
-    for dev in partners:
-        pl.semaphore_signal(barrier, inc=1, device_id=dev, device_id_type=MESH)
-    pl.semaphore_wait(barrier, len(partners))
 
 
 def others(x, zh):
@@ -400,7 +370,7 @@
 
 
 def moe_kernel(
-    s1, s2, s3, ms, wg_hbm, wu_hbm, wd_hbm,
+    ids_ref, logits_ref, x_hbm, dy_hbm, wg_hbm, wu_hbm, wd_hbm,
     back, backh, gback, mr, gg, gu, gd,
     *refs,
 ):
@@ -408,7 +378,7 @@
     c_refs, refs = refs[:17], refs[17:]
     h_refs, refs = refs[:17], refs[17:]
     (
-        cold, extra, weights, acc, lhs, rhs, dxc, dxh, gp,
+        s1, s2, s3, ms, in_s, cold, extra, weights, acc, lhs, rhs, dxc, dxh, gp,
         rc, hs, hin, outh, hp, gall, gsum,
         st_s, st_r, sd_s, sd_r, m_s, m_r, sib_s, sib_r, dp_s, dp_r, ex_s, ex_r, xs_s, xs_r, loc,
         g_s, g_r, b_s, b_r, gb_s, gb_r, x_s, x_r, q_s, q_r,
@@ -432,20 +402,38 @@
             row_peers.append((here, seen, expert_at(x2, zh2, c2), d2, x2 * 2 + c2))
     dps = [(d + k) % NDP for k in range(1, NDP)]
 
-    own_in = [
-        pltpu.make_async_copy(s2.at[:, :, 0:SLOT, :], cold.at[:, :, pl.ds(pl.multiple_of(c * SLOT, SLOT), SLOT), :], loc.at[0]),
-        pltpu.make_async_copy(s2.at[:, :, 2 * SLOT :, :], extra.at[:, :, pl.ds(pl.multiple_of(e * SLOT, SLOT), SLOT), :], loc.at[1]),
-        pltpu.make_async_copy(ms.at[e], mr.at[c], loc.at[2]),
-        pltpu.make_async_copy(wg_hbm, wg, loc.at[3]),
-        pltpu.make_async_copy(wu_hbm, wu, loc.at[4]),
-        pltpu.make_async_copy(wd_hbm, wd, loc.at[5]),
-    ]
-    for copy in own_in:
-        copy.start()
-    meet(
+    partners = (
         [to(e2, d) for e2 in peers] + [to(e, d2) for d2 in dps]
         + [to(p[2], dbar) for p in row_peers if p[0] >= 4]
     )
+    barrier = pltpu.get_barrier_semaphore()
+    for dev in partners:
+        pl.semaphore_signal(barrier, inc=1, device_id=dev, device_id_type=MESH)
+
+    R = ids_ref.shape[1]
+    loads = [
+        pltpu.make_async_copy(
+            ref.at[:, j * W : (j + 1) * W], dxc.at[j, a * R : (a + 1) * R], in_s.at[a, j]
+        )
+        for a, ref in ((0, x_hbm), (1, dy_hbm))
+        for j in range(NDP)
+    ]
+    loads += [
+        pltpu.make_async_copy(ref, weights.at[i], loc.at[3 + i])
+        for i, ref in enumerate((wg_hbm, wu_hbm, wd_hbm))
+    ]
+    for copy in loads:
+        copy.start()
+    ids = ids_ref[...]
+    onehot, rank = row_facts(ids, E)
+    maps = slot_maps(ids, rank)
+    for copy in loads[: 2 * NDP]:
+        copy.wait()
+    for a in (0, 1):
+        for g, chunk in ((0, d), (1, dbar)):
+            block = dxc[chunk, a * R : (a + 1) * R, :]
+            s1[a, g] = jnp.dot(maps[g], block, preferred_element_type=f32).astype(bf16)
+    pl.semaphore_wait(barrier, len(partners))
 
     rest = []
 
@@ -472,9 +460,15 @@
                 s1.at[a, here // 4, slots_at(q), :], cold.at[a, d2, slots_at(seen * 2 + c), :],
                 st_s.at[a], st_r.at[a], device_id=to(e2, d2), device_id_type=MESH,
             ).start()
-    meta_peers = row_peers + [(0, 0, expert_at(x, zh, 1 - c), d, 0)]
-    for n, (_, seen, e2, d2, _) in enumerate(meta_peers):
-        send(ms.at[e2], mr.at[seen * 2 + c], m_s.at[n], m_r.at[seen * 2 + c], to(e2, d2))
+    def lay(j, _):
+        got = jnp.dot(maps[2], dxc[j, 0:R, :], preferred_element_type=f32).astype(bf16)
+        s2[0, j] = got[: 3 * SLOT]
+        s3[j] = got[3 * SLOT :]
+        got = jnp.dot(maps[2][: 3 * SLOT], dxc[j, R : 2 * R, :], preferred_element_type=f32)
+        s2[1, j] = got.astype(bf16)
+        return 0
+
+    lax.fori_loop(0, NDP, lay, 0)
     send(s2.at[:, :, SLOT : 2 * SLOT, :], cold.at[:, :, slots_at(c), :], sib_s, sib_r, sib)
 
     def dp_piece(a, j, z, h):
@@ -591,12 +585,23 @@
             )
     share(0, x, zh, s2.at[0, :, 2 * SLOT :, :])
     share(1, x, zh, s2.at[1, :, 2 * SLOT :, :])
+    fill_meta(ms, ids, logits_ref[...], onehot, rank)
+    meta_peers = row_peers + [(0, 0, expert_at(x, zh, 1 - c), d, 0)]
+    for n, (_, seen, e2, d2, _) in enumerate(meta_peers):
+        send(ms.at[e2], mr.at[seen * 2 + c], m_s.at[n], m_r.at[seen * 2 + c], to(e2, d2))
+    own_in = [
+        pltpu.make_async_copy(s2.at[:, :, 0:SLOT, :], cold.at[:, :, slots_at(c), :], loc.at[0]),
+        pltpu.make_async_copy(s2.at[:, :, 2 * SLOT :, :], extra.at[:, :, slots_at(e), :], loc.at[1]),
+        pltpu.make_async_copy(ms.at[e], mr.at[c], loc.at[2]),
+    ]
+    for copy in own_in:
+        copy.start()
     acc[...] = jnp.zeros_like(acc)
     whole(0).wait_recv()
     dp.start(0)
     whole(1).wait_recv()
     dp.start(1)
-    for copy in own_in:
+    for copy in own_in + loads[2 * NDP :]:
         copy.wait()
     wait(cold.at[:, :, slots_at(1 - c), :], sib_s, sib_r)
     forward_dy(cold, 0, lambda i: d, 1)
@@ -758,13 +763,13 @@
     X.drain()
 
 
-def moe(s1, s2, s3, m, wg, wu, wd):
+def moe(ids, logits, x, dy, wg, wu, wd):
     FFL, width = wg.shape
     D = pltpu.SemaphoreType.DMA
     V = pltpu.VMEM
     return pl.pallas_call(
         moe_kernel,
-        in_specs=[ANY] * 7,
+        in_specs=[VM, VM] + [ANY] * 5,
         out_specs=[VM] * 7,
         out_shape=[
             pltpu.VMEM((E, SLOT, W), bf16),
@@ -776,6 +781,8 @@
         scratch_shapes=Scatter.scratch(C_PIECE, C_HALF)
         + Scatter.scratch(H_PIECE, H_HALF)
         + [
+            V((2, 2, ROWS // 2, W), bf16), V((2, NDP, 3 * SLOT, W), bf16),
+            V((NDP, 4 * SLOT, W), bf16), V((E, 8, 128), f32), D((2, NDP)),
             V((2, NDP, ROWS, W), bf16), V((2, NDP, ROWS, W), bf16),
             V((3, FFL, width), bf16),
             V((2, 3, FFL, ROWS), f32), V((2, 3, FFL, ROWS), bf16), V((2, ROWS, 2 * FFL), bf16),
@@ -793,7 +800,7 @@
             collective_id=1, has_side_effects=True, vmem_limit_bytes=54 * 1024 * 1024
         ),
         name="moe",
-    )(s1, s2, s3, m, wg, wu, wd)
+    )(ids, logits, x, dy, wg, wu, wd)
 
 
 def finish_kernel(
@@ -862,9 +869,8 @@
 def local(rows_x, rows_dy, router_logits, expert_of, w_gate, w_up, w_down):
     ids = expert_of.reshape(1, -1)
     logits = router_logits.T
-    s1, s2, s3, m = lay_out(ids, logits, rows_x, rows_dy)
     back, backh, gback, mr, gg, gu, gd = moe(
-        s1, s2, s3, m, w_gate[0], w_up[0], w_down[0]
+        ids, logits, rows_x, rows_dy, w_gate[0], w_up[0], w_down[0]
     )
     held = (back, backh, gback, mr, gg, gu, gd)
     held = [pltpu.with_memory_space_constraint(v, pltpu.VMEM) for v in held]

time: 123 us -> 119 us (0.967)
  Pallas kernels: 122 us -> 118 us
    pallas_call x2 -> x1, Pallas kernels: 117 us -> 113 us  [moe(): pl.pallas_call(moe_kernel, in_specs=[VM, VM] + [ANY] * 5, out_specs=[VM]...]
where the time goes in v6:
time: 119 us; the launch traced here: 118 us
  Pallas kernels  118 us (99%)
    pallas_call x1, Pallas kernels, moe(): pl.pallas_call(moe_kernel, in_specs=[VM, VM] + [ANY] * 5, out_specs=[VM]...  113 us
    pallas_call x1, Pallas kernels, finish(): pl.pallas_call(finish_kernel, in_specs=[VM] * 9, out_specs=[VM] * 3 + [AN...  4.87 us

profile of v6, /device:TPU:1, one launch (start us, length us, event | category | flops | bytes accessed | tf_op | source)
XLA Modules:
  0.0 118.5 jit_solution(17694797060291454964)
XLA Ops:
  0.6 0.0 copy-start
  0.6 0.0 copy-start.1
  0.7 112.9 %moe.1 = (bf16[16,32,512]{2,1,0:T(8,128)(2,1)S(1)}, bf16[32,512]{1,0:T(8,128)(2,1)S(1)}, f32[16,1,1280]{2,1,0:T(1,128)S(1)}, f32[16,8,128]{2,1,0:T(8,128)S(1)}, ...) custom-call(s32[1,256]{1,0:T(1,128)} %bitcast.13, f32[16,256]{1,0:T(8,128)} %bitcast.11, ...), custom_call_target="tpu_custom_call" | custom-call | tf_op jit(solution)/shard_map/moe/pallas_call | solution.py:770
  113.6 0.0 copy-done
  113.6 0.0 copy-done.1
  113.6 4.9 %finish.1 = (bf16[256,512]{1,0:T(8,128)(2,1)}, f32[16,256]{1,0:T(8,128)}, f32[1,128]{1,0:T(1,128)}, f32[192,4096]{1,0:T(8,128)}, f32[192,4096]{1,0:T(8,128)}, /*index=5*/f32[192,4096]{1,0:T(8,128)}) custom-call(s32[1,256]{1,0:T(1,128)S(1)} %bitcast.14, f32[16,256]{1,0:T(8,128)S(1)} %bitcast.12, bf16[16,32,512]{2,1,0:T(8,128)(2,1)S(1)} %get-tuple-element.19.back, ...), custom_call_target="tpu_custom_call" | custom-call | tf_op jit(solution)/shard_map/finish/pallas_call | solution.py:851
Async XLA Ops:
  0.6 112.9 %copy-start = (f32[256,16]{0,1:T(8,128)S(1)}, f32[256,16]{0,1:T(8,128)}, u32[]{:S(2)}) copy-start(f32[256,16]{0,1:T(8,128)} %param.9) | copy-start | bytes 49156
  0.6 112.9 %copy-start.1 = (s32[256,1]{0,1:T(1,128)S(1)}, s32[256,1]{0,1:T(1,128)}, u32[]{:S(2)}) copy-start(s32[256,1]{0,1:T(1,128)} %param.10) | copy-start | bytes 3076

commit v7 on v6

--- a/solution.py
+++ b/solution.py
@@ -604,7 +604,6 @@
     for copy in own_in + loads[2 * NDP :]:
         copy.wait()
     wait(cold.at[:, :, slots_at(1 - c), :], sib_s, sib_r)
-    forward_dy(cold, 0, lambda i: d, 1)
     ex.s2()
     ex.s3()
     dp.s2()
@@ -617,14 +616,15 @@
     dp.s4()
     dp.s5()
     dp.s6()
-    for i in range(4):
-        wait(cold.at[0, :, pl.ds((2 + i) * SLOT, SLOT), :], sd_s.at[0], sd_r.at[i])
     ex.s7()
     ex.s8()
     share(0, ex.jd, zh)
     dp.s7()
     dp.s8()
+    for i in range(4):
+        wait(cold.at[0, :, pl.ds((2 + i) * SLOT, SLOT), :], sd_s.at[0], sd_r.at[i])
     forward_x(cold, 0, lambda i: d, 1)
+    forward_dy(cold, 0, lambda i: d, 1)
     forward_x(cold, 0, lambda i: ((y + 1 + 2 * i) % 4) * 2 + zl, 2)
     ex.s9()
     ex.s10()
@@ -677,9 +677,9 @@
         wait(ex_other(*where, None), xs_s.at[i], xs_r.at[i])
     forward_x(extra, 1, lambda i: i, NDP)
     forward_dy(extra, 1, lambda i: i, NDP)
+    between(1)
     C.relay0()
     C.relay1_far()
-    between(1)
     far = [X.jd * 2, X.jd * 2 + 1, X.jr * 2, X.jl * 2, X.jr * 2 + 1, X.jl * 2 + 1, x * 2, x * 2 + 1]
     rows_back(1, dxh, lambda i: i, NDP)
 

time: 119 us -> 119 us (level)
  no operation moved by 1% of the time
where the time goes in v7:
time: 119 us; the launch traced here: 118 us
  Pallas kernels  118 us (99%)
    pallas_call x1, Pallas kernels, moe(): pl.pallas_call(moe_kernel, in_specs=[VM, VM] + [ANY] * 5, out_specs=[VM]...  113 us
    pallas_call x1, Pallas kernels, finish(): pl.pallas_call(finish_kernel, in_specs=[VM] * 9, out_specs=[VM] * 3 + [AN...  4.87 us

profile of v7, /device:TPU:1, one launch (start us, length us, event | category | flops | bytes accessed | tf_op | source)
XLA Modules:
  0.0 118.4 jit_solution(2016736651975043835)
XLA Ops:
  0.6 0.0 copy-start
  0.6 0.0 copy-start.1
  0.7 112.9 %moe.1 = (bf16[16,32,512]{2,1,0:T(8,128)(2,1)S(1)}, bf16[32,512]{1,0:T(8,128)(2,1)S(1)}, f32[16,1,1280]{2,1,0:T(1,128)S(1)}, f32[16,8,128]{2,1,0:T(8,128)S(1)}, ...) custom-call(s32[1,256]{1,0:T(1,128)} %bitcast.13, f32[16,256]{1,0:T(8,128)} %bitcast.11, ...), custom_call_target="tpu_custom_call" | custom-call | tf_op jit(solution)/shard_map/moe/pallas_call | solution.py:770
  113.6 0.0 copy-done
  113.6 0.0 copy-done.1
  113.6 4.9 %finish.1 = (bf16[256,512]{1,0:T(8,128)(2,1)}, f32[16,256]{1,0:T(8,128)}, f32[1,128]{1,0:T(1,128)}, f32[192,4096]{1,0:T(8,128)}, f32[192,4096]{1,0:T(8,128)}, /*index=5*/f32[192,4096]{1,0:T(8,128)}) custom-call(s32[1,256]{1,0:T(1,128)S(1)} %bitcast.14, f32[16,256]{1,0:T(8,128)S(1)} %bitcast.12, bf16[16,32,512]{2,1,0:T(8,128)(2,1)S(1)} %get-tuple-element.19.back, ...), custom_call_target="tpu_custom_call" | custom-call | tf_op jit(solution)/shard_map/finish/pallas_call | solution.py:851
Async XLA Ops:
  0.6 112.9 %copy-start = (f32[256,16]{0,1:T(8,128)S(1)}, f32[256,16]{0,1:T(8,128)}, u32[]{:S(2)}) copy-start(f32[256,16]{0,1:T(8,128)} %param.9) | copy-start | bytes 49156
  0.6 112.9 %copy-start.1 = (s32[256,1]{0,1:T(1,128)S(1)}, s32[256,1]{0,1:T(1,128)}, u32[]{:S(2)}) copy-start(s32[256,1]{0,1:T(1,128)} %param.10) | copy-start | bytes 3076
